TPU v7x, 32 devices: a whole 2x2x4 slice. The times are simulated.
32 devices in a mesh: section: 2 (over y), expert: 16 (over z, x, core).
Axes of the slice: x: 2, y: 2, z: 4, core: 2. Of those that a mesh axis runs over, the one named last changes fastest.
Arguments:
- x_forward: bfloat16 [2, 1024, 2048], P('section', 'expert'), may hold values from -6 to 6
- norm_gain: float32 [2, 2048], P('section'), may hold values from 0.1 to 1.9
- w_gate: bfloat16 [2, 16, 2048, 768], P('section', 'expert'), may hold values from -0.125 to 0.125
- w_up: bfloat16 [2, 16, 2048, 768], P('section', 'expert'), may hold values from -0.125 to 0.125
- w_down: bfloat16 [2, 16, 768, 2048], P('section', 'expert'), may hold values from -0.21875 to 0.21875
- ids_forward: int32 [2, 1024, 8], P('section', 'expert'), may hold values from 0 to 15, all different within a row; in each aligned block of 64 rows (0 to 63, 64 to 127, ..., all dimensions but the last counted through in order) at most 48 rows name the same one
- gates_forward: float32 [2, 1024, 8], P('section', 'expert'), may hold values from 0.02 to 0.4
- x_backward: bfloat16 [2, 1024, 2048], P('section', 'expert'), may hold values from -6 to 6
- dy_backward: bfloat16 [2, 1024, 2048], P('section', 'expert'), may hold values from -6 to 6
- ids_backward: int32 [2, 1024, 8], P('section', 'expert'), may hold values from 0 to 15, all different within a row; in each aligned block of 64 rows (0 to 63, 64 to 127, ..., all dimensions but the last counted through in order) at most 48 rows name the same one
- gates_backward: float32 [2, 1024, 8], P('section', 'expert'), may hold values from 0.02 to 0.4
- saved_gate: bfloat16 [2, 16, 16, 48, 768], P('section', 'expert'), may hold values from -6 to 6
- saved_up: bfloat16 [2, 16, 16, 48, 768], P('section', 'expert'), may hold values from -6 to 6
Outputs:
- next_forward: bfloat16 [2, 1024, 2048], P('section', 'expert')
- next_backward: bfloat16 [2, 1024, 2048], P('section', 'expert')
Inputs may be any that keep to these rules, and one draw needn't show every extreme that they name: `ids_forward`: each row names 8 different experts. In each aligned block of 64 tokens no expert is named by more than 48 tokens, a bound that some block reaches. `ids_backward`: each row names 8 different experts. In each aligned block of 64 tokens no expert is named by more than 48 tokens, a bound that some block reaches.
All inputs are finite; a program needn't handle non-finite values.
Results may differ from a plain program's by a relative error of at most 0.0043.
Values may be sent and summed in bfloat16 or wider, within the bound.
No kernel may reach another device: no remote copies, remote signals or barrier semaphores. Data moves between devices by JAX's collectives and lax.ppermute only.
A program may use at most 64 MiB of HBM per device.

v0:
```python
import jax
import jax.numpy as jnp
from jax import lax
from jax.sharding import PartitionSpec as P

epsilon = 1e-06


def from_behind(value, axis, steps):
    count = lax.axis_size(axis)
    pairs = [(source, (source + steps) % count) for source in range(count)]
    return lax.ppermute(value, axis, pairs)


def local_places(route_ids, experts, capacity):
    flattened = route_ids.reshape(-1)
    onehot = (flattened[:, None] == jnp.arange(experts, dtype=jnp.int32)[None, :]).astype(jnp.int32)
    before = jnp.cumsum(onehot, axis=0) - onehot
    slot_index = jnp.sum(before * onehot, axis=1)
    return flattened * capacity + slot_index


def local_dispatch(rows, places, experts, capacity, per_token):
    token_rows = jnp.arange(places.shape[0], dtype=jnp.int32) // per_token
    buffer = (
        jnp.zeros((experts * capacity, rows.shape[1]), rows.dtype).at[places].set(rows[token_rows])
    )
    return buffer.reshape(experts, capacity, rows.shape[1])


def local_combine(returned, places, weights):
    row_width = returned.shape[2]
    picked = returned.reshape(-1, row_width)[places].reshape(
        weights.shape[0], weights.shape[1], row_width
    )
    return jnp.sum(weights[:, :, None] * picked.astype(jnp.float32), axis=1)


def inverse_rms(values):
    widened = values.astype(jnp.float32)
    return lax.rsqrt(jnp.mean(widened * widened, axis=-1, keepdims=True) + epsilon)


def expert_forward(received, gate_matrix, up_matrix, down_matrix):
    sources, capacity, row_width = received.shape
    rows = received.reshape(sources * capacity, row_width)
    gate_pre = jnp.dot(rows, gate_matrix, preferred_element_type=jnp.float32)
    up_pre = jnp.dot(rows, up_matrix, preferred_element_type=jnp.float32)
    act_rows = (jax.nn.silu(gate_pre) * up_pre).astype(jnp.bfloat16)
    results = jnp.dot(act_rows, down_matrix, preferred_element_type=jnp.float32).astype(
        jnp.bfloat16
    )
    return results.reshape(sources, capacity, row_width)


def expert_backward(received, gate_saved, up_saved, gate_matrix, up_matrix, down_matrix):
    sources, capacity, row_width = received.shape
    grad_rows = received.reshape(sources * capacity, row_width)
    d_act = jnp.dot(grad_rows, down_matrix.T, preferred_element_type=jnp.float32)
    gate_pre = gate_saved.reshape(sources * capacity, -1).astype(jnp.float32)
    up_pre = up_saved.reshape(sources * capacity, -1).astype(jnp.float32)
    sigmoid_gate = jax.nn.sigmoid(gate_pre)
    d_gate = (d_act * up_pre * sigmoid_gate * (1.0 + gate_pre * (1.0 - sigmoid_gate))).astype(
        jnp.bfloat16
    )
    d_up = (d_act * gate_pre * sigmoid_gate).astype(jnp.bfloat16)
    summed = jnp.dot(d_gate, gate_matrix.T, preferred_element_type=jnp.float32)
    summed = summed + jnp.dot(d_up, up_matrix.T, preferred_element_type=jnp.float32)
    return summed.astype(jnp.bfloat16).reshape(sources, capacity, row_width)


def shards(
    x_forward,
    norm_gain,
    w_gate,
    w_up,
    w_down,
    ids_forward,
    gates_forward,
    x_backward,
    dy_backward,
    ids_backward,
    gates_backward,
    saved_gate,
    saved_up,
):
    experts = lax.axis_size("expert")
    capacity = saved_gate.shape[3]
    per_token = ids_forward.shape[2]
    layer_gain = norm_gain[0]
    gate_matrix = w_gate[0, 0]
    up_matrix = w_up[0, 0]
    down_matrix = w_down[0, 0]
    input_rows = x_forward[0]
    normed = (
        input_rows.astype(jnp.float32) * inverse_rms(input_rows) * layer_gain[None, :]
    ).astype(jnp.bfloat16)
    places_forward = local_places(ids_forward[0], experts, capacity)
    places_backward = local_places(ids_backward[0], experts, capacity)
    send_forward = local_dispatch(normed, places_forward, experts, capacity, per_token)
    send_backward = local_dispatch(dy_backward[0], places_backward, experts, capacity, per_token)
    gate_keep = saved_gate[0, 0]
    up_keep = saved_up[0, 0]
    recv_forward, recv_backward = (
        lax.all_to_all(send_forward, "expert", split_axis=0, concat_axis=0, tiled=True),
        lax.all_to_all(send_backward, "expert", split_axis=0, concat_axis=0, tiled=True),
    )
    expert_out = expert_forward(recv_forward, gate_matrix, up_matrix, down_matrix)
    d_rows = expert_backward(recv_backward, gate_keep, up_keep, gate_matrix, up_matrix, down_matrix)
    back_forward, back_backward = (
        lax.all_to_all(expert_out, "expert", split_axis=0, concat_axis=0, tiled=True),
        lax.all_to_all(d_rows, "expert", split_axis=0, concat_axis=0, tiled=True),
    )
    layer_out = (
        input_rows.astype(jnp.float32)
        + local_combine(back_forward, places_forward, gates_forward[0])
    ).astype(jnp.bfloat16)
    d_normed = local_combine(back_backward, places_backward, gates_backward[0])
    saved_input = x_backward[0].astype(jnp.float32)
    scale_rows = inverse_rms(x_backward[0])
    weighted = d_normed * layer_gain[None, :]
    inner = jnp.mean(weighted * saved_input, axis=-1, keepdims=True)
    d_input = (
        dy_backward[0].astype(jnp.float32)
        + scale_rows * weighted
        - saved_input * scale_rows * scale_rows * scale_rows * inner
    )
    d_input = d_input.astype(jnp.bfloat16)
    next_forward = from_behind(layer_out, "section", 1)
    next_backward = from_behind(d_input, "section", -1)
    return (next_forward[None], next_backward[None])


def solution(mesh):
    placed = (
        P("section", "expert", None),
        P("section", None),
        P("section", "expert", None, None),
        P("section", "expert", None, None),
        P("section", "expert", None, None),
        P("section", "expert", None),
        P("section", "expert", None),
        P("section", "expert", None),
        P("section", "expert", None),
        P("section", "expert", None),
        P("section", "expert", None),
        P("section", "expert", None, None, None),
        P("section", "expert", None, None, None),
    )
    return jax.shard_map(
        shards,
        mesh=mesh,
        in_specs=placed,
        out_specs=(P("section", "expert", None), P("section", "expert", None)),
        check_vma=False,
    )
```

profile of v0, /device:TPU:10, one launch (start us, length us, event | category | flops | bytes accessed | tf_op | source)
XLA Modules:
  0.0 404.2 jit_solution(12418467091648743205)
XLA Ops:
  0.6 0.0 copy-start
  0.6 0.9 copy.24
  1.6 0.1 eq.62
  1.7 0.1 eq.58
  1.7 0.7 broadcast_multiply_fusion
  2.5 1.2 reduce-window.16
  3.6 0.2 slice_reduce_fusion
  3.9 0.1 copy.23
  4.0 0.1 mul.163
  4.1 0.1 fusion.48
  4.2 12.9 %scatter_custom_fusion.1 = bf16[768,2048]{1,0:T(8,128)(2,1)} fusion(s32[512]{0:T(512)S(1)} %bitcast.113, bf16[64,2048]{1,0:T(8,128)(2,1)} %bitcast.108, s32[1024]{0:T(1024)S(1)} %pad_clamp_fusion.2, bf16[]{:T(256)} %constant.36.clone.1), kind=kCustom, calls=%fused_computation.36 | custom fusion | bytes 3146240 | tf_op jit(solution)/shard_map/scatter | solution.py:26
  17.1 0.0 copy-start.11
  17.1 87.5 %all_to_all.20 = bf16[16,48,2048]{2,1,0:T(8,128)(2,1)S(1)} all-to-all(bf16[16,48,2048]{2,1,0:T(8,128)(2,1)} %bitcast.101), channel_id=1, replica_groups=mesh['section'=2,'expert'=16] {'expert'}, dimensions={0} | all-to-all | bytes 6291456 | tf_op jit(solution)/shard_map/all_to_all | solution.py:106
  104.6 0.0 copy-done.11
  104.6 0.0 copy-start.12
  104.6 2.6 fusion.2
  107.3 0.0 copy-done
  107.3 0.0 copy-done.12
  107.3 0.0 copy-done.13
  107.3 0.0 copy-start.9
  107.3 3.1 fusion.8
  110.4 0.0 copy-done.9
  110.4 4.2 %add_convert_fusion = bf16[768,2048]{1,0:T(8,128)(2,1)} fusion(f32[768,2048]{1,0:T(8,128)S(1)} %fusion.8, bf16[1,1,2048,768]{3,2,1,0:T(8,128)(2,1)S(1)} %copy-done.9, f32[768,768]{1,0:T(8,128)S(1)} %fusion.2, bf16[768,768]{1,0:T(8,128)(2,1)S(1)} %bitcast.122), kind=kOutput, calls=%fused_computation.6 | convolution fusion | flops 2423193600 | bytes 16121856 | tf_op jit(solution)/shard_map/dot_general | solution.py:68
  114.6 5.5 %all-to-all-start.3 = ((bf16[16,48,2048]{2,1,0:T(8,128)(2,1)}), bf16[16,48,2048]{2,1,0:T(8,128)(2,1)}, u32[]{:S(2)}, u32[]{:S(2)}) async-start(bf16[16,48,2048]{2,1,0:T(8,128)(2,1)} %bitcast.102), calls=%async_computation.3 | async-start | bytes 6291456 | tf_op jit(solution)/shard_map/all_to_all | solution.py:112
  120.1 0.0 copy-done.6
  120.1 0.1 copy.19
  120.2 0.1 eq.54
  120.3 0.1 eq.50
  120.4 0.0 copy-done.7
  120.4 0.1 copy.22
  120.5 1.2 reduce-window.14
  121.6 0.2 slice_reduce_fusion.1
  121.9 0.1 copy.18
  122.0 0.1 mul.147
  122.1 0.1 fusion.51
  122.2 0.0 copy-done.2
  122.2 0.2 fusion.35
  122.4 67.6 %all-to-all-done.3 = bf16[16,48,2048]{2,1,0:T(8,128)(2,1)} async-done(((bf16[16,48,2048]{2,1,0:T(8,128)(2,1)}), bf16[16,48,2048]{2,1,0:T(8,128)(2,1)}, u32[]{:S(2)}, u32[]{:S(2)}) %all-to-all-start.3) | async-done | bytes 3145760 | tf_op jit(solution)/shard_map/all_to_all | solution.py:112
  189.9 7.5 %gather_fusion.1 = bf16[512,2048]{1,0:T(8,128)(2,1)} fusion(bf16[768,2048]{1,0:T(8,128)(2,1)} %bitcast.29, s32[1024]{0:T(1024)S(1)} %pad_clamp_fusion), kind=kCustom, calls=%fused_computation.3 | custom fusion | bytes 4196352 | tf_op jit(solution)/shard_map/gather | solution.py:33
  197.5 3.5 fusion
  201.0 0.0 copy-done.3
  201.0 0.0 copy-done.5
  201.0 0.2 fusion.39
  201.2 0.0 copy-done.4
  201.2 1.1 fusion.44
  202.3 13.1 %scatter_custom_fusion = bf16[768,2048]{1,0:T(8,128)(2,1)} fusion(s32[512]{0:T(512)S(1)} %bitcast.111, bf16[64,2048]{1,0:T(8,128)(2,1)} %get-tuple-element.5, s32[1024]{0:T(1024)S(1)} %pad_clamp_fusion.2, bf16[]{:T(256)} %constant.36.clone.1), kind=kCustom, calls=%fused_computation.38 | custom fusion | bytes 3146240 | tf_op jit(solution)/shard_map/scatter | solution.py:26
  215.4 74.9 %all_to_all.21 = bf16[16,48,2048]{2,1,0:T(8,128)(2,1)S(1)} all-to-all(bf16[16,48,2048]{2,1,0:T(8,128)(2,1)} %bitcast.100), channel_id=1, replica_groups=mesh['section'=2,'expert'=16] {'expert'}, dimensions={0} | all-to-all | bytes 6291456 | tf_op jit(solution)/shard_map/all_to_all | solution.py:105
  290.4 1.7 copy-done.1
  292.1 0.0 copy-done.10
  292.1 4.0 fusion.6
  296.1 10.0 %convolution_convert_fusion = bf16[768,2048]{1,0:T(8,128)(2,1)} fusion(bf16[1,1,768,2048]{3,2,1,0:T(8,128)(2,1)} %param.17, f32[768,768]{1,0:T(8,128)} %fusion.6, bf16[768,2048]{1,0:T(8,128)(2,1)} %bitcast.105, bf16[1,1,2048,768]{3,2,1,0:T(8,128)(2,1)S(1)} %copy-done), kind=kOutput, calls=%fused_computation.14 | convolution fusion | flops 4836950016 | bytes 14942208 | tf_op jit(solution)/shard_map/dot_general | solution.py:50
  306.1 5.9 %all-to-all-start.1 = ((bf16[16,48,2048]{2,1,0:T(8,128)(2,1)}), bf16[16,48,2048]{2,1,0:T(8,128)(2,1)}, u32[]{:S(2)}, u32[]{:S(2)}) async-start(bf16[16,48,2048]{2,1,0:T(8,128)(2,1)} %bitcast.103), calls=%async_computation.1 | async-start | bytes 6291456 | tf_op jit(solution)/shard_map/all_to_all | solution.py:111
  312.0 0.0 copy-done.8
  312.0 0.1 copy.17
  312.1 1.6 collective-permute-start.1
  313.7 68.0 %all-to-all-done.1 = bf16[16,48,2048]{2,1,0:T(8,128)(2,1)} async-done(((bf16[16,48,2048]{2,1,0:T(8,128)(2,1)}), bf16[16,48,2048]{2,1,0:T(8,128)(2,1)}, u32[]{:S(2)}, u32[]{:S(2)}) %all-to-all-start.1) | async-done | bytes 3145760 | tf_op jit(solution)/shard_map/all_to_all | solution.py:111
  381.7 7.6 %gather_fusion = bf16[512,2048]{1,0:T(8,128)(2,1)} fusion(bf16[768,2048]{1,0:T(8,128)(2,1)} %bitcast.14, s32[1024]{0:T(1024)S(1)} %pad_clamp_fusion.1), kind=kCustom, calls=%fused_computation.1 | custom fusion | bytes 4196352 | tf_op jit(solution)/shard_map/gather | solution.py:33
  389.3 3.4 fusion.1
  392.7 0.1 fusion.38
  392.8 1.6 collective-permute-start
  394.4 0.0 collective-permute-done.1
  394.4 7.0 %collective-permute-done = bf16[64,2048]{1,0:T(8,128)(2,1)S(1)} collective-permute-done((bf16[64,2048]{1,0:T(8,128)(2,1)S(1)}, bf16[64,2048]{1,0:T(8,128)(2,1)S(1)}, u32[]{:S(2)}, u32[]{:S(2)}) %collective-permute-start) | collective-permute-done | bytes 262176 | tf_op jit(solution)/shard_map/ppermute | solution.py:12
  401.4 0.7 copy.33
  402.1 1.7 copy.34
  (25 shorter events, 0.2 us)
Async XLA Ops:
  0.6 106.6 %copy-start = (bf16[1,1,2048,768]{3,2,1,0:T(8,128)(2,1)S(1)}, bf16[1,1,2048,768]{3,2,1,0:T(8,128)(2,1)}, u32[]{:S(2)}) copy-start(bf16[1,1,2048,768]{3,2,1,0:T(8,128)(2,1)} %param.15) | copy-start | bytes 9437188
  17.1 87.5 %copy-start.11 = (bf16[1,1,768,2048]{3,2,1,0:T(8,128)(2,1)S(1)}, bf16[1,1,768,2048]{3,2,1,0:T(8,128)(2,1)}, u32[]{:S(2)}) copy-start(bf16[1,1,768,2048]{3,2,1,0:T(8,128)(2,1)} %param.17) | copy-start | bytes 9437188
  104.6 2.7 copy-start.12
  104.6 2.7 copy-start.13
  107.3 3.1 copy-start.9
  114.6 5.5 %copy-start.6 = (s32[1,64,8]{1,2,0:T(8,128)S(1)}, s32[1,64,8]{1,2,0:T(8,128)}, u32[]{:S(2)}) copy-start(s32[1,64,8]{1,2,0:T(8,128)} %param.18) | copy-start | bytes 6148
  114.6 5.7 %copy-start.7 = (f32[1,64,8]{1,2,0:T(8,128)S(1)}, f32[1,64,8]{1,2,0:T(8,128)}, u32[]{:S(2)}) copy-start(f32[1,64,8]{1,2,0:T(8,128)} %param.23) | copy-start | bytes 6148
  114.6 7.6 %copy-start.2 = (bf16[1,64,2048]{2,1,0:T(8,128)(2,1)S(1)}, bf16[1,64,2048]{2,1,0:T(8,128)(2,1)}, u32[]{:S(2)}) copy-start(bf16[1,64,2048]{2,1,0:T(8,128)(2,1)} %param.13) | copy-start | bytes 786436
  114.6 75.3 %all-to-all-start.3 = ((bf16[16,48,2048]{2,1,0:T(8,128)(2,1)}), bf16[16,48,2048]{2,1,0:T(8,128)(2,1)}, u32[]{:S(2)}, u32[]{:S(2)}) async-start(bf16[16,48,2048]{2,1,0:T(8,128)(2,1)} %bitcast.102), calls=%async_computation.3 | async-start | bytes 6291456 | tf_op jit(solution)/shard_map/all_to_all | solution.py:112
  197.5 3.5 copy-start.3
  197.5 3.5 copy-start.5
  197.5 3.7 copy-start.4
  215.4 76.7 %copy-start.10 = (bf16[1,1,2048,768]{3,2,1,0:T(8,128)(2,1)S(1)}, bf16[1,1,2048,768]{3,2,1,0:T(8,128)(2,1)}, u32[]{:S(2)}) copy-start(bf16[1,1,2048,768]{3,2,1,0:T(8,128)(2,1)} %param.16) | copy-start | bytes 9437188
  290.4 1.7 copy-start.1
  306.1 5.9 %copy-start.8 = (f32[1,64,8]{1,2,0:T(8,128)S(1)}, f32[1,64,8]{1,2,0:T(8,128)}, u32[]{:S(2)}) copy-start(f32[1,64,8]{1,2,0:T(8,128)} %param.19) | copy-start | bytes 6148
  306.1 75.6 %all-to-all-start.1 = ((bf16[16,48,2048]{2,1,0:T(8,128)(2,1)}), bf16[16,48,2048]{2,1,0:T(8,128)(2,1)}, u32[]{:S(2)}, u32[]{:S(2)}) async-start(bf16[16,48,2048]{2,1,0:T(8,128)(2,1)} %bitcast.103), calls=%async_computation.1 | async-start | bytes 6291456 | tf_op jit(solution)/shard_map/all_to_all | solution.py:111
  312.1 82.3 %collective-permute-start.1 = (bf16[64,2048]{1,0:T(8,128)(2,1)}, bf16[64,2048]{1,0:T(8,128)(2,1)}, u32[]{:S(2)}, u32[]{:S(2)}) collective-permute-start(bf16[64,2048]{1,0:T(8,128)(2,1)} %get-tuple-element.4), channel_id=1, source_target_pairs={{0,16},{16,0},{1,17},{17,1},{2,18},{18,2},{3,19},{19,3},{4,20},{20... | collective-permute-start | bytes 786440 | tf_op jit(solution)/shard_map/ppermute | solution.py:12
  392.8 8.6 %collective-permute-start = (bf16[64,2048]{1,0:T(8,128)(2,1)S(1)}, bf16[64,2048]{1,0:T(8,128)(2,1)S(1)}, u32[]{:S(2)}, u32[]{:S(2)}) collective-permute-start(bf16[64,2048]{1,0:T(8,128)(2,1)S(1)} %fusion.38), channel_id=1, source_target_pairs={{0,16},{16,0},{1,17},{17,1},{2,18},{18,2},{3,19},{19,3},{4,20},{20... | collective-permute-start | bytes 786440 | tf_op jit(solution)/shard_map/ppermute | solution.py:12
where the time goes:
time: 406 us; the launch traced here: 404 us
  blocking collectives  162 us (40%)
  waiting for transfers between devices  143 us (35%)
  local copies, waits for them, and re-layouts  47.6 us (12%)
  matrix products  24 us (6%)
  starting transfers between devices  14.5 us (4%)
  other arithmetic  11.7 us (3%)
    all_to_all x1, blocking collectives, shards(): lax.all_to_all(send_backward, 'expert', split_axis=0, concat_axis=0, tile...  87.5 us
    all_to_all x1, blocking collectives, shards(): lax.all_to_all(send_forward, 'expert', split_axis=0, concat_axis=0, tiled...  74.9 us
    all_to_all x1, waiting for transfers between devices, shards(): lax.all_to_all(expert_out, 'expert', split_axis=0, concat_axis=0, tiled=T...  68 us
    all_to_all x1, waiting for transfers between devices, shards(): lax.all_to_all(d_rows, 'expert', split_axis=0, concat_axis=0, tiled=True)  67.6 us
    scatter x2, local copies, waits for them, and re-layouts, local_dispatch(): jnp.zeros((experts * capacity, rows.shape[1]), rows.dtype).at[places]  26 us
    gather x2, local copies, waits for them, and re-layouts, local_combine(): returned.reshape(-1, row_width)[places]  15.1 us
    dot_general x1, matrix products, expert_forward(): jnp.dot(act_rows, down_matrix, preferred_element_type=jnp.float32)  10 us
  transfers between devices with their start and end apart: 4, of which 3 were waited for; matrix products, arithmetic and copies ran while one was open for 3% of the time, Pallas kernels for 0%

commit v1 on v0

v1 whole, which is shorter than its diff:
```python
import functools

import jax
import jax.numpy as jnp
from jax import lax
from jax.experimental import pallas as pl
from jax.experimental.pallas import tpu as pltpu
from jax.sharding import PartitionSpec as P

epsilon = 1e-06
f32 = jnp.float32
bf16 = jnp.bfloat16
LANES = 128
TILE = 256
TURNED = (((1,), (1,)), ((), ()))


def inverse_rms(values):
    widened = values.astype(f32)
    return lax.rsqrt(jnp.mean(widened * widened, axis=-1, keepdims=True) + epsilon)


def gate_columns(ids, gates, experts):
    onehot = ids[:, :, None] == jnp.arange(experts, dtype=jnp.int32)[None, None, :]
    dense = jnp.sum(jnp.where(onehot, gates[:, :, None], 0.0), axis=1)
    high = lax.reduce_precision(dense, 8, 7)
    low = dense - high
    both = jnp.concatenate([high, low], axis=1).astype(bf16)
    padded = -(-both.shape[1] // LANES) * LANES
    return jnp.pad(both, ((0, 0), (0, padded - both.shape[1])))


def experts_kernel(backward, experts, tokens, capacity, count, steps, scalars, *refs):
    rows, refs = refs[:count], refs[count:]
    mine, theirs, refs = refs[:3], refs[3:6], refs[6:]
    kept_mine, kept_theirs = (), ()
    if backward:
        kept_mine, kept_theirs, refs = refs[: 2 * count], refs[2 * count : 4 * count], refs[4 * count :]
    outs, refs = refs[:count], refs[count:]
    (gathered, total, gate_of), refs = refs[:3], refs[3:]
    width = gathered.shape[1]
    spaced = -(-capacity // 16) * 16
    which, tile = pl.program_id(0), pl.program_id(1)

    @pl.when((which == 0) & (tile == 0))
    def _():
        for i in range(count):
            gathered[i * tokens : (i + 1) * tokens, :] = rows[i][:, :width]
        total[...] = jnp.zeros_like(total)
        if backward and spaced != capacity:
            for kept in refs[1:3]:
                kept[...] = jnp.zeros_like(kept)

    @pl.when(tile == 0)
    def _():
        expert = scalars[which]
        columns = jnp.concatenate([r[:, width:] for r in rows], axis=0).astype(f32)
        lane = lax.broadcasted_iota(jnp.int32, columns.shape, 1)
        chosen = (lane == expert) | (lane == expert + experts)
        gate = jnp.sum(jnp.where(chosen, columns, 0.0), axis=1, keepdims=True)
        gate_of[...] = jnp.broadcast_to(gate, gate_of.shape)
        if backward:
            place = refs[0]
            total_rows = count * tokens
            slots = count * spaced
            row = lax.broadcasted_iota(jnp.int32, (total_rows, total_rows), 0)
            column = lax.broadcasted_iota(jnp.int32, (total_rows, total_rows), 1)
            earlier = column < row
            same = jnp.zeros_like(earlier)
            base = jnp.zeros((total_rows, slots), jnp.int32)
            placed_row = lax.broadcasted_iota(jnp.int32, (total_rows, slots), 0)
            for i in range(count):
                low, high = i * tokens, (i + 1) * tokens
                same = same | ((row >= low) & (row < high) & (column >= low) & (column < high))
                base = jnp.where(placed_row >= low, i * spaced, base)
            below = jnp.where(earlier & same, 1.0, 0.0).astype(bf16)
            routed = jnp.broadcast_to(jnp.where(gate > 0.0, 1.0, 0.0), (total_rows, slots))
            before = jnp.dot(below, routed.astype(bf16), preferred_element_type=f32)
            target = before.astype(jnp.int32) + base
            lane = lax.broadcasted_iota(jnp.int32, (total_rows, slots), 1)
            place[...] = jnp.where((lane == target) & (routed > 0.0), 1.0, 0.0).astype(bf16)

    def work(weights, kept):
        w_gate, w_up, w_down = weights
        gate = gate_of[:, 0:1]
        if not backward:
            value = gathered[...]
            gate_pre = jnp.dot(value, w_gate[...], preferred_element_type=f32)
            up_pre = jnp.dot(value, w_up[...], preferred_element_type=f32)
            act = (gate_pre * jax.nn.sigmoid(gate_pre) * (up_pre * gate)).astype(bf16)
            total[...] += jnp.dot(act, w_down[...], preferred_element_type=f32)
            return
        place, all_gate, all_up = refs[0], refs[1], refs[2]
        for i in range(count):
            all_gate[i * spaced : i * spaced + capacity, :] = kept[i][...]
            all_up[i * spaced : i * spaced + capacity, :] = kept[count + i][...]
        d_act = lax.dot_general(gathered[...], w_down[...], TURNED, preferred_element_type=f32)
        d_act = d_act * gate
        g = jnp.dot(place[...], all_gate[...], preferred_element_type=f32)
        u = jnp.dot(place[...], all_up[...], preferred_element_type=f32)
        q = jax.nn.sigmoid(g)
        d_gate = (d_act * u * q * (1.0 + g * (1.0 - q))).astype(bf16)
        d_up = (d_act * g * q).astype(bf16)
        total[...] += lax.dot_general(
            d_gate, w_gate[...], TURNED, preferred_element_type=f32
        ) + lax.dot_general(d_up, w_up[...], TURNED, preferred_element_type=f32)

    @pl.when(which == 0)
    def _():
        work(mine, kept_mine)

    @pl.when(which == 1)
    def _():
        work(theirs, kept_theirs)

    @pl.when((which == 1) & (tile == steps - 1))
    def _():
        for i in range(count):
            outs[i][...] = total[i * tokens : (i + 1) * tokens, :].astype(outs[i].dtype)


def run_experts(backward, experts, scalars, rows, mine, theirs, kept_mine, kept_theirs):
    count = len(rows)
    tokens = rows[0].shape[0]
    width, hidden = mine[0].shape[2:]
    steps = hidden // TILE
    capacity = kept_mine[0].shape[3]
    spaced = -(-capacity // 16) * 16

    def tile_of(turn):
        if turn == 0:
            return lambda which, tile: jnp.where(which == 0, tile, steps - 1)
        return lambda which, tile: jnp.where(which == 1, tile, 0)

    in_specs = [pl.BlockSpec(rows[0].shape, lambda which, tile, s: (0, 0)) for _ in rows]
    operands = list(rows)
    for turn, weights in enumerate((mine, theirs)):
        pick = tile_of(turn)
        for w in weights[:2]:
            in_specs.append(
                pl.BlockSpec(
                    (None, None, width, TILE),
                    lambda which, tile, s, pick=pick: (0, 0, 0, pick(which, tile)),
                )
            )
        in_specs.append(
            pl.BlockSpec(
                (None, None, TILE, width),
                lambda which, tile, s, pick=pick: (0, 0, pick(which, tile), 0),
            )
        )
        operands += list(weights)
    scratch = [
        pltpu.VMEM((count * tokens, width), bf16),
        pltpu.VMEM((count * tokens, width), f32),
        pltpu.VMEM((count * tokens, LANES), f32),
    ]
    if backward:
        for turn, kept in enumerate((kept_mine, kept_theirs)):
            pick = tile_of(turn)
            for array in kept:
                for i in range(count):
                    in_specs.append(
                        pl.BlockSpec(
                            (None, None, None, capacity, TILE),
                            lambda which, tile, s, pick=pick, i=i: (
                                0, 0, s[2 + i], 0, pick(which, tile),
                            ),
                        )
                    )
                    operands.append(array)
        scratch += [
            pltpu.VMEM((count * tokens, count * spaced), bf16),
            pltpu.VMEM((count * spaced, TILE), bf16),
            pltpu.VMEM((count * spaced, TILE), bf16),
        ]
    kinds = [f32 if i % 2 == 0 else bf16 for i in range(count)]
    amount = count * tokens * width * hidden
    return pl.pallas_call(
        functools.partial(
            experts_kernel, backward, experts, tokens, capacity, count, steps
        ),
        out_shape=[jax.ShapeDtypeStruct((tokens, width), kind) for kind in kinds],
        grid_spec=pltpu.PrefetchScalarGridSpec(
            num_scalar_prefetch=1,
            grid=(2, steps),
            in_specs=in_specs,
            out_specs=[pl.BlockSpec((tokens, width), lambda which, tile, s: (0, 0)) for _ in rows],
            scratch_shapes=scratch,
        ),
        compiler_params=pltpu.CompilerParams(
            dimension_semantics=("arbitrary", "arbitrary"), vmem_limit_bytes=40 * 1024 * 1024
        ),
        cost_estimate=pl.CostEstimate(
            flops=12 * amount, bytes_accessed=6 * width * hidden * 2, transcendentals=0
        ),
        name="experts_backward" if backward else "experts_forward",
    )(scalars, *operands)


def shards(
    x_forward,
    norm_gain,
    w_gate,
    w_up,
    w_down,
    ids_forward,
    gates_forward,
    x_backward,
    dy_backward,
    ids_backward,
    gates_backward,
    saved_gate,
    saved_up,
):
    experts = lax.axis_size("expert")
    sections = lax.axis_size("section")
    line = experts // 4
    me = lax.axis_index("expert")
    a, b, c = me // 4, (me // 2) % 2, me % 2

    def swap(value, bit):
        return lax.ppermute(value, "expert", [(i, i ^ bit) for i in range(experts)])

    def shift(value, steps):
        return lax.ppermute(
            value, "expert", [(i, (i + 4 * steps) % experts) for i in range(experts)]
        )

    def relay(value, section_steps, steps=0):
        pairs = []
        for s in range(sections):
            for i in range(experts):
                target = ((s + section_steps) % sections) * experts + (i + 4 * steps) % experts
                pairs.append((s * experts + i, target))
        return lax.ppermute(value, ("section", "expert"), pairs)

    order = []
    for k in range(1, line // 2 + 1):
        order += [k] if 2 * k == line else [k, line - k]
    order.append(0)
    chunks = [order[i : i + 2] for i in range(0, line, 2)]

    def gather(payload):
        held = {0: payload}
        for k in order[:-1]:
            held[k] = shift(held[k - 1], 1) if 2 * k <= line else shift(held[(k + 1) % line], -1)
        return {k: (held[k], swap(held[k], 2)) for k in order}

    def block_of(k, other):
        return (((a - k) % line) * 2 + (b ^ other)) * 2 + c

    mine = (w_gate, w_up, w_down)
    theirs = tuple(swap(w, 1) for w in mine)
    kept_mine = (saved_gate, saved_up)
    kept_theirs = tuple(swap(s, 1) for s in kept_mine)

    def experts_on(backward, arrived):
        pieces = {}
        for chunk in chunks:
            scalars = jnp.stack([me, me ^ 1] + [block_of(k, o) for k in chunk for o in (0, 1)])
            rows = [arrived[k][o] for k in chunk for o in (0, 1)]
            out = run_experts(
                backward, experts, scalars.astype(jnp.int32), rows, mine, theirs, kept_mine, kept_theirs
            )
            for i, k in enumerate(chunk):
                pieces[k] = (out[2 * i], out[2 * i + 1])
        return pieces

    def scatter(pieces, section_steps):
        total = None
        for k in order:
            chip = pieces[k][0] + swap(pieces[k][1], 2).astype(f32)
            came = relay(chip.astype(bf16), section_steps, -k).astype(f32)
            total = came if total is None else total + came
        return total

    input_rows = x_forward[0]
    normed = input_rows.astype(f32) * inverse_rms(input_rows) * norm_gain[0][None, :]
    payload_b = jnp.concatenate(
        [dy_backward[0], gate_columns(ids_backward[0], gates_backward[0], experts)], axis=1
    )
    payload_f = jnp.concatenate(
        [normed.astype(bf16), gate_columns(ids_forward[0], gates_forward[0], experts)], axis=1
    )
    residual = relay(input_rows, 1)
    saved_input = relay(x_backward[0], -1).astype(f32)
    gradient = relay(dy_backward[0], -1)
    gain = relay(norm_gain, -1)[0]

    arrived_b = gather(payload_b)
    arrived_f = gather(payload_f)

    d_normed = scatter(experts_on(True, arrived_b), -1)
    scale_rows = inverse_rms(saved_input)
    weighted = d_normed * gain[None, :]
    inner = jnp.mean(weighted * saved_input, axis=-1, keepdims=True)
    next_backward = (
        gradient.astype(f32)
        + scale_rows * weighted
        - saved_input * scale_rows * scale_rows * scale_rows * inner
    ).astype(bf16)

    combined = scatter(experts_on(False, arrived_f), 1)
    next_forward = (residual.astype(f32) + combined).astype(bf16)
    return (next_forward[None], next_backward[None])


def solution(mesh):
    rows = P("section", "expert", None)
    weights = P("section", "expert", None, None)
    saved = P("section", "expert", None, None, None)
    placed = (
        rows, P("section", None), weights, weights, weights, rows, rows,
        rows, rows, rows, rows, saved, saved,
    )
    return jax.shard_map(
        shards, mesh=mesh, in_specs=placed, out_specs=(rows, rows), check_vma=False
    )
```

time: 406 us -> 201 us (0.50)
  the two profiles are of different devices: /device:TPU:10 before, /device:TPU:0 now
where the time goes in v1:
time: 201 us; the launch traced here: 200 us
  waiting for transfers between devices  74 us (37%)
  Pallas kernels  54.8 us (27%)
  starting transfers between devices  49.5 us (25%)
  local copies, waits for them, and re-layouts  13.6 us (7%)
  other arithmetic  7.47 us (4%)
    pallas_call x4, Pallas kernels, run_experts(): pl.pallas_call(functools.partial(experts_kernel, backward, experts, token...  54.8 us
    ppermute x12, waiting for transfers between devices, relay(): return lax.ppermute(value, ('section', 'expert'), pairs)  32.6 us
    ppermute x21, waiting for transfers between devices, swap(): return lax.ppermute(value, 'expert', [(i, i ^ bit) for i in range(experts)])  24.2 us
    ppermute x12, starting transfers between devices, relay(): return lax.ppermute(value, ('section', 'expert'), pairs)  22.8 us
    ppermute x21, starting transfers between devices, swap(): return lax.ppermute(value, 'expert', [(i, i ^ bit) for i in range(experts)])  17.6 us
    ppermute x6, waiting for transfers between devices, shift(): lax.ppermute(value, 'expert', [(i, (i + 4 * steps) % experts) for i in ra...  17.1 us
    unnamed x44, local copies, waits for them, and re-layouts  13.1 us
    ppermute x6, starting transfers between devices, shift(): lax.ppermute(value, 'expert', [(i, (i + 4 * steps) % experts) for i in ra...  9.09 us
  transfers between devices with their start and end apart: 39, of which 16 were waited for; matrix products, arithmetic and copies ran while one was open for 4% of the time, Pallas kernels for 27%

profile of v1, /device:TPU:0, one launch (start us, length us, event | category | flops | bytes accessed | tf_op | source)
XLA Modules:
  0.0 200.2 jit_solution(12730889048067194068)
XLA Ops:
  1.7 0.7 select_reduce_fusion
  2.7 1.0 pad_maximum_fusion.1.refs_2_
  3.6 2.7 %collective-permute-start.21 = (bf16[64,2176]{1,0:T(8,128)(2,1)S(1)}, bf16[64,2176]{1,0:T(8,128)(2,1)S(1)}, u32[]{:S(2)}, u32[]{:S(2)}) collective-permute-start(bf16[64,2176]{1,0:T(8,128)(2,1)S(1)} %pad_maximum_fusion.1.refs_2_), channel_id=1, source_target_pairs={{0,4},{1,5},{2,6},{3,7},{4,8},{5,9},{6,10},{7,11},{8,12},{9,13},{1... | collective-permute-start | bytes 835592 | tf_op jit(solution)/shard_map/ppermute | solution.py:226
  6.3 2.1 %collective-permute-start.23 = (bf16[64,2176]{1,0:T(8,128)(2,1)S(1)}, bf16[64,2176]{1,0:T(8,128)(2,1)S(1)}, u32[]{:S(2)}, u32[]{:S(2)}) collective-permute-start(bf16[64,2176]{1,0:T(8,128)(2,1)S(1)} %pad_maximum_fusion.1.refs_2_), channel_id=1, source_target_pairs={{0,12},{1,13},{2,14},{3,15},{4,0},{5,1},{6,2},{7,3},{8,4},{9,5},{1... | collective-permute-start | bytes 835592 | tf_op jit(solution)/shard_map/ppermute | solution.py:226
  8.4 0.7 select_reduce_fusion.1
  9.4 1.1 fusion
  10.5 1.1 fusion.2
  11.7 4.2 %collective-permute-done.21.refs_0_ = bf16[64,2176]{1,0:T(8,128)(2,1)S(1)} collective-permute-done((bf16[64,2176]{1,0:T(8,128)(2,1)S(1)}, bf16[64,2176]{1,0:T(8,128)(2,1)S(1)}, u32[]{:S(2)}, u32[]{:S(2)}) %collective-permute-start.21) | collective-permute-done | bytes 278560 | tf_op jit(solution)/shard_map/ppermute | solution.py:226
  15.9 5.1 %collective-permute-done.23.refs_2_ = bf16[64,2176]{1,0:T(8,128)(2,1)S(1)} collective-permute-done((bf16[64,2176]{1,0:T(8,128)(2,1)S(1)}, bf16[64,2176]{1,0:T(8,128)(2,1)S(1)}, u32[]{:S(2)}, u32[]{:S(2)}) %collective-permute-start.23) | collective-permute-done | bytes 278560 | tf_op jit(solution)/shard_map/ppermute | solution.py:226
  21.0 2.6 %collective-permute-start.3 = (bf16[64,2176]{1,0:T(8,128)(2,1)S(1)}, bf16[64,2176]{1,0:T(8,128)(2,1)S(1)}, u32[]{:S(2)}, u32[]{:S(2)}) collective-permute-start(bf16[64,2176]{1,0:T(8,128)(2,1)S(1)} %pad_maximum_fusion.refs_2_), channel_id=1, source_target_pairs={{0,12},{1,13},{2,14},{3,15},{4,0},{5,1},{6,2},{7,3},{8,4},{9,5},{1... | collective-permute-start | bytes 835592 | tf_op jit(solution)/shard_map/ppermute | solution.py:226
  23.6 7.0 %collective-permute-done.1.refs_0_ = bf16[64,2176]{1,0:T(8,128)(2,1)S(1)} collective-permute-done((bf16[64,2176]{1,0:T(8,128)(2,1)S(1)}, bf16[64,2176]{1,0:T(8,128)(2,1)S(1)}, u32[]{:S(2)}, u32[]{:S(2)}) %collective-permute-start.1) | collective-permute-done | bytes 278560 | tf_op jit(solution)/shard_map/ppermute | solution.py:226
  30.6 1.5 collective-permute-start.2
  32.1 0.7 copy-done.7
  32.8 0.8 collective-permute-done.3.refs_2_
  33.6 1.5 collective-permute-start.4
  35.1 0.7 copy-done.9
  35.8 2.3 %collective-permute-done.2.refs_1_ = bf16[64,2176]{1,0:T(8,128)(2,1)S(1)} collective-permute-done((bf16[64,2176]{1,0:T(8,128)(2,1)S(1)}, bf16[64,2176]{1,0:T(8,128)(2,1)S(1)}, u32[]{:S(2)}, u32[]{:S(2)}) %collective-permute-start.2) | collective-permute-done | bytes 278560 | tf_op jit(solution)/shard_map/ppermute | solution.py:223
  38.0 0.7 copy-done.11
  38.7 4.4 %collective-permute-done.4.refs_3_ = bf16[64,2176]{1,0:T(8,128)(2,1)S(1)} collective-permute-done((bf16[64,2176]{1,0:T(8,128)(2,1)S(1)}, bf16[64,2176]{1,0:T(8,128)(2,1)S(1)}, u32[]{:S(2)}, u32[]{:S(2)}) %collective-permute-start.4) | collective-permute-done | bytes 278560 | tf_op jit(solution)/shard_map/ppermute | solution.py:223
  43.1 0.7 copy-done.13
  44.0 1.6 collective-permute-start.22
  45.6 0.6 collective-permute-start.24
  46.2 1.9 copy-done.2
  48.1 1.9 copy-done.4
  50.0 1.9 copy-done.5
  51.8 1.0 copy-done.8
  52.8 1.0 copy-done.10
  53.8 1.0 copy-done.12
  54.7 1.0 copy-done.14
  55.7 11.0 %experts_forward.2 = (f32[64,2048]{1,0:T(8,128)S(1)}, bf16[64,2048]{1,0:T(8,128)(2,1)S(1)}, f32[64,2048]{1,0:T(8,128)S(1)}, bf16[64,2048]{1,0:T(8,128)(2,1)S(1)}) custom-call(s32[6]{0:T(128)S(1)} %stack.58.scalars, bf16[64,2176]{1,0:T(8,128)(2,1)S(1)} %copy-done.8, bf16[64,2176]{1,0:T(8,128)(2,1)S(1)} %copy-done.12, bf16[64,2176]{1,0:T(8,128)(2,1)S(1)} %copy-done.10, ...), custom_call_target="tpu_custom_call" | custom-call | flops 4831838208 | bytes 18874368 | tf_op jit(solution)/shard_map/experts_forward/pallas_call | solution.py:179
  66.6 0.7 copy-done.15
  67.3 1.5 collective-permute-start.33
  68.8 1.5 collective-permute-start.38
  70.9 1.7 collective-permute-start.12
  72.6 1.5 collective-permute-start.32
  74.1 16.8 %experts_backward.2 = (f32[64,2048]{1,0:T(8,128)S(1)}, bf16[64,2048]{1,0:T(8,128)(2,1)}, f32[64,2048]{1,0:T(8,128)S(1)}, bf16[64,2048]{1,0:T(8,128)(2,1)}) custom-call(s32[6]{0:T(128)S(1)} %stack.58.scalars, bf16[64,2176]{1,0:T(8,128)(2,1)S(1)} %collective-permute-done.21.refs_0_, bf16[64,2176]{1,0:T(8,128)(2,1)S(1)} %collective-permute-done.22.refs_1_, ...), custom_call_target="tpu_custom_call" | custom-call | flops 4831838208 | bytes 18874368 | tf_op jit(solution)/shard_map/experts_backward/pallas_call | solution.py:179
  92.0 1.5 collective-permute-start.27
  93.5 16.0 %experts_backward.3 = (f32[64,2048]{1,0:T(8,128)S(1)}, bf16[64,2048]{1,0:T(8,128)(2,1)S(1)}, f32[64,2048]{1,0:T(8,128)S(1)}, bf16[64,2048]{1,0:T(8,128)(2,1)S(1)}) custom-call(s32[6]{0:T(128)S(1)} %stack.63.scalars, bf16[64,2176]{1,0:T(8,128)(2,1)S(1)} %collective-permute-done.31.refs_0_, bf16[64,2176]{1,0:T(8,128)(2,1)S(1)} %collective-permute-done.32.refs_1_, ...), custom_call_target="tpu_custom_call" | custom-call | flops 4831838208 | bytes 18874368 | tf_op jit(solution)/shard_map/experts_backward/pallas_call | solution.py:179
  109.6 0.6 collective-permute-start.29
  110.2 1.5 collective-permute-start.34
  111.7 11.0 %experts_forward.3 = (f32[64,2048]{1,0:T(8,128)S(1)}, bf16[64,2048]{1,0:T(8,128)(2,1)S(1)}, f32[64,2048]{1,0:T(8,128)S(1)}, bf16[64,2048]{1,0:T(8,128)(2,1)S(1)}) custom-call(s32[6]{0:T(128)S(1)} %stack.63.scalars, bf16[64,2176]{1,0:T(8,128)(2,1)S(1)} %collective-permute-done.12.refs_0_, bf16[64,2176]{1,0:T(8,128)(2,1)S(1)} %collective-permute-done.13.refs_1_, ...), custom_call_target="tpu_custom_call" | custom-call | flops 4831838208 | bytes 18874368 | tf_op jit(solution)/shard_map/experts_forward/pallas_call | solution.py:179
  122.7 0.6 collective-permute-start.36
  123.3 1.6 collective-permute-start.8
  125.0 0.6 collective-permute-start.10
  125.6 6.4 %collective-permute-done.36 = bf16[64,2048]{1,0:T(8,128)(2,1)S(1)} collective-permute-done((bf16[64,2048]{1,0:T(8,128)(2,1)S(1)}, bf16[64,2048]{1,0:T(8,128)(2,1)S(1)}, u32[]{:S(2)}, u32[]{:S(2)}) %collective-permute-start.36) | collective-permute-done | bytes 262176 | tf_op jit(solution)/shard_map/ppermute | solution.py:223
  132.6 5.0 %collective-permute-done.8 = bf16[64,2048]{1,0:T(8,128)(2,1)S(1)} collective-permute-done((bf16[64,2048]{1,0:T(8,128)(2,1)S(1)}, bf16[64,2048]{1,0:T(8,128)(2,1)S(1)}, u32[]{:S(2)}, u32[]{:S(2)}) %collective-permute-start.8) | collective-permute-done | bytes 262176 | tf_op jit(solution)/shard_map/ppermute | solution.py:223
  138.2 5.0 %collective-permute-done.10 = bf16[64,2048]{1,0:T(8,128)(2,1)S(1)} collective-permute-done((bf16[64,2048]{1,0:T(8,128)(2,1)S(1)}, bf16[64,2048]{1,0:T(8,128)(2,1)S(1)}, u32[]{:S(2)}, u32[]{:S(2)}) %collective-permute-start.10) | collective-permute-done | bytes 262176 | tf_op jit(solution)/shard_map/ppermute | solution.py:223
  143.2 3.1 %collective-permute-start.28 = (bf16[64,2048]{1,0:T(8,128)(2,1)S(1)}, bf16[64,2048]{1,0:T(8,128)(2,1)S(1)}, u32[]{:S(2)}, u32[]{:S(2)}) collective-permute-start(bf16[64,2048]{1,0:T(8,128)(2,1)S(1)} %add_convert_fusion.3), channel_id=1, source_target_pairs={{0,28},{1,29},{2,30},{3,31},{4,16},{5,17},{6,18},{7,19},{8,20},{9,... | collective-permute-start | bytes 786440 | tf_op jit(solution)/shard_map/ppermute | solution.py:236
  146.4 1.1 collective-permute-done.15
  147.5 3.6 %collective-permute-start.30 = (bf16[64,2048]{1,0:T(8,128)(2,1)S(1)}, bf16[64,2048]{1,0:T(8,128)(2,1)S(1)}, u32[]{:S(2)}, u32[]{:S(2)}) collective-permute-start(bf16[64,2048]{1,0:T(8,128)(2,1)S(1)} %add_convert_fusion.2), channel_id=1, source_target_pairs={{0,20},{1,21},{2,22},{3,23},{4,24},{5,25},{6,26},{7,27},{8,28},{9,... | collective-permute-start | bytes 786440 | tf_op jit(solution)/shard_map/ppermute | solution.py:236
  151.5 1.5 collective-permute-start.37
  153.7 1.5 collective-permute-start
  155.2 5.1 %collective-permute-done.30 = bf16[64,2048]{1,0:T(8,128)(2,1)S(1)} collective-permute-done((bf16[64,2048]{1,0:T(8,128)(2,1)S(1)}, bf16[64,2048]{1,0:T(8,128)(2,1)S(1)}, u32[]{:S(2)}, u32[]{:S(2)}) %collective-permute-start.30) | collective-permute-done | bytes 262176 | tf_op jit(solution)/shard_map/ppermute | solution.py:236
  160.3 3.7 %collective-permute-start.9 = (bf16[64,2048]{1,0:T(8,128)(2,1)S(1)}, bf16[64,2048]{1,0:T(8,128)(2,1)S(1)}, u32[]{:S(2)}, u32[]{:S(2)}) collective-permute-start(bf16[64,2048]{1,0:T(8,128)(2,1)S(1)} %add_convert_fusion.8), channel_id=1, source_target_pairs={{0,28},{1,29},{2,30},{3,31},{4,16},{5,17},{6,18},{7,19},{8,20},{9,... | collective-permute-start | bytes 786440 | tf_op jit(solution)/shard_map/ppermute | solution.py:236
  164.0 8.0 %collective-permute-done.35 = bf16[64,2048]{1,0:T(8,128)(2,1)S(1)} collective-permute-done((bf16[64,2048]{1,0:T(8,128)(2,1)S(1)}, bf16[64,2048]{1,0:T(8,128)(2,1)S(1)}, u32[]{:S(2)}, u32[]{:S(2)}) %collective-permute-start.35) | collective-permute-done | bytes 262176 | tf_op jit(solution)/shard_map/ppermute | solution.py:236
  172.0 1.3 collective-permute-start.11
  173.4 1.1 collective-permute-done.37
  174.5 3.2 %collective-permute-start.16 = (bf16[64,2048]{1,0:T(8,128)(2,1)S(1)}, bf16[64,2048]{1,0:T(8,128)(2,1)S(1)}, u32[]{:S(2)}, u32[]{:S(2)}) collective-permute-start(bf16[64,2048]{1,0:T(8,128)(2,1)S(1)} %add_convert_fusion.6), channel_id=1, source_target_pairs={{0,24},{1,25},{2,26},{3,27},{4,28},{5,29},{6,30},{7,31},{8,16},{9,... | collective-permute-start | bytes 786440 | tf_op jit(solution)/shard_map/ppermute | solution.py:236
  178.0 10.1 %collective-permute-done.19 = bf16[64,2048]{1,0:T(8,128)(2,1)S(1)} collective-permute-done((bf16[64,2048]{1,0:T(8,128)(2,1)S(1)}, bf16[64,2048]{1,0:T(8,128)(2,1)S(1)}, u32[]{:S(2)}, u32[]{:S(2)}) %collective-permute-start.19) | collective-permute-done | bytes 262176 | tf_op jit(solution)/shard_map/ppermute | solution.py:236
  188.1 1.8 collective-permute-start.18
  189.9 1.0 fusion.11
  190.9 3.2 %collective-permute-done = bf16[64,2048]{1,0:T(8,128)(2,1)S(1)} collective-permute-done((bf16[64,2048]{1,0:T(8,128)(2,1)S(1)}, bf16[64,2048]{1,0:T(8,128)(2,1)S(1)}, u32[]{:S(2)}, u32[]{:S(2)}) %collective-permute-start) | collective-permute-done | bytes 262176 | tf_op jit(solution)/shard_map/ppermute | solution.py:236
  194.1 5.1 %collective-permute-done.18 = bf16[64,2048]{1,0:T(8,128)(2,1)S(1)} collective-permute-done((bf16[64,2048]{1,0:T(8,128)(2,1)S(1)}, bf16[64,2048]{1,0:T(8,128)(2,1)S(1)}, u32[]{:S(2)}, u32[]{:S(2)}) %collective-permute-start.18) | collective-permute-done | bytes 262176 | tf_op jit(solution)/shard_map/ppermute | solution.py:236
  199.3 0.9 fusion.10
  (93 shorter events, 6.2 us)
Async XLA Ops:
  0.6 43.4 %collective-permute-start.5 = (bf16[1,1,2048,768]{3,2,1,0:T(8,128)(2,1)}, bf16[1,1,2048,768]{3,2,1,0:T(8,128)(2,1)}, u32[]{:S(2)}, u32[]{:S(2)}) collective-permute-start(bf16[1,1,2048,768]{3,2,1,0:T(8,128)(2,1)} %refs_4_.7), channel_id=1, source_target_pairs={{0,1},{1,0},{2,3},{3,2},{4,5},{5,4},{6,7},{7,6},{8,9},{9,8},{10,11... | collective-permute-start | bytes 9437192 | tf_op jit(solution)/shard_map/ppermute | solution.py:223
  1.1 44.4 %collective-permute-start.6 = (bf16[1,1,2048,768]{3,2,1,0:T(8,128)(2,1)}, bf16[1,1,2048,768]{3,2,1,0:T(8,128)(2,1)}, u32[]{:S(2)}, u32[]{:S(2)}) collective-permute-start(bf16[1,1,2048,768]{3,2,1,0:T(8,128)(2,1)} %refs_5_.7), channel_id=1, source_target_pairs={{0,1},{1,0},{2,3},{3,2},{4,5},{5,4},{6,7},{7,6},{8,9},{9,8},{10,11... | collective-permute-start | bytes 9437192 | tf_op jit(solution)/shard_map/ppermute | solution.py:223
  1.2 44.3 %collective-permute-start.7 = (bf16[1,1,768,2048]{3,2,1,0:T(8,128)(2,1)}, bf16[1,1,768,2048]{3,2,1,0:T(8,128)(2,1)}, u32[]{:S(2)}, u32[]{:S(2)}) collective-permute-start(bf16[1,1,768,2048]{3,2,1,0:T(8,128)(2,1)} %refs_6_.7), channel_id=1, source_target_pairs={{0,1},{1,0},{2,3},{3,2},{4,5},{5,4},{6,7},{7,6},{8,9},{9,8},{10,11... | collective-permute-start | bytes 9437192 | tf_op jit(solution)/shard_map/ppermute | solution.py:223
  3.6 12.3 %collective-permute-start.21 = (bf16[64,2176]{1,0:T(8,128)(2,1)S(1)}, bf16[64,2176]{1,0:T(8,128)(2,1)S(1)}, u32[]{:S(2)}, u32[]{:S(2)}) collective-permute-start(bf16[64,2176]{1,0:T(8,128)(2,1)S(1)} %pad_maximum_fusion.1.refs_2_), channel_id=1, source_target_pairs={{0,4},{1,5},{2,6},{3,7},{4,8},{5,9},{6,10},{7,11},{8,12},{9,13},{1... | collective-permute-start | bytes 835592 | tf_op jit(solution)/shard_map/ppermute | solution.py:226
  6.3 14.7 %collective-permute-start.23 = (bf16[64,2176]{1,0:T(8,128)(2,1)S(1)}, bf16[64,2176]{1,0:T(8,128)(2,1)S(1)}, u32[]{:S(2)}, u32[]{:S(2)}) collective-permute-start(bf16[64,2176]{1,0:T(8,128)(2,1)S(1)} %pad_maximum_fusion.1.refs_2_), channel_id=1, source_target_pairs={{0,12},{1,13},{2,14},{3,15},{4,0},{5,1},{6,2},{7,3},{8,4},{9,5},{1... | collective-permute-start | bytes 835592 | tf_op jit(solution)/shard_map/ppermute | solution.py:226
  15.9 14.7 %collective-permute-start.1 = (bf16[64,2176]{1,0:T(8,128)(2,1)S(1)}, bf16[64,2176]{1,0:T(8,128)(2,1)S(1)}, u32[]{:S(2)}, u32[]{:S(2)}) collective-permute-start(bf16[64,2176]{1,0:T(8,128)(2,1)S(1)} %pad_maximum_fusion.refs_2_), channel_id=1, source_target_pairs={{0,4},{1,5},{2,6},{3,7},{4,8},{5,9},{6,10},{7,11},{8,12},{9,13},{1... | collective-permute-start | bytes 835592 | tf_op jit(solution)/shard_map/ppermute | solution.py:226
  21.0 12.5 %collective-permute-start.3 = (bf16[64,2176]{1,0:T(8,128)(2,1)S(1)}, bf16[64,2176]{1,0:T(8,128)(2,1)S(1)}, u32[]{:S(2)}, u32[]{:S(2)}) collective-permute-start(bf16[64,2176]{1,0:T(8,128)(2,1)S(1)} %pad_maximum_fusion.refs_2_), channel_id=1, source_target_pairs={{0,12},{1,13},{2,14},{3,15},{4,0},{5,1},{6,2},{7,3},{8,4},{9,5},{1... | collective-permute-start | bytes 835592 | tf_op jit(solution)/shard_map/ppermute | solution.py:226
  30.6 7.4 %collective-permute-start.2 = (bf16[64,2176]{1,0:T(8,128)(2,1)S(1)}, bf16[64,2176]{1,0:T(8,128)(2,1)S(1)}, u32[]{:S(2)}, u32[]{:S(2)}) collective-permute-start(bf16[64,2176]{1,0:T(8,128)(2,1)S(1)} %collective-permute-done.1.refs_0_), channel_id=1, source_target_pairs={{0,2},{1,3},{2,0},{3,1},{4,6},{5,7},{6,4},{7,5},{8,10},{9,11},{10,... | collective-permute-start | bytes 835592 | tf_op jit(solution)/shard_map/ppermute | solution.py:223
  32.1 0.7 copy-start.7
  33.6 9.5 %collective-permute-start.4 = (bf16[64,2176]{1,0:T(8,128)(2,1)S(1)}, bf16[64,2176]{1,0:T(8,128)(2,1)S(1)}, u32[]{:S(2)}, u32[]{:S(2)}) collective-permute-start(bf16[64,2176]{1,0:T(8,128)(2,1)S(1)} %collective-permute-done.3.refs_2_), channel_id=1, source_target_pairs={{0,2},{1,3},{2,0},{3,1},{4,6},{5,7},{6,4},{7,5},{8,10},{9,11},{10,... | collective-permute-start | bytes 835592 | tf_op jit(solution)/shard_map/ppermute | solution.py:223
  35.1 0.7 copy-start.9
  38.0 0.7 copy-start.11
  38.7 32.2 %collective-permute-start.25 = (bf16[1,1,16,48,768]{4,3,2,1,0:T(8,128)(2,1)}, bf16[1,1,16,48,768]{4,3,2,1,0:T(8,128)(2,1)S(1)}, u32[]{:S(2)}, u32[]{:S(2)}) collective-permute-start(bf16[1,1,16,48,768]{4,3,2,1,0:T(8,128)(2,1)} %refs_13_.3), channel_id=1, source_target_pairs={{0,1},{1,0},{2,3},{3,2},{4,5},{5,4},{6,7},{7,6},{8,9},{9,8},{10,11... | collective-permute-start | bytes 3538952 | tf_op jit(solution)/shard_map/ppermute | solution.py:223
  43.1 0.7 copy-start.13
  43.8 28.8 %collective-permute-start.26 = (bf16[1,1,16,48,768]{4,3,2,1,0:T(8,128)(2,1)}, bf16[1,1,16,48,768]{4,3,2,1,0:T(8,128)(2,1)S(1)}, u32[]{:S(2)}, u32[]{:S(2)}) collective-permute-start(bf16[1,1,16,48,768]{4,3,2,1,0:T(8,128)(2,1)} %refs_17_.3), channel_id=1, source_target_pairs={{0,1},{1,0},{2,3},{3,2},{4,5},{5,4},{6,7},{7,6},{8,9},{9,8},{10,11... | collective-permute-start | bytes 3538952 | tf_op jit(solution)/shard_map/ppermute | solution.py:223
  43.9 24.9 %copy-start.21 = (f32[1,2048]{1,0:T(1,128)S(1)}, f32[1,2048]{1,0:T(1,128)}, u32[]{:S(2)}) copy-start(f32[1,2048]{1,0:T(1,128)} %param.14) | copy-start | bytes 24580
  44.0 30.1 %copy-start = (bf16[1,1,16,48,768]{4,3,2,1,0:T(8,128)(2,1)S(1)}, bf16[1,1,16,48,768]{4,3,2,1,0:T(8,128)(2,1)}, u32[]{:S(2)}) copy-start(bf16[1,1,16,48,768]{4,3,2,1,0:T(8,128)(2,1)} %refs_13_.3) | copy-start | bytes 3538948
  44.0 30.1 %copy-start.1 = (bf16[1,1,16,48,768]{4,3,2,1,0:T(8,128)(2,1)S(1)}, bf16[1,1,16,48,768]{4,3,2,1,0:T(8,128)(2,1)}, u32[]{:S(2)}) copy-start(bf16[1,1,16,48,768]{4,3,2,1,0:T(8,128)(2,1)} %refs_17_.3) | copy-start | bytes 3538948
  44.0 23.3 %collective-permute-start.22 = (bf16[64,2176]{1,0:T(8,128)(2,1)S(1)}, bf16[64,2176]{1,0:T(8,128)(2,1)S(1)}, u32[]{:S(2)}, u32[]{:S(2)}) collective-permute-start(bf16[64,2176]{1,0:T(8,128)(2,1)S(1)} %collective-permute-done.21.refs_0_), channel_id=1, source_target_pairs={{0,2},{1,3},{2,0},{3,1},{4,6},{5,7},{6,4},{7,5},{8,10},{9,11},{10,... | collective-permute-start | bytes 835592 | tf_op jit(solution)/shard_map/ppermute | solution.py:223
  45.6 24.8 %collective-permute-start.31 = (bf16[64,2176]{1,0:T(8,128)(2,1)S(1)}, bf16[64,2176]{1,0:T(8,128)(2,1)S(1)}, u32[]{:S(2)}, u32[]{:S(2)}) collective-permute-start(bf16[64,2176]{1,0:T(8,128)(2,1)S(1)} %collective-permute-done.21.refs_0_), channel_id=1, source_target_pairs={{0,4},{1,5},{2,6},{3,7},{4,8},{5,9},{6,10},{7,11},{8,12},{9,13},{1... | collective-permute-start | bytes 835592 | tf_op jit(solution)/shard_map/ppermute | solution.py:226
  45.6 23.3 %collective-permute-start.24 = (bf16[64,2176]{1,0:T(8,128)(2,1)S(1)}, bf16[64,2176]{1,0:T(8,128)(2,1)S(1)}, u32[]{:S(2)}, u32[]{:S(2)}) collective-permute-start(bf16[64,2176]{1,0:T(8,128)(2,1)S(1)} %collective-permute-done.23.refs_2_), channel_id=1, source_target_pairs={{0,2},{1,3},{2,0},{3,1},{4,6},{5,7},{6,4},{7,5},{8,10},{9,11},{10,... | collective-permute-start | bytes 835592 | tf_op jit(solution)/shard_map/ppermute | solution.py:223
  46.2 1.9 copy-start.2
  48.1 1.9 copy-start.4
  50.0 1.9 copy-start.5
  51.8 1.0 copy-start.8
  52.8 1.0 copy-start.10
  53.8 1.0 copy-start.12
  54.7 1.0 copy-start.14
  66.6 0.7 copy-start.15
  67.3 23.6 %copy-start.17 = (bf16[64,2048]{1,0:T(8,128)(2,1)}, bf16[64,2048]{1,0:T(8,128)(2,1)S(1)}, u32[]{:S(2)}) copy-start(bf16[64,2048]{1,0:T(8,128)(2,1)S(1)} %get-tuple-element.19) | copy-start | bytes 786436
  67.3 26.2 %copy-start.3 = (bf16[1,1,2048,768]{3,2,1,0:T(8,128)(2,1)S(1)}, bf16[1,1,2048,768]{3,2,1,0:T(8,128)(2,1)}, u32[]{:S(2)}) copy-start(bf16[1,1,2048,768]{3,2,1,0:T(8,128)(2,1)} %refs_4_.7) | copy-start | bytes 9437188
  67.3 23.6 %collective-permute-start.33 = (bf16[64,2176]{1,0:T(8,128)(2,1)S(1)}, bf16[64,2176]{1,0:T(8,128)(2,1)S(1)}, u32[]{:S(2)}, u32[]{:S(2)}) collective-permute-start(bf16[64,2176]{1,0:T(8,128)(2,1)S(1)} %pad_maximum_fusion.1.refs_2_), channel_id=1, source_target_pairs={{0,2},{1,3},{2,0},{3,1},{4,6},{5,7},{6,4},{7,5},{8,10},{9,11},{10,... | collective-permute-start | bytes 835592 | tf_op jit(solution)/shard_map/ppermute | solution.py:223
  68.8 82.3 %collective-permute-start.38 = (f32[1,2048]{1,0:T(1,128)S(1)}, f32[1,2048]{1,0:T(1,128)S(1)}, u32[]{:S(2)}, u32[]{:S(2)}) collective-permute-start(f32[1,2048]{1,0:T(1,128)S(1)} %copy-done.21), channel_id=1, source_target_pairs={{0,16},{1,17},{2,18},{3,19},{4,20},{5,21},{6,22},{7,23},{8,24},{9,... | collective-permute-start | bytes 24584 | tf_op jit(solution)/shard_map/ppermute | solution.py:236
  70.4 39.2 %collective-permute-start.14 = (bf16[64,2176]{1,0:T(8,128)(2,1)S(1)}, bf16[64,2176]{1,0:T(8,128)(2,1)S(1)}, u32[]{:S(2)}, u32[]{:S(2)}) collective-permute-start(bf16[64,2176]{1,0:T(8,128)(2,1)S(1)} %pad_maximum_fusion.refs_2_), channel_id=1, source_target_pairs={{0,2},{1,3},{2,0},{3,1},{4,6},{5,7},{6,4},{7,5},{8,10},{9,11},{10,... | collective-permute-start | bytes 835592 | tf_op jit(solution)/shard_map/ppermute | solution.py:223
  70.9 20.6 %collective-permute-start.12 = (bf16[64,2176]{1,0:T(8,128)(2,1)S(1)}, bf16[64,2176]{1,0:T(8,128)(2,1)S(1)}, u32[]{:S(2)}, u32[]{:S(2)}) collective-permute-start(bf16[64,2176]{1,0:T(8,128)(2,1)S(1)} %copy-done.8), channel_id=1, source_target_pairs={{0,4},{1,5},{2,6},{3,7},{4,8},{5,9},{6,10},{7,11},{8,12},{9,13},{1... | collective-permute-start | bytes 835592 | tf_op jit(solution)/shard_map/ppermute | solution.py:226
  72.6 19.4 %collective-permute-start.32 = (bf16[64,2176]{1,0:T(8,128)(2,1)S(1)}, bf16[64,2176]{1,0:T(8,128)(2,1)S(1)}, u32[]{:S(2)}, u32[]{:S(2)}) collective-permute-start(bf16[64,2176]{1,0:T(8,128)(2,1)S(1)} %collective-permute-done.31.refs_0_), channel_id=1, source_target_pairs={{0,2},{1,3},{2,0},{3,1},{4,6},{5,7},{6,4},{7,5},{8,10},{9,11},{10,... | collective-permute-start | bytes 835592 | tf_op jit(solution)/shard_map/ppermute | solution.py:223
  90.9 62.2 %collective-permute-start.20 = (bf16[64,2048]{1,0:T(8,128)(2,1)}, bf16[64,2048]{1,0:T(8,128)(2,1)S(1)}, u32[]{:S(2)}, u32[]{:S(2)}) collective-permute-start(bf16[64,2048]{1,0:T(8,128)(2,1)} %bitcast.16), channel_id=1, source_target_pairs={{0,16},{1,17},{2,18},{3,19},{4,20},{5,21},{6,22},{7,23},{8,24},{9,... | collective-permute-start | bytes 786440 | tf_op jit(solution)/shard_map/ppermute | solution.py:236
  91.5 18.7 %collective-permute-start.13 = (bf16[64,2176]{1,0:T(8,128)(2,1)S(1)}, bf16[64,2176]{1,0:T(8,128)(2,1)S(1)}, u32[]{:S(2)}, u32[]{:S(2)}) collective-permute-start(bf16[64,2176]{1,0:T(8,128)(2,1)S(1)} %collective-permute-done.12.refs_0_), channel_id=1, source_target_pairs={{0,2},{1,3},{2,0},{3,1},{4,6},{5,7},{6,4},{7,5},{8,10},{9,11},{10,... | collective-permute-start | bytes 835592 | tf_op jit(solution)/shard_map/ppermute | solution.py:223
  92.0 19.7 %copy-start.6 = (bf16[1,1,768,2048]{3,2,1,0:T(8,128)(2,1)S(1)}, bf16[1,1,768,2048]{3,2,1,0:T(8,128)(2,1)}, u32[]{:S(2)}) copy-start(bf16[1,1,768,2048]{3,2,1,0:T(8,128)(2,1)} %refs_6_.7) | copy-start | bytes 9437188
  92.0 30.7 %collective-permute-start.27 = (bf16[64,2048]{1,0:T(8,128)(2,1)}, bf16[64,2048]{1,0:T(8,128)(2,1)S(1)}, u32[]{:S(2)}, u32[]{:S(2)}) collective-permute-start(bf16[64,2048]{1,0:T(8,128)(2,1)} %get-tuple-element.27), channel_id=1, source_target_pairs={{0,2},{1,3},{2,0},{3,1},{4,6},{5,7},{6,4},{7,5},{8,10},{9,11},{10,... | collective-permute-start | bytes 786440 | tf_op jit(solution)/shard_map/ppermute | solution.py:223
  109.6 13.7 %collective-permute-start.29 = (bf16[64,2048]{1,0:T(8,128)(2,1)}, bf16[64,2048]{1,0:T(8,128)(2,1)S(1)}, u32[]{:S(2)}, u32[]{:S(2)}) collective-permute-start(bf16[64,2048]{1,0:T(8,128)(2,1)} %get-tuple-element.29), channel_id=1, source_target_pairs={{0,2},{1,3},{2,0},{3,1},{4,6},{5,7},{6,4},{7,5},{8,10},{9,11},{10,... | collective-permute-start | bytes 786440 | tf_op jit(solution)/shard_map/ppermute | solution.py:223
  110.2 13.2 %copy-start.18 = (bf16[64,2048]{1,0:T(8,128)(2,1)S(1)}, bf16[64,2048]{1,0:T(8,128)(2,1)}, u32[]{:S(2)}) copy-start(bf16[64,2048]{1,0:T(8,128)(2,1)} %copy-done.17) | copy-start | bytes 786436
  110.2 14.8 %copy-start.16 = (bf16[64,2048]{1,0:T(8,128)(2,1)S(1)}, bf16[64,2048]{1,0:T(8,128)(2,1)}, u32[]{:S(2)}) copy-start(bf16[64,2048]{1,0:T(8,128)(2,1)} %copy-done.15) | copy-start | bytes 786436
  110.2 14.8 %collective-permute-start.34 = (bf16[64,2048]{1,0:T(8,128)(2,1)S(1)}, bf16[64,2048]{1,0:T(8,128)(2,1)S(1)}, u32[]{:S(2)}, u32[]{:S(2)}) collective-permute-start(bf16[64,2048]{1,0:T(8,128)(2,1)S(1)} %get-tuple-element.31), channel_id=1, source_target_pairs={{0,2},{1,3},{2,0},{3,1},{4,6},{5,7},{6,4},{7,5},{8,10},{9,11},{10,... | collective-permute-start | bytes 786440 | tf_op jit(solution)/shard_map/ppermute | solution.py:223
  122.7 9.3 %collective-permute-start.36 = (bf16[64,2048]{1,0:T(8,128)(2,1)S(1)}, bf16[64,2048]{1,0:T(8,128)(2,1)S(1)}, u32[]{:S(2)}, u32[]{:S(2)}) collective-permute-start(bf16[64,2048]{1,0:T(8,128)(2,1)S(1)} %get-tuple-element.33), channel_id=1, source_target_pairs={{0,2},{1,3},{2,0},{3,1},{4,6},{5,7},{6,4},{7,5},{8,10},{9,11},{10,... | collective-permute-start | bytes 786440 | tf_op jit(solution)/shard_map/ppermute | solution.py:223
  123.3 14.3 %collective-permute-start.8 = (bf16[64,2048]{1,0:T(8,128)(2,1)S(1)}, bf16[64,2048]{1,0:T(8,128)(2,1)S(1)}, u32[]{:S(2)}, u32[]{:S(2)}) collective-permute-start(bf16[64,2048]{1,0:T(8,128)(2,1)S(1)} %copy-done.18), channel_id=1, source_target_pairs={{0,2},{1,3},{2,0},{3,1},{4,6},{5,7},{6,4},{7,5},{8,10},{9,11},{10,... | collective-permute-start | bytes 786440 | tf_op jit(solution)/shard_map/ppermute | solution.py:223
  125.0 18.2 %collective-permute-start.10 = (bf16[64,2048]{1,0:T(8,128)(2,1)S(1)}, bf16[64,2048]{1,0:T(8,128)(2,1)S(1)}, u32[]{:S(2)}, u32[]{:S(2)}) collective-permute-start(bf16[64,2048]{1,0:T(8,128)(2,1)S(1)} %copy-done.16), channel_id=1, source_target_pairs={{0,2},{1,3},{2,0},{3,1},{4,6},{5,7},{6,4},{7,5},{8,10},{9,11},{10,... | collective-permute-start | bytes 786440 | tf_op jit(solution)/shard_map/ppermute | solution.py:223
  125.6 27.5 %copy-start.20 = (bf16[1,64,2048]{2,1,0:T(8,128)(2,1)S(1)}, bf16[1,64,2048]{2,1,0:T(8,128)(2,1)}, u32[]{:S(2)}) copy-start(bf16[1,64,2048]{2,1,0:T(8,128)(2,1)} %param.21) | copy-start | bytes 786436
  125.6 28.1 %copy-start.19 = (bf16[1,64,2048]{2,1,0:T(8,128)(2,1)S(1)}, bf16[1,64,2048]{2,1,0:T(8,128)(2,1)}, u32[]{:S(2)}) copy-start(bf16[1,64,2048]{2,1,0:T(8,128)(2,1)} %param.13) | copy-start | bytes 786436
  132.0 15.5 %collective-permute-start.15 = (bf16[64,2048]{1,0:T(8,128)(2,1)S(1)}, bf16[64,2048]{1,0:T(8,128)(2,1)S(1)}, u32[]{:S(2)}, u32[]{:S(2)}) collective-permute-start(bf16[64,2048]{1,0:T(8,128)(2,1)S(1)} %get-tuple-element.23), channel_id=1, source_target_pairs={{0,2},{1,3},{2,0},{3,1},{4,6},{5,7},{6,4},{7,5},{8,10},{9,11},{10,... | collective-permute-start | bytes 786440 | tf_op jit(solution)/shard_map/ppermute | solution.py:223
  137.6 13.9 %collective-permute-start.17 = (bf16[64,2048]{1,0:T(8,128)(2,1)S(1)}, bf16[64,2048]{1,0:T(8,128)(2,1)S(1)}, u32[]{:S(2)}, u32[]{:S(2)}) collective-permute-start(bf16[64,2048]{1,0:T(8,128)(2,1)S(1)} %get-tuple-element.25), channel_id=1, source_target_pairs={{0,2},{1,3},{2,0},{3,1},{4,6},{5,7},{6,4},{7,5},{8,10},{9,11},{10,... | collective-permute-start | bytes 786440 | tf_op jit(solution)/shard_map/ppermute | solution.py:223
  143.2 10.5 %collective-permute-start.28 = (bf16[64,2048]{1,0:T(8,128)(2,1)S(1)}, bf16[64,2048]{1,0:T(8,128)(2,1)S(1)}, u32[]{:S(2)}, u32[]{:S(2)}) collective-permute-start(bf16[64,2048]{1,0:T(8,128)(2,1)S(1)} %add_convert_fusion.3), channel_id=1, source_target_pairs={{0,28},{1,29},{2,30},{3,31},{4,16},{5,17},{6,18},{7,19},{8,20},{9,... | collective-permute-start | bytes 786440 | tf_op jit(solution)/shard_map/ppermute | solution.py:236
  147.5 12.8 %collective-permute-start.30 = (bf16[64,2048]{1,0:T(8,128)(2,1)S(1)}, bf16[64,2048]{1,0:T(8,128)(2,1)S(1)}, u32[]{:S(2)}, u32[]{:S(2)}) collective-permute-start(bf16[64,2048]{1,0:T(8,128)(2,1)S(1)} %add_convert_fusion.2), channel_id=1, source_target_pairs={{0,20},{1,21},{2,22},{3,23},{4,24},{5,25},{6,26},{7,27},{8,28},{9,... | collective-permute-start | bytes 786440 | tf_op jit(solution)/shard_map/ppermute | solution.py:236
  151.1 20.9 %collective-permute-start.35 = (bf16[64,2048]{1,0:T(8,128)(2,1)S(1)}, bf16[64,2048]{1,0:T(8,128)(2,1)S(1)}, u32[]{:S(2)}, u32[]{:S(2)}) collective-permute-start(bf16[64,2048]{1,0:T(8,128)(2,1)S(1)} %add_convert_fusion.1), channel_id=1, source_target_pairs={{0,24},{1,25},{2,26},{3,27},{4,28},{5,29},{6,30},{7,31},{8,16},{9,... | collective-permute-start | bytes 786440 | tf_op jit(solution)/shard_map/ppermute | solution.py:236
  151.5 22.9 %collective-permute-start.37 = (bf16[64,2048]{1,0:T(8,128)(2,1)S(1)}, bf16[64,2048]{1,0:T(8,128)(2,1)S(1)}, u32[]{:S(2)}, u32[]{:S(2)}) collective-permute-start(bf16[64,2048]{1,0:T(8,128)(2,1)S(1)} %add_convert_fusion), channel_id=1, source_target_pairs={{0,16},{1,17},{2,18},{3,19},{4,20},{5,21},{6,22},{7,23},{8,24},{9,... | collective-permute-start | bytes 786440 | tf_op jit(solution)/shard_map/ppermute | solution.py:236
  153.1 35.0 %collective-permute-start.19 = (bf16[64,2048]{1,0:T(8,128)(2,1)S(1)}, bf16[64,2048]{1,0:T(8,128)(2,1)S(1)}, u32[]{:S(2)}, u32[]{:S(2)}) collective-permute-start(bf16[64,2048]{1,0:T(8,128)(2,1)S(1)} %bitcast.27), channel_id=1, source_target_pairs={{0,16},{1,17},{2,18},{3,19},{4,20},{5,21},{6,22},{7,23},{8,24},{9,... | collective-permute-start | bytes 786440 | tf_op jit(solution)/shard_map/ppermute | solution.py:236
  153.7 40.4 %collective-permute-start = (bf16[64,2048]{1,0:T(8,128)(2,1)S(1)}, bf16[64,2048]{1,0:T(8,128)(2,1)S(1)}, u32[]{:S(2)}, u32[]{:S(2)}) collective-permute-start(bf16[64,2048]{1,0:T(8,128)(2,1)S(1)} %bitcast.25), channel_id=1, source_target_pairs={{0,16},{1,17},{2,18},{3,19},{4,20},{5,21},{6,22},{7,23},{8,24},{9,... | collective-permute-start | bytes 786440 | tf_op jit(solution)/shard_map/ppermute | solution.py:236
  160.3 33.9 %collective-permute-start.9 = (bf16[64,2048]{1,0:T(8,128)(2,1)S(1)}, bf16[64,2048]{1,0:T(8,128)(2,1)S(1)}, u32[]{:S(2)}, u32[]{:S(2)}) collective-permute-start(bf16[64,2048]{1,0:T(8,128)(2,1)S(1)} %add_convert_fusion.8), channel_id=1, source_target_pairs={{0,28},{1,29},{2,30},{3,31},{4,16},{5,17},{6,18},{7,19},{8,20},{9,... | collective-permute-start | bytes 786440 | tf_op jit(solution)/shard_map/ppermute | solution.py:236
  172.0 22.1 %collective-permute-start.11 = (bf16[64,2048]{1,0:T(8,128)(2,1)S(1)}, bf16[64,2048]{1,0:T(8,128)(2,1)S(1)}, u32[]{:S(2)}, u32[]{:S(2)}) collective-permute-start(bf16[64,2048]{1,0:T(8,128)(2,1)S(1)} %add_convert_fusion.7), channel_id=1, source_target_pairs={{0,20},{1,21},{2,22},{3,23},{4,24},{5,25},{6,26},{7,27},{8,28},{9,... | collective-permute-start | bytes 786440 | tf_op jit(solution)/shard_map/ppermute | solution.py:236
  174.5 19.7 %collective-permute-start.16 = (bf16[64,2048]{1,0:T(8,128)(2,1)S(1)}, bf16[64,2048]{1,0:T(8,128)(2,1)S(1)}, u32[]{:S(2)}, u32[]{:S(2)}) collective-permute-start(bf16[64,2048]{1,0:T(8,128)(2,1)S(1)} %add_convert_fusion.6), channel_id=1, source_target_pairs={{0,24},{1,25},{2,26},{3,27},{4,28},{5,29},{6,30},{7,31},{8,16},{9,... | collective-permute-start | bytes 786440 | tf_op jit(solution)/shard_map/ppermute | solution.py:236
  188.1 11.2 %collective-permute-start.18 = (bf16[64,2048]{1,0:T(8,128)(2,1)S(1)}, bf16[64,2048]{1,0:T(8,128)(2,1)S(1)}, u32[]{:S(2)}, u32[]{:S(2)}) collective-permute-start(bf16[64,2048]{1,0:T(8,128)(2,1)S(1)} %add_convert_fusion.5), channel_id=1, source_target_pairs={{0,16},{1,17},{2,18},{3,19},{4,20},{5,21},{6,22},{7,23},{8,24},{9,... | collective-permute-start | bytes 786440 | tf_op jit(solution)/shard_map/ppermute | solution.py:236

commit v2 on v0

v2 whole, which is shorter than its diff:
```python
import functools

import jax
import jax.numpy as jnp
from jax import lax
from jax.experimental import pallas as pl
from jax.experimental.pallas import tpu as pltpu
from jax.sharding import PartitionSpec as P

epsilon = 1e-06
f32 = jnp.float32
bf16 = jnp.bfloat16
LANES = 128
TILE = 256
OWN = f32
VMEM_LIMIT = 56 * 1024 * 1024
PACK_VMEM_LIMIT = 56 * 1024 * 1024
TURNED = (((1,), (1,)), ((), ()))


def inverse_rms(values):
    widened = values.astype(f32)
    return lax.rsqrt(jnp.mean(widened * widened, axis=-1, keepdims=True) + epsilon)


def pack_kernel(experts, dy, x, gain, ids_b, gates_b, ids_f, gates_f, x_b, out_b, out_f, pair):
    tokens, width = dy.shape
    wide = x[...].astype(f32)
    scale = lax.rsqrt(jnp.mean(wide * wide, axis=-1, keepdims=True) + epsilon)
    pair[:tokens, :] = x_b[...]
    pair[tokens:, :] = dy[...]
    values = (dy[...], (wide * scale * gain[...]).astype(bf16))
    spread = (experts, out_b.shape[1] - width)
    row = lax.broadcasted_iota(jnp.int32, spread, 0)
    lane = lax.broadcasted_iota(jnp.int32, spread, 1)
    first = jnp.where(lane == row, 1.0, 0.0).astype(bf16)
    second = jnp.where(lane == row + experts, 1.0, 0.0).astype(bf16)
    expert = lax.broadcasted_iota(jnp.int32, (experts, tokens), 0)
    turned = (((0,), (0,)), ((), ()))
    for i, (ids, gates, out) in enumerate(((ids_b, gates_b, out_b), (ids_f, gates_f, out_f))):
        dense = jnp.zeros((experts, tokens), f32)
        for k in range(ids.shape[0]):
            dense = dense + jnp.where(expert == ids[k : k + 1, :], gates[k : k + 1, :], 0.0)
        high = dense.astype(bf16)
        low = (dense - high.astype(f32)).astype(bf16)
        columns = lax.dot_general(high, first, turned, preferred_element_type=f32)
        columns += lax.dot_general(low, second, turned, preferred_element_type=f32)
        out[:, :width] = values[i]
        out[:, width:] = columns.astype(bf16)


def pack(experts, dy, x, gain, ids_b, gates_b, ids_f, gates_f, x_b):
    tokens, width = dy.shape
    columns = -(-2 * experts // LANES) * LANES
    vmem = pl.BlockSpec(memory_space=pltpu.VMEM)
    one = jax.ShapeDtypeStruct((tokens, width + columns), bf16)
    return pl.pallas_call(
        functools.partial(pack_kernel, experts),
        out_shape=[one, one, jax.ShapeDtypeStruct((2 * tokens, width), bf16)],
        in_specs=[vmem] * 8,
        out_specs=[vmem] * 3,
        compiler_params=pltpu.CompilerParams(vmem_limit_bytes=PACK_VMEM_LIMIT),
        name="pack",
    )(dy, x, gain, ids_b.T, gates_b.T, ids_f.T, gates_f.T, x_b)


def experts_kernel(backward, experts, tokens, capacity, chunk, apart, starts, table, *refs):
    count = len(starts)
    rows, refs = refs[:count], refs[count:]
    weights, refs = (refs[:3], refs[3:6]), refs[6:]
    if backward:
        kept, gain, refs = (refs[:2], refs[2:4]), refs[4], refs[5:]
    outs, refs = refs[: count // 2], refs[count // 2 :]
    sent, refs = (refs[: count // 2], refs[count // 2 :]) if apart else (refs[:1], refs[1:])
    gathered, columns_of, hidden, gates_ups, downs, sems = refs[:6]
    amount = count * tokens
    width = gathered.shape[1]
    inner = hidden.shape[1] // (4 if backward else 2)
    spaced = -(-capacity // 16) * 16
    slots = count * spaced

    copies = []

    def fetch(source, target):
        copies.append(pltpu.make_async_copy(source, target, sems.at[len(copies)]))
        copies[-1].start()
        return copies[-1]

    def fetch_first(e):
        if not backward:
            return [fetch(weights[e][j].at[0, 0], gates_ups.at[e, j]) for j in range(2)]
        group = [fetch(weights[e][2].at[0, 0], downs.at[e])]
        for i in range(count):
            block = table[chunk, 2 + i]
            for j in range(2):
                to = refs[6].at[e, j, i * spaced : i * spaced + capacity, :]
                group.append(fetch(kept[e][j].at[0, 0, block], to))
        return group

    def fetch_second(e):
        if not backward:
            return [fetch(weights[e][2].at[0, 0], downs.at[e])]
        return [fetch(weights[e][j].at[0, 0], gates_ups.at[e, j]) for j in range(2)]

    if backward and spaced != capacity:
        refs[6][...] = jnp.zeros_like(refs[6])
    group = []
    for i in range(count):
        here = slice(i * tokens, (i + 1) * tokens)
        source = slice(starts[i], starts[i] + tokens)
        group.append(fetch(rows[i].at[source, :width], gathered.at[here, :]))
        group.append(fetch(rows[i].at[source, width:], columns_of.at[here, :]))
    groups = [group, fetch_first(0), fetch_first(1)]
    for copy in groups[0]:
        copy.wait()

    columns = columns_of[...].astype(f32)
    lane = lax.broadcasted_iota(jnp.int32, columns.shape, 1)
    if backward:
        row = lax.broadcasted_iota(jnp.int32, (amount, amount), 0)
        column = lax.broadcasted_iota(jnp.int32, (amount, amount), 1)
        below = column < row
        placed_row = lax.broadcasted_iota(jnp.int32, (amount, slots), 0)
        base = jnp.zeros((amount, slots), jnp.int32)
        for i in range(1, count):
            below = below & ((row < i * tokens) | (column >= i * tokens))
            base = jnp.where(placed_row >= i * tokens, i * spaced, base)
        below = jnp.where(below, 1.0, 0.0).astype(bf16)
        slot_lane = lax.broadcasted_iota(jnp.int32, (amount, slots), 1)

    for e in range(2):
        expert = table[chunk, e]
        chosen = (lane == expert) | (lane == expert + experts)
        gate = jnp.sum(jnp.where(chosen, columns, 0.0), axis=1, keepdims=True)
        if backward:
            routed = jnp.broadcast_to(jnp.where(gate > 0.0, 1.0, 0.0), (amount, slots))
            before = jnp.dot(below, routed.astype(bf16), preferred_element_type=f32)
            target = before.astype(jnp.int32) + base
            place = jnp.where((slot_lane == target) & (routed > 0.0), 1.0, 0.0).astype(bf16)
        for copy in groups[1 + e]:
            copy.wait()
        groups.append(fetch_second(e))
        value = gathered[...]
        if not backward:
            gate_pre = jnp.dot(value, gates_ups[e, 0], preferred_element_type=f32)
            up_pre = jnp.dot(value, gates_ups[e, 1], preferred_element_type=f32)
            act = gate_pre * jax.nn.sigmoid(gate_pre) * (up_pre * gate)
            hidden[:, e * inner : (e + 1) * inner] = act.astype(bf16)
            continue
        d_act = gate * lax.dot_general(value, downs[e], TURNED, preferred_element_type=f32)
        g = jnp.dot(place, refs[6][e, 0], preferred_element_type=f32)
        u = jnp.dot(place, refs[6][e, 1], preferred_element_type=f32)
        q = jax.nn.sigmoid(g)
        at = 2 * e * inner
        hidden[:, at : at + inner] = (d_act * u * q * (1.0 + g * (1.0 - q))).astype(bf16)
        hidden[:, at + inner : at + 2 * inner] = (d_act * g * q).astype(bf16)

    total = None
    for e in range(2):
        for copy in groups[3 + e]:
            copy.wait()
        if backward:
            for j in range(2):
                left = hidden[:, (2 * e + j) * inner : (2 * e + j + 1) * inner]
                term = lax.dot_general(left, gates_ups[e, j], TURNED, preferred_element_type=f32)
                total = term if total is None else total + term
        else:
            left = hidden[:, e * inner : (e + 1) * inner]
            term = jnp.dot(left, downs[e], preferred_element_type=f32)
            total = term if total is None else total + term
    if backward:
        total = total * gain[...]
    for i in range(count):
        piece = total[i * tokens : (i + 1) * tokens, :]
        if i % 2 == 0:
            outs[i // 2][...] = piece.astype(outs[i // 2].dtype)
        else:
            at = 0 if apart else i // 2 * tokens
            sent[i // 2 if apart else 0][at : at + tokens, :] = piece.astype(bf16)


def run_experts(backward, experts, tokens, chunk, apart, table, rows, mine, theirs, kept_mine, kept_theirs, gain):
    count = len(rows)
    starts = [start for _, start in rows]
    rows = [array for array, _ in rows]
    width, inner = mine[0].shape[2:]
    capacity = kept_mine[0].shape[3]
    spaced = -(-capacity // 16) * 16
    vmem, anywhere = pl.BlockSpec(memory_space=pltpu.VMEM), pl.BlockSpec(memory_space=pl.ANY)
    operands = list(rows) + list(mine) + list(theirs)
    copies = 2 * count + 6
    scratch = [
        pltpu.VMEM((count * tokens, width), bf16),
        pltpu.VMEM((count * tokens, rows[0].shape[1] - width), bf16),
        pltpu.VMEM((count * tokens, (4 if backward else 2) * inner), bf16),
        pltpu.VMEM((2, 2, width, inner), bf16),
        pltpu.VMEM((2, inner, width), bf16),
    ]
    in_specs = [pl.BlockSpec(memory_space=pltpu.SMEM)] + [anywhere] * len(operands)
    if backward:
        operands += list(kept_mine) + list(kept_theirs) + [gain]
        in_specs += [anywhere] * 4 + [vmem]
        copies += 4 * count
    scratch.append(pltpu.SemaphoreType.DMA((copies,)))
    if backward:
        scratch.append(pltpu.VMEM((2, 2, count * spaced, inner), bf16))
    out_shape = [jax.ShapeDtypeStruct((tokens, width), OWN)] * (count // 2)
    if apart:
        out_shape += [jax.ShapeDtypeStruct((tokens, width), bf16)] * (count // 2)
    else:
        out_shape += [jax.ShapeDtypeStruct((count // 2 * tokens, width), bf16)]
    return pl.pallas_call(
        functools.partial(
            experts_kernel, backward, experts, tokens, capacity, chunk, apart, starts
        ),
        out_shape=out_shape,
        in_specs=in_specs,
        out_specs=[vmem] * len(out_shape),
        scratch_shapes=scratch,
        compiler_params=pltpu.CompilerParams(vmem_limit_bytes=VMEM_LIMIT),
        cost_estimate=pl.CostEstimate(
            flops=12 * count * tokens * width * inner,
            bytes_accessed=12 * width * inner,
            transcendentals=0,
        ),
        name="experts_backward" if backward else "experts_forward",
    )(table, *operands)


def shards(
    x_forward,
    norm_gain,
    w_gate,
    w_up,
    w_down,
    ids_forward,
    gates_forward,
    x_backward,
    dy_backward,
    ids_backward,
    gates_backward,
    saved_gate,
    saved_up,
):
    experts = lax.axis_size("expert")
    sections = lax.axis_size("section")
    line = experts // 4
    me = lax.axis_index("expert")
    a, b, c = me // 4, (me // 2) % 2, me % 2

    def swap(value, bit, label):
        with jax.named_scope(label):
            return lax.ppermute(value, "expert", [(i, i ^ bit) for i in range(experts)])

    def shift(value, steps, label):
        with jax.named_scope(label):
            return lax.ppermute(
                value, "expert", [(i, (i + 4 * steps) % experts) for i in range(experts)]
            )

    def relay(value, section_steps, label, steps=0):
        pairs = []
        for s in range(sections):
            for i in range(experts):
                target = ((s + section_steps) % sections) * experts + (i + 4 * steps) % experts
                pairs.append((s * experts + i, target))
        with jax.named_scope(label):
            return lax.ppermute(value, ("section", "expert"), pairs)

    order = [0, 1]
    for k in range(2, line // 2 + 1):
        order += [k, line + 1 - k]
    chunks = [order[i : i + 2] for i in range(0, line, 2)]
    last = len(chunks) - 1

    def after(value, *others):
        return lax.optimization_barrier((value,) + others)[0]

    def farther(held, k, label):
        if 2 * k <= line:
            return shift(held[k - 1], 1, f"T_{label}_z{k}")
        return shift(held[(k + 1) % line], -1, f"T_{label}_z{k}")

    def block_of(k, other):
        return (((a - k) % line) * 2 + (b ^ other)) * 2 + c

    def scalars_of(chunk):
        blocks = [block_of(k, o) for k in chunk for o in (0, 1)]
        return jnp.stack([me, me ^ 1] + blocks).astype(jnp.int32)

    gain = norm_gain
    input_rows = x_forward[0]
    tokens = input_rows.shape[0]
    table = jnp.stack([scalars_of(chunk) for chunk in chunks])
    packed = pack(
        experts, dy_backward[0], input_rows, gain,
        ids_backward[0], gates_backward[0], ids_forward[0], gates_forward[0], x_backward[0],
    )
    held = {True: {0: packed[0]}, False: {0: packed[1]}}
    across = {True: {}, False: {}}
    names = {True: "b", False: "f"}

    def go_along(backward, i, *earlier):
        before, moved = held[backward], []
        ready = {k: after(v, *earlier) for k, v in before.items()}
        for k in chunks[i]:
            if k:
                before[k] = farther(ready, k, names[backward])
                moved.append(before[k])
        return moved

    def go_across(backward, ks, *earlier):
        moved = []
        for k in ks:
            value = swap(after(held[backward][k], *earlier), 2, f"T_{names[backward]}_x{k}")
            across[backward][k] = value
            moved.append(value)
        return moved

    def experts_on(backward, i, *earlier):
        chunk, apart = chunks[i], not backward and i == last
        rows = [(r, 0) for k in chunk for r in (held[backward][k], across[backward][k])]
        out = run_experts(
            backward, experts, tokens, i, apart, after(table, *earlier), rows,
            mine, theirs, kept_mine, kept_theirs, gain,
        )
        return dict(zip(chunk, out)), out[len(chunk) :]

    def chip_sums(chunk, own, sent, label, *earlier):
        came = swap(after(sent[0], *earlier), 2, label)
        return {
            k: (own[k] + came[i * tokens : (i + 1) * tokens].astype(f32)).astype(bf16)
            for i, k in enumerate(chunk)
        }, came

    def send_sums(backward, sums, *earlier):
        moved = []
        for k, value in sums.items():
            label = f"T_{names[backward]}_r{k}"
            moved.append(relay(after(value, *earlier), -1 if backward else 1, label, -k))
        return moved

    wave = go_along(True, 0) + go_across(True, [0]) + go_across(False, [0])
    theirs_gate = swap(after(w_gate, packed[0]), 1, "T_wg")
    theirs_up = swap(after(w_up, packed[0]), 1, "T_wu")
    wave += [theirs_gate, theirs_up]
    table = after(table, *wave)
    theirs_down = swap(after(w_down, *wave), 1, "T_wd")
    theirs_kept_gate = swap(after(saved_gate, *wave), 1, "T_sg")
    theirs_kept_up = swap(after(saved_up, *wave), 1, "T_su")
    near = go_across(True, chunks[0][1:], *wave)
    wave = near + [theirs_down, theirs_kept_gate, theirs_kept_up]
    flying = go_along(True, 1)
    mine, theirs = (w_gate, w_up, w_down), (theirs_gate, theirs_up, theirs_down)
    kept_mine, kept_theirs = (saved_gate, saved_up), (theirs_kept_gate, theirs_kept_up)

    steps = [(True, i) for i in range(last + 1)] + [(False, i) for i in range(last + 1)]
    half = last + 1
    runs, sums, ends = {}, {}, {}
    came = {True: [], False: []}
    for p, (backward, i) in enumerate(steps):
        if backward and i:
            wave += go_across(True, chunks[i], *wave)
        moved, flying = flying, []
        if p == 0:
            moved += go_along(False, 0, *wave)
            pair = relay(after(packed[2], *wave), -1, "T_y2")
            moved.append(pair)
        if backward and 0 < i < last:
            moved += go_along(True, i + 1, *wave)
        ahead, side = p - half + 2, p - half + 1
        if 1 <= ahead <= last:
            moved += go_along(False, ahead, *wave)
        if 0 <= side <= last:
            moved += go_across(False, [k for k in chunks[side] if k], *wave)
        if p == half - 1:
            ends["residual"] = relay(after(input_rows, *wave), 1, "T_y1")
            moved.append(ends["residual"])
        if p >= 2:
            way, j = steps[p - 2]
            moved += send_sums(way, sums[p - 2], *wave)
            came[way] += moved[-len(chunks[j]) :]
        if p:
            way, j = steps[p - 1]
            sums[p - 1], arrived = chip_sums(
                chunks[j], *runs[p - 1], f"T_{names[way]}_s{j}", *wave
            )
            moved.append(arrived)
        runs[p] = experts_on(backward, i, *wave)
        wave = moved + list(runs[p][1])
    p = len(steps)
    came[False] += send_sums(False, sums[p - 2], *wave)
    own, sent = runs[p - 1]
    for k, value in zip(chunks[last], sent):
        arrived = swap(after(value, *wave), 2, f"T_f_s{k}")
        chip = (own[k] + arrived.astype(f32)).astype(bf16)
        came[False] += send_sums(False, {k: chip})
        wave = [arrived]

    def summed(values):
        total = values[0].astype(f32)
        for value in values[1:]:
            total = total + value.astype(f32)
        return total

    residual = ends["residual"].astype(f32)
    saved_input, gradient = pair[:tokens].astype(f32), pair[tokens:].astype(f32)
    weighted = summed(came[True])
    scale_rows = inverse_rms(saved_input)
    inner = jnp.mean(weighted * saved_input, axis=-1, keepdims=True)
    next_backward = (
        gradient
        + scale_rows * weighted
        - saved_input * scale_rows * scale_rows * scale_rows * inner
    ).astype(bf16)

    combined = summed(came[False])
    next_forward = (residual + combined).astype(bf16)
    return (next_forward[None], next_backward[None])


def solution(mesh):
    rows = P("section", "expert", None)
    weights = P("section", "expert", None, None)
    saved = P("section", "expert", None, None, None)
    placed = (
        rows, P("section", None), weights, weights, weights, rows, rows,
        rows, rows, rows, rows, saved, saved,
    )
    return jax.shard_map(
        shards, mesh=mesh, in_specs=placed, out_specs=(rows, rows), check_vma=False
    )
```

time: 406 us -> 147 us (0.36)
  the two profiles are of different devices: /device:TPU:10 before, /device:TPU:0 now
where the time goes in v2:
time: 147 us
  waiting for transfers between devices  52.7 us (36%)
  Pallas kernels  46.9 us (32%)
  starting transfers between devices  42 us (29%)
  other arithmetic  3.22 us (2%)
    pallas_call x4, Pallas kernels, run_experts(): pl.pallas_call(functools.partial(experts_kernel, backward, experts, token...  44.4 us
    ppermute x18, waiting for transfers between devices, swap(): return lax.ppermute(value, 'expert', [(i, i ^ bit) for i in range(experts)])  38.9 us
    ppermute x18, starting transfers between devices, swap(): return lax.ppermute(value, 'expert', [(i, i ^ bit) for i in range(experts)])  18.4 us
    ppermute x6, starting transfers between devices, shift(): lax.ppermute(value, 'expert', [(i, (i + 4 * steps) % experts) for i in ra...  12.9 us
    ppermute x10, waiting for transfers between devices, relay(): return lax.ppermute(value, ('section', 'expert'), pairs)  12.3 us
    ppermute x10, starting transfers between devices, relay(): return lax.ppermute(value, ('section', 'expert'), pairs)  10.7 us
  transfers between devices with their start and end apart: 34, of which 13 were waited for; matrix products, arithmetic and copies ran while one was open for 2% of the time, Pallas kernels for 30%

profile of v2, /device:TPU:0, one launch (start us, length us, event | category | flops | bytes accessed | tf_op | source)
XLA Modules:
  0.0 146.6 jit_solution(16356781760162065931)
XLA Ops:
  0.6 2.4 %pack.1 = (bf16[64,2176]{1,0:T(8,128)(2,1)}, bf16[64,2176]{1,0:T(8,128)(2,1)}, bf16[128,2048]{1,0:T(8,128)(2,1)}) custom-call(bf16[64,2048]{1,0:T(8,128)(2,1)} %bitcast.31, bf16[64,2048]{1,0:T(8,128)(2,1)} %bitcast.x, f32[1,2048]{1,0:T(1,128)} %refs_14_.3, s32[8,64]{1,0:T(8,128)} %bitcast.33, f32[8,64]{1,0:T(8,128)} %bitcast.34, s32[8,64]{1,0:T(8,128)} %bitcast.35, ...), custom_call_target="tpu_custom_call" | custom-call | tf_op jit(solution)/shard_map/pack/pallas_call | solution.py:57
  3.1 0.5 collective-permute-start.5
  3.5 0.1 collective-permute-start.6
  3.6 2.9 %collective-permute-start.4 = (bf16[64,2176]{1,0:T(8,128)(2,1)}, bf16[64,2176]{1,0:T(8,128)(2,1)S(1)}, u32[]{:S(2)}, u32[]{:S(2)}) collective-permute-start(bf16[64,2176]{1,0:T(8,128)(2,1)} %get-tuple-element.67.refs_0_), channel_id=1, source_target_pairs={{0,2},{1,3},{2,0},{3,1},{4,6},{5,7},{6,4},{7,5},{8,10},{9,11},{10,... | collective-permute-start | bytes 835592 | tf_op jit(solution)/shard_map/T_f_x0/ppermute | solution.py:253
  6.5 0.0 collective-permute-start.3
  6.6 2.1 %collective-permute-start = (bf16[64,2176]{1,0:T(8,128)(2,1)}, bf16[64,2176]{1,0:T(8,128)(2,1)}, u32[]{:S(2)}, u32[]{:S(2)}) collective-permute-start(bf16[64,2176]{1,0:T(8,128)(2,1)} %get-tuple-element.49.refs_0_), channel_id=1, source_target_pairs={{0,4},{1,5},{2,6},{3,7},{4,8},{5,9},{6,10},{7,11},{8,12},{9,13},{1... | collective-permute-start | bytes 835592 | tf_op jit(solution)/shard_map/T_b_z1/ppermute | solution.py:257
  8.6 5.6 %collective-permute-done.4.refs_1_ = bf16[64,2176]{1,0:T(8,128)(2,1)S(1)} collective-permute-done((bf16[64,2176]{1,0:T(8,128)(2,1)}, bf16[64,2176]{1,0:T(8,128)(2,1)S(1)}, u32[]{:S(2)}, u32[]{:S(2)}) %collective-permute-start.4) | collective-permute-done | bytes 278560 | tf_op jit(solution)/shard_map/T_f_x0/ppermute | solution.py:253
  14.2 5.3 %collective-permute-done.3.refs_1_ = bf16[64,2176]{1,0:T(8,128)(2,1)S(1)} collective-permute-done((bf16[64,2176]{1,0:T(8,128)(2,1)}, bf16[64,2176]{1,0:T(8,128)(2,1)S(1)}, u32[]{:S(2)}, u32[]{:S(2)}) %collective-permute-start.3) | collective-permute-done | bytes 278560 | tf_op jit(solution)/shard_map/T_b_x0/ppermute | solution.py:253
  19.5 0.7 copy-done.17
  20.3 0.5 collective-permute-start.9
  20.8 0.1 collective-permute-start.10
  20.8 1.7 %collective-permute-start.7 = (bf16[64,2176]{1,0:T(8,128)(2,1)}, bf16[64,2176]{1,0:T(8,128)(2,1)}, u32[]{:S(2)}, u32[]{:S(2)}) collective-permute-start(bf16[64,2176]{1,0:T(8,128)(2,1)} %collective-permute-done.refs_2_), channel_id=1, source_target_pairs={{0,2},{1,3},{2,0},{3,1},{4,6},{5,7},{6,4},{7,5},{8,10},{9,11},{10,... | collective-permute-start | bytes 835592 | tf_op jit(solution)/shard_map/T_b_x1/ppermute | solution.py:253
  22.6 3.6 %collective-permute-start.2 = (bf16[64,2176]{1,0:T(8,128)(2,1)}, bf16[64,2176]{1,0:T(8,128)(2,1)}, u32[]{:S(2)}, u32[]{:S(2)}) collective-permute-start(bf16[64,2176]{1,0:T(8,128)(2,1)} %get-tuple-element.49.refs_0_), channel_id=1, source_target_pairs={{0,12},{1,13},{2,14},{3,15},{4,0},{5,1},{6,2},{7,3},{8,4},{9,5},{1... | collective-permute-start | bytes 835592 | tf_op jit(solution)/shard_map/T_b_z3/ppermute | solution.py:257
  26.2 0.1 stack.59
  26.3 0.1 stack.53
  26.3 3.8 %collective-permute-done.7.refs_3_ = bf16[64,2176]{1,0:T(8,128)(2,1)} collective-permute-done((bf16[64,2176]{1,0:T(8,128)(2,1)}, bf16[64,2176]{1,0:T(8,128)(2,1)}, u32[]{:S(2)}, u32[]{:S(2)}) %collective-permute-start.7) | collective-permute-done | bytes 278560 | tf_op jit(solution)/shard_map/T_b_x1/ppermute | solution.py:253
  30.2 1.8 %collective-permute-start.12 = (bf16[128,2048]{1,0:T(8,128)(2,1)}, bf16[128,2048]{1,0:T(8,128)(2,1)S(1)}, u32[]{:S(2)}, u32[]{:S(2)}) collective-permute-start(bf16[128,2048]{1,0:T(8,128)(2,1)} %get-tuple-element.59), channel_id=1, source_target_pairs={{0,16},{1,17},{2,18},{3,19},{4,20},{5,21},{6,22},{7,23},{8,24},{9,... | collective-permute-start | bytes 1572872 | tf_op jit(solution)/shard_map/T_y2/ppermute | solution.py:268
  32.0 0.6 pad_add_fusion.table
  32.6 1.6 %collective-permute-start.1 = (bf16[64,2176]{1,0:T(8,128)(2,1)}, bf16[64,2176]{1,0:T(8,128)(2,1)S(1)}, u32[]{:S(2)}, u32[]{:S(2)}) collective-permute-start(bf16[64,2176]{1,0:T(8,128)(2,1)} %collective-permute-done.refs_2_), channel_id=1, source_target_pairs={{0,4},{1,5},{2,6},{3,7},{4,8},{5,9},{6,10},{7,11},{8,12},{9,13},{1... | collective-permute-start | bytes 835592 | tf_op jit(solution)/shard_map/T_b_z2/ppermute | solution.py:257
  34.2 1.6 %collective-permute-start.11 = (bf16[64,2176]{1,0:T(8,128)(2,1)}, bf16[64,2176]{1,0:T(8,128)(2,1)S(1)}, u32[]{:S(2)}, u32[]{:S(2)}) collective-permute-start(bf16[64,2176]{1,0:T(8,128)(2,1)} %get-tuple-element.67.refs_0_), channel_id=1, source_target_pairs={{0,4},{1,5},{2,6},{3,7},{4,8},{5,9},{6,10},{7,11},{8,12},{9,13},{1... | collective-permute-start | bytes 835592 | tf_op jit(solution)/shard_map/T_f_z1/ppermute | solution.py:257
  35.7 11.4 %experts_backward.2 = (f32[64,2048]{1,0:T(8,128)}, f32[64,2048]{1,0:T(8,128)}, bf16[128,2048]{1,0:T(8,128)(2,1)}) custom-call(s32[2,6]{1,0:T(2,128)} %pad_add_fusion.table, bf16[64,2176]{1,0:T(8,128)(2,1)} %get-tuple-element.49.refs_0_, bf16[64,2176]{1,0:T(8,128)(2,1)} %copy-done.17, bf16[64,2176]{1,0:T(8,128)(2,1)} %collective-permute-done.refs_2_, ...), custom_call_target="tpu_custom_call" | custom-call | flops 4831838208 | bytes 18874368 | tf_op jit(solution)/shard_map/experts_backward/pallas_call | solution.py:212
  47.2 1.4 collective-permute-done.11.refs_2_
  48.6 1.6 %collective-permute-start.13 = (bf16[64,2176]{1,0:T(8,128)(2,1)S(1)}, bf16[64,2176]{1,0:T(8,128)(2,1)S(1)}, u32[]{:S(2)}, u32[]{:S(2)}) collective-permute-start(bf16[64,2176]{1,0:T(8,128)(2,1)S(1)} %collective-permute-done.1.refs_0_), channel_id=1, source_target_pairs={{0,2},{1,3},{2,0},{3,1},{4,6},{5,7},{6,4},{7,5},{8,10},{9,11},{10,... | collective-permute-start | bytes 835592 | tf_op jit(solution)/shard_map/T_b_x2/ppermute | solution.py:253
  50.1 0.5 collective-permute-start.14
  50.7 7.6 %collective-permute-done.13.refs_1_ = bf16[64,2176]{1,0:T(8,128)(2,1)S(1)} collective-permute-done((bf16[64,2176]{1,0:T(8,128)(2,1)S(1)}, bf16[64,2176]{1,0:T(8,128)(2,1)S(1)}, u32[]{:S(2)}, u32[]{:S(2)}) %collective-permute-start.13) | collective-permute-done | bytes 278560 | tf_op jit(solution)/shard_map/T_b_x2/ppermute | solution.py:253
  58.2 3.4 %collective-permute-done.14.refs_3_ = bf16[64,2176]{1,0:T(8,128)(2,1)S(1)} collective-permute-done((bf16[64,2176]{1,0:T(8,128)(2,1)}, bf16[64,2176]{1,0:T(8,128)(2,1)S(1)}, u32[]{:S(2)}, u32[]{:S(2)}) %collective-permute-start.14) | collective-permute-done | bytes 278560 | tf_op jit(solution)/shard_map/T_b_x3/ppermute | solution.py:253
  61.7 1.5 %collective-permute-start.19 = (bf16[128,2048]{1,0:T(8,128)(2,1)}, bf16[128,2048]{1,0:T(8,128)(2,1)S(1)}, u32[]{:S(2)}, u32[]{:S(2)}) collective-permute-start(bf16[128,2048]{1,0:T(8,128)(2,1)} %get-tuple-element.68), channel_id=1, source_target_pairs={{0,2},{1,3},{2,0},{3,1},{4,6},{5,7},{6,4},{7,5},{8,10},{9,11},{10,... | collective-permute-start | bytes 1572872 | tf_op jit(solution)/shard_map/T_b_s0/ppermute | solution.py:253
  63.2 0.5 collective-permute-start.18
  63.7 0.5 collective-permute-start.16
  64.2 0.5 collective-permute-start.15
  64.7 3.5 %collective-permute-start.17 = (bf16[64,2176]{1,0:T(8,128)(2,1)S(1)}, bf16[64,2176]{1,0:T(8,128)(2,1)S(1)}, u32[]{:S(2)}, u32[]{:S(2)}) collective-permute-start(bf16[64,2176]{1,0:T(8,128)(2,1)S(1)} %copy-done.9), channel_id=1, source_target_pairs={{0,12},{1,13},{2,14},{3,15},{4,0},{5,1},{6,2},{7,3},{8,4},{9,5},{1... | collective-permute-start | bytes 835592 | tf_op jit(solution)/shard_map/T_f_z3/ppermute | solution.py:257
  68.3 11.4 %experts_backward.3 = (f32[64,2048]{1,0:T(8,128)}, f32[64,2048]{1,0:T(8,128)}, bf16[128,2048]{1,0:T(8,128)(2,1)}) custom-call(s32[2,6]{1,0:T(2,128)} %pad_add_fusion.table, bf16[64,2176]{1,0:T(8,128)(2,1)} %copy-done.18, bf16[64,2176]{1,0:T(8,128)(2,1)} %copy-done.19, bf16[64,2176]{1,0:T(8,128)(2,1)} %collective-permute-done.2.refs_2_, ...), custom_call_target="tpu_custom_call" | custom-call | flops 4831838208 | bytes 18874368 | tf_op jit(solution)/shard_map/experts_backward/pallas_call | solution.py:212
  79.8 1.4 collective-permute-start.24
  81.2 0.1 add_convert_fusion.7
  81.4 1.5 collective-permute-start.22
  82.8 1.7 %collective-permute-start.23 = (bf16[64,2048]{1,0:T(8,128)(2,1)S(1)}, bf16[64,2048]{1,0:T(8,128)(2,1)S(1)}, u32[]{:S(2)}, u32[]{:S(2)}) collective-permute-start(bf16[64,2048]{1,0:T(8,128)(2,1)S(1)} %get-tuple-element.79), channel_id=1, source_target_pairs={{0,28},{1,29},{2,30},{3,31},{4,16},{5,17},{6,18},{7,19},{8,20},{9,... | collective-permute-start | bytes 786440 | tf_op jit(solution)/shard_map/T_b_r1/ppermute | solution.py:268
  84.6 0.5 collective-permute-start.20
  85.1 1.5 %collective-permute-start.21 = (bf16[64,2176]{1,0:T(8,128)(2,1)S(1)}, bf16[64,2176]{1,0:T(8,128)(2,1)S(1)}, u32[]{:S(2)}, u32[]{:S(2)}) collective-permute-start(bf16[64,2176]{1,0:T(8,128)(2,1)S(1)} %collective-permute-done.17.refs_2_), channel_id=1, source_target_pairs={{0,2},{1,3},{2,0},{3,1},{4,6},{5,7},{6,4},{7,5},{8,10},{9,11},{10,... | collective-permute-start | bytes 835592 | tf_op jit(solution)/shard_map/T_f_x3/ppermute | solution.py:253
  86.6 10.8 %experts_forward.2 = (f32[64,2048]{1,0:T(8,128)}, f32[64,2048]{1,0:T(8,128)}, bf16[128,2048]{1,0:T(8,128)(2,1)}) custom-call(s32[2,6]{1,0:T(2,128)} %pad_add_fusion.table, bf16[64,2176]{1,0:T(8,128)(2,1)} %get-tuple-element.67.refs_0_, bf16[64,2176]{1,0:T(8,128)(2,1)} %copy-done.10, bf16[64,2176]{1,0:T(8,128)(2,1)} %copy-done.12, ...), custom_call_target="tpu_custom_call" | custom-call | flops 4831838208 | bytes 18874368 | tf_op jit(solution)/shard_map/experts_forward/pallas_call | solution.py:212
  97.5 0.1 add_convert_fusion.4
  97.6 1.8 %collective-permute-done.20.refs_1_ = bf16[64,2176]{1,0:T(8,128)(2,1)S(1)} collective-permute-done((bf16[64,2176]{1,0:T(8,128)(2,1)S(1)}, bf16[64,2176]{1,0:T(8,128)(2,1)S(1)}, u32[]{:S(2)}, u32[]{:S(2)}) %collective-permute-start.20) | collective-permute-done | bytes 278560 | tf_op jit(solution)/shard_map/T_f_x2/ppermute | solution.py:253
  99.4 3.0 %collective-permute-done.21.refs_3_ = bf16[64,2176]{1,0:T(8,128)(2,1)S(1)} collective-permute-done((bf16[64,2176]{1,0:T(8,128)(2,1)S(1)}, bf16[64,2176]{1,0:T(8,128)(2,1)S(1)}, u32[]{:S(2)}, u32[]{:S(2)}) %collective-permute-start.21) | collective-permute-done | bytes 278560 | tf_op jit(solution)/shard_map/T_f_x3/ppermute | solution.py:253
  102.4 0.6 collective-permute-start.26
  103.0 2.5 %collective-permute-start.27 = (bf16[64,2048]{1,0:T(8,128)(2,1)S(1)}, bf16[64,2048]{1,0:T(8,128)(2,1)S(1)}, u32[]{:S(2)}, u32[]{:S(2)}) collective-permute-start(bf16[64,2048]{1,0:T(8,128)(2,1)S(1)} %get-tuple-element.85), channel_id=1, source_target_pairs={{0,20},{1,21},{2,22},{3,23},{4,24},{5,25},{6,26},{7,27},{8,28},{9,... | collective-permute-start | bytes 786440 | tf_op jit(solution)/shard_map/T_b_r3/ppermute | solution.py:268
  105.5 1.5 %collective-permute-start.25 = (bf16[128,2048]{1,0:T(8,128)(2,1)}, bf16[128,2048]{1,0:T(8,128)(2,1)S(1)}, u32[]{:S(2)}, u32[]{:S(2)}) collective-permute-start(bf16[128,2048]{1,0:T(8,128)(2,1)} %get-tuple-element.81), channel_id=1, source_target_pairs={{0,2},{1,3},{2,0},{3,1},{4,6},{5,7},{6,4},{7,5},{8,10},{9,11},{10,... | collective-permute-start | bytes 1572872 | tf_op jit(solution)/shard_map/T_f_s0/ppermute | solution.py:253
  107.0 10.8 %experts_forward.3 = (f32[64,2048]{1,0:T(8,128)}, f32[64,2048]{1,0:T(8,128)}, bf16[64,2048]{1,0:T(8,128)(2,1)}, bf16[64,2048]{1,0:T(8,128)(2,1)}) custom-call(s32[2,6]{1,0:T(2,128)} %pad_add_fusion.table, bf16[64,2176]{1,0:T(8,128)(2,1)} %copy-done.11, bf16[64,2176]{1,0:T(8,128)(2,1)} %copy-done.15, bf16[64,2176]{1,0:T(8,128)(2,1)} %copy-done.13, ...), custom_call_target="tpu_custom_call" | custom-call | flops 4831838208 | bytes 18874368 | tf_op jit(solution)/shard_map/experts_forward/pallas_call | solution.py:212
  117.9 0.0 copy-start.21
  117.9 1.5 %collective-permute-done.26 = bf16[64,2048]{1,0:T(8,128)(2,1)S(1)} collective-permute-done((bf16[64,2048]{1,0:T(8,128)(2,1)S(1)}, bf16[64,2048]{1,0:T(8,128)(2,1)S(1)}, u32[]{:S(2)}, u32[]{:S(2)}) %collective-permute-start.26) | collective-permute-done | bytes 262176 | tf_op jit(solution)/shard_map/T_b_r2/ppermute | solution.py:268
  119.4 0.3 fusion
  119.7 1.7 %collective-permute-start.30 = (bf16[64,2048]{1,0:T(8,128)(2,1)}, bf16[64,2048]{1,0:T(8,128)(2,1)S(1)}, u32[]{:S(2)}, u32[]{:S(2)}) collective-permute-start(bf16[64,2048]{1,0:T(8,128)(2,1)} %get-tuple-element.93), channel_id=1, source_target_pairs={{0,2},{1,3},{2,0},{3,1},{4,6},{5,7},{6,4},{7,5},{8,10},{9,11},{10,... | collective-permute-start | bytes 786440 | tf_op jit(solution)/shard_map/T_f_s2/ppermute | solution.py:253
  121.4 0.1 add_convert_fusion.6
  121.5 0.1 collective-permute-start.29
  121.6 1.1 collective-permute-start.28
  122.7 4.3 %collective-permute-done.30 = bf16[64,2048]{1,0:T(8,128)(2,1)S(1)} collective-permute-done((bf16[64,2048]{1,0:T(8,128)(2,1)}, bf16[64,2048]{1,0:T(8,128)(2,1)S(1)}, u32[]{:S(2)}, u32[]{:S(2)}) %collective-permute-start.30) | collective-permute-done | bytes 262176 | tf_op jit(solution)/shard_map/T_f_s2/ppermute | solution.py:253
  127.0 1.7 %collective-permute-start.32 = (bf16[64,2048]{1,0:T(8,128)(2,1)S(1)}, bf16[64,2048]{1,0:T(8,128)(2,1)S(1)}, u32[]{:S(2)}, u32[]{:S(2)}) collective-permute-start(bf16[64,2048]{1,0:T(8,128)(2,1)S(1)} %copy-done.21), channel_id=1, source_target_pairs={{0,2},{1,3},{2,0},{3,1},{4,6},{5,7},{6,4},{7,5},{8,10},{9,11},{10,... | collective-permute-start | bytes 786440 | tf_op jit(solution)/shard_map/T_f_s3/ppermute | solution.py:253
  128.7 0.1 add_convert_fusion.2
  128.8 0.4 collective-permute-start.31
  129.2 4.1 %collective-permute-done.32 = bf16[64,2048]{1,0:T(8,128)(2,1)S(1)} collective-permute-done((bf16[64,2048]{1,0:T(8,128)(2,1)S(1)}, bf16[64,2048]{1,0:T(8,128)(2,1)S(1)}, u32[]{:S(2)}, u32[]{:S(2)}) %collective-permute-start.32) | collective-permute-done | bytes 262176 | tf_op jit(solution)/shard_map/T_f_s3/ppermute | solution.py:253
  133.3 0.1 add_convert_fusion.1
  133.4 0.5 collective-permute-start.33
  133.9 1.0 fusion.8
  134.9 0.2 collective-permute-done.28
  135.1 10.7 %collective-permute-done.31 = bf16[64,2048]{1,0:T(8,128)(2,1)S(1)} collective-permute-done((bf16[64,2048]{1,0:T(8,128)(2,1)S(1)}, bf16[64,2048]{1,0:T(8,128)(2,1)S(1)}, u32[]{:S(2)}, u32[]{:S(2)}) %collective-permute-start.31) | collective-permute-done | bytes 262176 | tf_op jit(solution)/shard_map/T_f_r2/ppermute | solution.py:268
  145.8 0.9 fusion.7
  (65 shorter events, 0.1 us)
Async XLA Ops:
  3.1 16.5 %collective-permute-start.5 = (bf16[1,1,2048,768]{3,2,1,0:T(8,128)(2,1)}, bf16[1,1,2048,768]{3,2,1,0:T(8,128)(2,1)S(1)}, u32[]{:S(2)}, u32[]{:S(2)}) collective-permute-start(bf16[1,1,2048,768]{3,2,1,0:T(8,128)(2,1)} %refs_4_.7), channel_id=1, source_target_pairs={{0,1},{1,0},{2,3},{3,2},{4,5},{5,4},{6,7},{7,6},{8,9},{9,8},{10,11... | collective-permute-start | bytes 9437192 | tf_op jit(solution)/shard_map/T_wg/ppermute | solution.py:253
  3.5 16.7 %collective-permute-start.6 = (bf16[1,1,2048,768]{3,2,1,0:T(8,128)(2,1)}, bf16[1,1,2048,768]{3,2,1,0:T(8,128)(2,1)}, u32[]{:S(2)}, u32[]{:S(2)}) collective-permute-start(bf16[1,1,2048,768]{3,2,1,0:T(8,128)(2,1)} %refs_5_.7), channel_id=1, source_target_pairs={{0,1},{1,0},{2,3},{3,2},{4,5},{5,4},{6,7},{7,6},{8,9},{9,8},{10,11... | collective-permute-start | bytes 9437192 | tf_op jit(solution)/shard_map/T_wu/ppermute | solution.py:253
  3.6 10.6 %collective-permute-start.4 = (bf16[64,2176]{1,0:T(8,128)(2,1)}, bf16[64,2176]{1,0:T(8,128)(2,1)S(1)}, u32[]{:S(2)}, u32[]{:S(2)}) collective-permute-start(bf16[64,2176]{1,0:T(8,128)(2,1)} %get-tuple-element.67.refs_0_), channel_id=1, source_target_pairs={{0,2},{1,3},{2,0},{3,1},{4,6},{5,7},{6,4},{7,5},{8,10},{9,11},{10,... | collective-permute-start | bytes 835592 | tf_op jit(solution)/shard_map/T_f_x0/ppermute | solution.py:253
  6.5 13.0 %collective-permute-start.3 = (bf16[64,2176]{1,0:T(8,128)(2,1)}, bf16[64,2176]{1,0:T(8,128)(2,1)S(1)}, u32[]{:S(2)}, u32[]{:S(2)}) collective-permute-start(bf16[64,2176]{1,0:T(8,128)(2,1)} %get-tuple-element.49.refs_0_), channel_id=1, source_target_pairs={{0,2},{1,3},{2,0},{3,1},{4,6},{5,7},{6,4},{7,5},{8,10},{9,11},{10,... | collective-permute-start | bytes 835592 | tf_op jit(solution)/shard_map/T_b_x0/ppermute | solution.py:253
  6.6 13.0 %collective-permute-start = (bf16[64,2176]{1,0:T(8,128)(2,1)}, bf16[64,2176]{1,0:T(8,128)(2,1)}, u32[]{:S(2)}, u32[]{:S(2)}) collective-permute-start(bf16[64,2176]{1,0:T(8,128)(2,1)} %get-tuple-element.49.refs_0_), channel_id=1, source_target_pairs={{0,4},{1,5},{2,6},{3,7},{4,8},{5,9},{6,10},{7,11},{8,12},{9,13},{1... | collective-permute-start | bytes 835592 | tf_op jit(solution)/shard_map/T_b_z1/ppermute | solution.py:257
  14.2 32.9 %copy-start.10 = (bf16[64,2176]{1,0:T(8,128)(2,1)}, bf16[64,2176]{1,0:T(8,128)(2,1)S(1)}, u32[]{:S(2)}) copy-start(bf16[64,2176]{1,0:T(8,128)(2,1)S(1)} %collective-permute-done.4.refs_1_) | copy-start | bytes 835588
  19.5 0.7 copy-start.17
  20.2 15.5 %copy-start = (bf16[1,1,2048,768]{3,2,1,0:T(8,128)(2,1)}, bf16[1,1,2048,768]{3,2,1,0:T(8,128)(2,1)S(1)}, u32[]{:S(2)}) copy-start(bf16[1,1,2048,768]{3,2,1,0:T(8,128)(2,1)S(1)} %collective-permute-done.5.refs_7_) | copy-start | bytes 9437188
  20.2 9.9 %collective-permute-start.8 = (bf16[1,1,768,2048]{3,2,1,0:T(8,128)(2,1)}, bf16[1,1,768,2048]{3,2,1,0:T(8,128)(2,1)}, u32[]{:S(2)}, u32[]{:S(2)}) collective-permute-start(bf16[1,1,768,2048]{3,2,1,0:T(8,128)(2,1)} %refs_6_.7), channel_id=1, source_target_pairs={{0,1},{1,0},{2,3},{3,2},{4,5},{5,4},{6,7},{7,6},{8,9},{9,8},{10,11... | collective-permute-start | bytes 9437192 | tf_op jit(solution)/shard_map/T_wd/ppermute | solution.py:253
  20.3 9.9 %collective-permute-start.9 = (bf16[1,1,16,48,768]{4,3,2,1,0:T(8,128)(2,1)}, bf16[1,1,16,48,768]{4,3,2,1,0:T(8,128)(2,1)}, u32[]{:S(2)}, u32[]{:S(2)}) collective-permute-start(bf16[1,1,16,48,768]{4,3,2,1,0:T(8,128)(2,1)} %refs_10_.3), channel_id=1, source_target_pairs={{0,1},{1,0},{2,3},{3,2},{4,5},{5,4},{6,7},{7,6},{8,9},{9,8},{10,11... | collective-permute-start | bytes 3538952 | tf_op jit(solution)/shard_map/T_sg/ppermute | solution.py:253
  20.8 9.4 %collective-permute-start.10 = (bf16[1,1,16,48,768]{4,3,2,1,0:T(8,128)(2,1)}, bf16[1,1,16,48,768]{4,3,2,1,0:T(8,128)(2,1)}, u32[]{:S(2)}, u32[]{:S(2)}) collective-permute-start(bf16[1,1,16,48,768]{4,3,2,1,0:T(8,128)(2,1)} %refs_11_.3), channel_id=1, source_target_pairs={{0,1},{1,0},{2,3},{3,2},{4,5},{5,4},{6,7},{7,6},{8,9},{9,8},{10,11... | collective-permute-start | bytes 3538952 | tf_op jit(solution)/shard_map/T_su/ppermute | solution.py:253
  20.8 9.3 %collective-permute-start.7 = (bf16[64,2176]{1,0:T(8,128)(2,1)}, bf16[64,2176]{1,0:T(8,128)(2,1)}, u32[]{:S(2)}, u32[]{:S(2)}) collective-permute-start(bf16[64,2176]{1,0:T(8,128)(2,1)} %collective-permute-done.refs_2_), channel_id=1, source_target_pairs={{0,2},{1,3},{2,0},{3,1},{4,6},{5,7},{6,4},{7,5},{8,10},{9,11},{10,... | collective-permute-start | bytes 835592 | tf_op jit(solution)/shard_map/T_b_x1/ppermute | solution.py:253
  22.6 24.6 %collective-permute-start.2 = (bf16[64,2176]{1,0:T(8,128)(2,1)}, bf16[64,2176]{1,0:T(8,128)(2,1)}, u32[]{:S(2)}, u32[]{:S(2)}) collective-permute-start(bf16[64,2176]{1,0:T(8,128)(2,1)} %get-tuple-element.49.refs_0_), channel_id=1, source_target_pairs={{0,12},{1,13},{2,14},{3,15},{4,0},{5,1},{6,2},{7,3},{8,4},{9,5},{1... | collective-permute-start | bytes 835592 | tf_op jit(solution)/shard_map/T_b_z3/ppermute | solution.py:257
  30.2 18.4 %collective-permute-start.12 = (bf16[128,2048]{1,0:T(8,128)(2,1)}, bf16[128,2048]{1,0:T(8,128)(2,1)S(1)}, u32[]{:S(2)}, u32[]{:S(2)}) collective-permute-start(bf16[128,2048]{1,0:T(8,128)(2,1)} %get-tuple-element.59), channel_id=1, source_target_pairs={{0,16},{1,17},{2,18},{3,19},{4,20},{5,21},{6,22},{7,23},{8,24},{9,... | collective-permute-start | bytes 1572872 | tf_op jit(solution)/shard_map/T_y2/ppermute | solution.py:268
  32.6 32.2 %copy-start.9 = (bf16[64,2176]{1,0:T(8,128)(2,1)S(1)}, bf16[64,2176]{1,0:T(8,128)(2,1)}, u32[]{:S(2)}) copy-start(bf16[64,2176]{1,0:T(8,128)(2,1)} %get-tuple-element.67.refs_0_) | copy-start | bytes 835588
  32.6 14.6 %collective-permute-start.1 = (bf16[64,2176]{1,0:T(8,128)(2,1)}, bf16[64,2176]{1,0:T(8,128)(2,1)S(1)}, u32[]{:S(2)}, u32[]{:S(2)}) collective-permute-start(bf16[64,2176]{1,0:T(8,128)(2,1)} %collective-permute-done.refs_2_), channel_id=1, source_target_pairs={{0,4},{1,5},{2,6},{3,7},{4,8},{5,9},{6,10},{7,11},{8,12},{9,13},{1... | collective-permute-start | bytes 835592 | tf_op jit(solution)/shard_map/T_b_z2/ppermute | solution.py:257
  34.2 14.4 %collective-permute-start.11 = (bf16[64,2176]{1,0:T(8,128)(2,1)}, bf16[64,2176]{1,0:T(8,128)(2,1)S(1)}, u32[]{:S(2)}, u32[]{:S(2)}) collective-permute-start(bf16[64,2176]{1,0:T(8,128)(2,1)} %get-tuple-element.67.refs_0_), channel_id=1, source_target_pairs={{0,4},{1,5},{2,6},{3,7},{4,8},{5,9},{6,10},{7,11},{8,12},{9,13},{1... | collective-permute-start | bytes 835592 | tf_op jit(solution)/shard_map/T_f_z1/ppermute | solution.py:257
  47.2 21.1 %copy-start.18 = (bf16[64,2176]{1,0:T(8,128)(2,1)}, bf16[64,2176]{1,0:T(8,128)(2,1)S(1)}, u32[]{:S(2)}) copy-start(bf16[64,2176]{1,0:T(8,128)(2,1)S(1)} %collective-permute-done.1.refs_0_) | copy-start | bytes 835588
  48.5 31.1 %copy-start.12 = (bf16[64,2176]{1,0:T(8,128)(2,1)}, bf16[64,2176]{1,0:T(8,128)(2,1)S(1)}, u32[]{:S(2)}) copy-start(bf16[64,2176]{1,0:T(8,128)(2,1)S(1)} %collective-permute-done.11.refs_2_) | copy-start | bytes 835588
  48.6 32.7 %copy-start.3 = (f32[64,2048]{1,0:T(8,128)S(1)}, f32[64,2048]{1,0:T(8,128)}, u32[]{:S(2)}) copy-start(f32[64,2048]{1,0:T(8,128)} %get-tuple-element.76) | copy-start | bytes 1572868
  48.6 32.7 %copy-start.4 = (f32[64,2048]{1,0:T(8,128)S(1)}, f32[64,2048]{1,0:T(8,128)}, u32[]{:S(2)}) copy-start(f32[64,2048]{1,0:T(8,128)} %get-tuple-element.78) | copy-start | bytes 1572868
  48.6 9.7 %collective-permute-start.13 = (bf16[64,2176]{1,0:T(8,128)(2,1)S(1)}, bf16[64,2176]{1,0:T(8,128)(2,1)S(1)}, u32[]{:S(2)}, u32[]{:S(2)}) collective-permute-start(bf16[64,2176]{1,0:T(8,128)(2,1)S(1)} %collective-permute-done.1.refs_0_), channel_id=1, source_target_pairs={{0,2},{1,3},{2,0},{3,1},{4,6},{5,7},{6,4},{7,5},{8,10},{9,11},{10,... | collective-permute-start | bytes 835592 | tf_op jit(solution)/shard_map/T_b_x2/ppermute | solution.py:253
  50.1 11.5 %collective-permute-start.14 = (bf16[64,2176]{1,0:T(8,128)(2,1)}, bf16[64,2176]{1,0:T(8,128)(2,1)S(1)}, u32[]{:S(2)}, u32[]{:S(2)}) collective-permute-start(bf16[64,2176]{1,0:T(8,128)(2,1)} %collective-permute-done.2.refs_2_), channel_id=1, source_target_pairs={{0,2},{1,3},{2,0},{3,1},{4,6},{5,7},{6,4},{7,5},{8,10},{9,11},{10,... | collective-permute-start | bytes 835592 | tf_op jit(solution)/shard_map/T_b_x3/ppermute | solution.py:253
  58.2 10.1 %copy-start.19 = (bf16[64,2176]{1,0:T(8,128)(2,1)}, bf16[64,2176]{1,0:T(8,128)(2,1)S(1)}, u32[]{:S(2)}) copy-start(bf16[64,2176]{1,0:T(8,128)(2,1)S(1)} %collective-permute-done.13.refs_1_) | copy-start | bytes 835588
  61.7 6.6 %copy-start.20 = (bf16[64,2176]{1,0:T(8,128)(2,1)}, bf16[64,2176]{1,0:T(8,128)(2,1)S(1)}, u32[]{:S(2)}) copy-start(bf16[64,2176]{1,0:T(8,128)(2,1)S(1)} %collective-permute-done.14.refs_3_) | copy-start | bytes 835588
  61.7 18.1 %collective-permute-start.19 = (bf16[128,2048]{1,0:T(8,128)(2,1)}, bf16[128,2048]{1,0:T(8,128)(2,1)S(1)}, u32[]{:S(2)}, u32[]{:S(2)}) collective-permute-start(bf16[128,2048]{1,0:T(8,128)(2,1)} %get-tuple-element.68), channel_id=1, source_target_pairs={{0,2},{1,3},{2,0},{3,1},{4,6},{5,7},{6,4},{7,5},{8,10},{9,11},{10,... | collective-permute-start | bytes 1572872 | tf_op jit(solution)/shard_map/T_b_s0/ppermute | solution.py:253
  63.2 16.5 %collective-permute-start.18 = (bf16[64,2176]{1,0:T(8,128)(2,1)S(1)}, bf16[64,2176]{1,0:T(8,128)(2,1)S(1)}, u32[]{:S(2)}, u32[]{:S(2)}) collective-permute-start(bf16[64,2176]{1,0:T(8,128)(2,1)S(1)} %collective-permute-done.11.refs_2_), channel_id=1, source_target_pairs={{0,2},{1,3},{2,0},{3,1},{4,6},{5,7},{6,4},{7,5},{8,10},{9,11},{10,... | collective-permute-start | bytes 835592 | tf_op jit(solution)/shard_map/T_f_x1/ppermute | solution.py:253
  63.7 16.0 %collective-permute-start.16 = (bf16[64,2176]{1,0:T(8,128)(2,1)S(1)}, bf16[64,2176]{1,0:T(8,128)(2,1)S(1)}, u32[]{:S(2)}, u32[]{:S(2)}) collective-permute-start(bf16[64,2176]{1,0:T(8,128)(2,1)S(1)} %collective-permute-done.11.refs_2_), channel_id=1, source_target_pairs={{0,4},{1,5},{2,6},{3,7},{4,8},{5,9},{6,10},{7,11},{8,12},{9,13},{1... | collective-permute-start | bytes 835592 | tf_op jit(solution)/shard_map/T_f_z2/ppermute | solution.py:257
  64.2 15.5 %collective-permute-start.15 = (bf16[64,2048]{1,0:T(8,128)(2,1)}, bf16[64,2048]{1,0:T(8,128)(2,1)S(1)}, u32[]{:S(2)}, u32[]{:S(2)}) collective-permute-start(bf16[64,2048]{1,0:T(8,128)(2,1)} %bitcast.x), channel_id=1, source_target_pairs={{0,16},{1,17},{2,18},{3,19},{4,20},{5,21},{6,22},{7,23},{8,24},{9,... | collective-permute-start | bytes 786440 | tf_op jit(solution)/shard_map/T_y1/ppermute | solution.py:268
  64.7 15.0 %collective-permute-start.17 = (bf16[64,2176]{1,0:T(8,128)(2,1)S(1)}, bf16[64,2176]{1,0:T(8,128)(2,1)S(1)}, u32[]{:S(2)}, u32[]{:S(2)}) collective-permute-start(bf16[64,2176]{1,0:T(8,128)(2,1)S(1)} %copy-done.9), channel_id=1, source_target_pairs={{0,12},{1,13},{2,14},{3,15},{4,0},{5,1},{6,2},{7,3},{8,4},{9,5},{1... | collective-permute-start | bytes 835592 | tf_op jit(solution)/shard_map/T_f_z3/ppermute | solution.py:257
  79.7 6.9 %copy-start.14 = (bf16[64,2176]{1,0:T(8,128)(2,1)}, bf16[64,2176]{1,0:T(8,128)(2,1)S(1)}, u32[]{:S(2)}) copy-start(bf16[64,2176]{1,0:T(8,128)(2,1)S(1)} %collective-permute-done.18.refs_3_) | copy-start | bytes 835588
  79.7 17.7 %copy-start.11 = (bf16[64,2176]{1,0:T(8,128)(2,1)}, bf16[64,2176]{1,0:T(8,128)(2,1)S(1)}, u32[]{:S(2)}) copy-start(bf16[64,2176]{1,0:T(8,128)(2,1)S(1)} %collective-permute-done.16.refs_0_) | copy-start | bytes 835588
  79.8 17.7 %copy-start.13 = (bf16[64,2176]{1,0:T(8,128)(2,1)}, bf16[64,2176]{1,0:T(8,128)(2,1)S(1)}, u32[]{:S(2)}) copy-start(bf16[64,2176]{1,0:T(8,128)(2,1)S(1)} %collective-permute-done.17.refs_2_) | copy-start | bytes 835588
  79.8 17.7 %collective-permute-start.24 = (bf16[128,2048]{1,0:T(8,128)(2,1)}, bf16[128,2048]{1,0:T(8,128)(2,1)S(1)}, u32[]{:S(2)}, u32[]{:S(2)}) collective-permute-start(bf16[128,2048]{1,0:T(8,128)(2,1)} %get-tuple-element.80), channel_id=1, source_target_pairs={{0,2},{1,3},{2,0},{3,1},{4,6},{5,7},{6,4},{7,5},{8,10},{9,11},{10,... | collective-permute-start | bytes 1572872 | tf_op jit(solution)/shard_map/T_b_s1/ppermute | solution.py:253
  81.3 16.1 %copy-start.7 = (f32[64,2048]{1,0:T(8,128)S(1)}, f32[64,2048]{1,0:T(8,128)}, u32[]{:S(2)}) copy-start(f32[64,2048]{1,0:T(8,128)} %get-tuple-element.82) | copy-start | bytes 1572868
  81.3 16.1 %copy-start.8 = (f32[64,2048]{1,0:T(8,128)S(1)}, f32[64,2048]{1,0:T(8,128)}, u32[]{:S(2)}) copy-start(f32[64,2048]{1,0:T(8,128)} %get-tuple-element.84) | copy-start | bytes 1572868
  81.4 16.2 %collective-permute-start.22 = (bf16[64,2048]{1,0:T(8,128)(2,1)S(1)}, bf16[64,2048]{1,0:T(8,128)(2,1)S(1)}, u32[]{:S(2)}, u32[]{:S(2)}) collective-permute-start(bf16[64,2048]{1,0:T(8,128)(2,1)S(1)} %get-tuple-element.77), channel_id=1, source_target_pairs={{0,16},{1,17},{2,18},{3,19},{4,20},{5,21},{6,22},{7,23},{8,24},{9,... | collective-permute-start | bytes 786440 | tf_op jit(solution)/shard_map/T_b_r0/ppermute | solution.py:268
  82.8 14.8 %collective-permute-start.23 = (bf16[64,2048]{1,0:T(8,128)(2,1)S(1)}, bf16[64,2048]{1,0:T(8,128)(2,1)S(1)}, u32[]{:S(2)}, u32[]{:S(2)}) collective-permute-start(bf16[64,2048]{1,0:T(8,128)(2,1)S(1)} %get-tuple-element.79), channel_id=1, source_target_pairs={{0,28},{1,29},{2,30},{3,31},{4,16},{5,17},{6,18},{7,19},{8,20},{9,... | collective-permute-start | bytes 786440 | tf_op jit(solution)/shard_map/T_b_r1/ppermute | solution.py:268
  84.6 14.9 %collective-permute-start.20 = (bf16[64,2176]{1,0:T(8,128)(2,1)S(1)}, bf16[64,2176]{1,0:T(8,128)(2,1)S(1)}, u32[]{:S(2)}, u32[]{:S(2)}) collective-permute-start(bf16[64,2176]{1,0:T(8,128)(2,1)S(1)} %collective-permute-done.16.refs_0_), channel_id=1, source_target_pairs={{0,2},{1,3},{2,0},{3,1},{4,6},{5,7},{6,4},{7,5},{8,10},{9,11},{10,... | collective-permute-start | bytes 835592 | tf_op jit(solution)/shard_map/T_f_x2/ppermute | solution.py:253
  85.1 17.3 %collective-permute-start.21 = (bf16[64,2176]{1,0:T(8,128)(2,1)S(1)}, bf16[64,2176]{1,0:T(8,128)(2,1)S(1)}, u32[]{:S(2)}, u32[]{:S(2)}) collective-permute-start(bf16[64,2176]{1,0:T(8,128)(2,1)S(1)} %collective-permute-done.17.refs_2_), channel_id=1, source_target_pairs={{0,2},{1,3},{2,0},{3,1},{4,6},{5,7},{6,4},{7,5},{8,10},{9,11},{10,... | collective-permute-start | bytes 835592 | tf_op jit(solution)/shard_map/T_f_x3/ppermute | solution.py:253
  99.4 7.6 %copy-start.15 = (bf16[64,2176]{1,0:T(8,128)(2,1)}, bf16[64,2176]{1,0:T(8,128)(2,1)S(1)}, u32[]{:S(2)}) copy-start(bf16[64,2176]{1,0:T(8,128)(2,1)S(1)} %collective-permute-done.20.refs_1_) | copy-start | bytes 835588
  102.4 4.6 %copy-start.16 = (bf16[64,2176]{1,0:T(8,128)(2,1)}, bf16[64,2176]{1,0:T(8,128)(2,1)S(1)}, u32[]{:S(2)}) copy-start(bf16[64,2176]{1,0:T(8,128)(2,1)S(1)} %collective-permute-done.21.refs_3_) | copy-start | bytes 835588
  102.4 19.0 %copy-start.5 = (f32[64,2048]{1,0:T(8,128)S(1)}, f32[64,2048]{1,0:T(8,128)}, u32[]{:S(2)}) copy-start(f32[64,2048]{1,0:T(8,128)} %get-tuple-element.72) | copy-start | bytes 1572868
  102.4 19.0 %copy-start.6 = (f32[64,2048]{1,0:T(8,128)S(1)}, f32[64,2048]{1,0:T(8,128)}, u32[]{:S(2)}) copy-start(f32[64,2048]{1,0:T(8,128)} %get-tuple-element.90) | copy-start | bytes 1572868
  102.4 16.9 %collective-permute-start.26 = (bf16[64,2048]{1,0:T(8,128)(2,1)S(1)}, bf16[64,2048]{1,0:T(8,128)(2,1)S(1)}, u32[]{:S(2)}, u32[]{:S(2)}) collective-permute-start(bf16[64,2048]{1,0:T(8,128)(2,1)S(1)} %get-tuple-element.83), channel_id=1, source_target_pairs={{0,24},{1,25},{2,26},{3,27},{4,28},{5,29},{6,30},{7,31},{8,16},{9,... | collective-permute-start | bytes 786440 | tf_op jit(solution)/shard_map/T_b_r2/ppermute | solution.py:268
  103.0 16.4 %collective-permute-start.27 = (bf16[64,2048]{1,0:T(8,128)(2,1)S(1)}, bf16[64,2048]{1,0:T(8,128)(2,1)S(1)}, u32[]{:S(2)}, u32[]{:S(2)}) collective-permute-start(bf16[64,2048]{1,0:T(8,128)(2,1)S(1)} %get-tuple-element.85), channel_id=1, source_target_pairs={{0,20},{1,21},{2,22},{3,23},{4,24},{5,25},{6,26},{7,27},{8,28},{9,... | collective-permute-start | bytes 786440 | tf_op jit(solution)/shard_map/T_b_r3/ppermute | solution.py:268
  105.5 14.1 %collective-permute-start.25 = (bf16[128,2048]{1,0:T(8,128)(2,1)}, bf16[128,2048]{1,0:T(8,128)(2,1)S(1)}, u32[]{:S(2)}, u32[]{:S(2)}) collective-permute-start(bf16[128,2048]{1,0:T(8,128)(2,1)} %get-tuple-element.81), channel_id=1, source_target_pairs={{0,2},{1,3},{2,0},{3,1},{4,6},{5,7},{6,4},{7,5},{8,10},{9,11},{10,... | collective-permute-start | bytes 1572872 | tf_op jit(solution)/shard_map/T_f_s0/ppermute | solution.py:253
  117.9 9.1 %copy-start.21 = (bf16[64,2048]{1,0:T(8,128)(2,1)S(1)}, bf16[64,2048]{1,0:T(8,128)(2,1)}, u32[]{:S(2)}) copy-start(bf16[64,2048]{1,0:T(8,128)(2,1)} %get-tuple-element.95) | copy-start | bytes 786436
  117.9 10.8 %copy-start.2 = (f32[64,2048]{1,0:T(8,128)S(1)}, f32[64,2048]{1,0:T(8,128)}, u32[]{:S(2)}) copy-start(f32[64,2048]{1,0:T(8,128)} %get-tuple-element.92) | copy-start | bytes 1572868
  117.9 15.5 %copy-start.1 = (f32[64,2048]{1,0:T(8,128)S(1)}, f32[64,2048]{1,0:T(8,128)}, u32[]{:S(2)}) copy-start(f32[64,2048]{1,0:T(8,128)} %get-tuple-element.94) | copy-start | bytes 1572868
  119.7 7.3 %collective-permute-start.30 = (bf16[64,2048]{1,0:T(8,128)(2,1)}, bf16[64,2048]{1,0:T(8,128)(2,1)S(1)}, u32[]{:S(2)}, u32[]{:S(2)}) collective-permute-start(bf16[64,2048]{1,0:T(8,128)(2,1)} %get-tuple-element.93), channel_id=1, source_target_pairs={{0,2},{1,3},{2,0},{3,1},{4,6},{5,7},{6,4},{7,5},{8,10},{9,11},{10,... | collective-permute-start | bytes 786440 | tf_op jit(solution)/shard_map/T_f_s2/ppermute | solution.py:253
  121.5 13.4 %collective-permute-start.29 = (bf16[64,2048]{1,0:T(8,128)(2,1)S(1)}, bf16[64,2048]{1,0:T(8,128)(2,1)S(1)}, u32[]{:S(2)}, u32[]{:S(2)}) collective-permute-start(bf16[64,2048]{1,0:T(8,128)(2,1)S(1)} %get-tuple-element.91), channel_id=1, source_target_pairs={{0,28},{1,29},{2,30},{3,31},{4,16},{5,17},{6,18},{7,19},{8,20},{9,... | collective-permute-start | bytes 786440 | tf_op jit(solution)/shard_map/T_f_r1/ppermute | solution.py:268
  121.6 13.5 %collective-permute-start.28 = (bf16[64,2048]{1,0:T(8,128)(2,1)S(1)}, bf16[64,2048]{1,0:T(8,128)(2,1)S(1)}, u32[]{:S(2)}, u32[]{:S(2)}) collective-permute-start(bf16[64,2048]{1,0:T(8,128)(2,1)S(1)} %get-tuple-element.89), channel_id=1, source_target_pairs={{0,16},{1,17},{2,18},{3,19},{4,20},{5,21},{6,22},{7,23},{8,24},{9,... | collective-permute-start | bytes 786440 | tf_op jit(solution)/shard_map/T_f_r0/ppermute | solution.py:268
  127.0 6.4 %collective-permute-start.32 = (bf16[64,2048]{1,0:T(8,128)(2,1)S(1)}, bf16[64,2048]{1,0:T(8,128)(2,1)S(1)}, u32[]{:S(2)}, u32[]{:S(2)}) collective-permute-start(bf16[64,2048]{1,0:T(8,128)(2,1)S(1)} %copy-done.21), channel_id=1, source_target_pairs={{0,2},{1,3},{2,0},{3,1},{4,6},{5,7},{6,4},{7,5},{8,10},{9,11},{10,... | collective-permute-start | bytes 786440 | tf_op jit(solution)/shard_map/T_f_s3/ppermute | solution.py:253
  128.8 17.0 %collective-permute-start.31 = (bf16[64,2048]{1,0:T(8,128)(2,1)S(1)}, bf16[64,2048]{1,0:T(8,128)(2,1)S(1)}, u32[]{:S(2)}, u32[]{:S(2)}) collective-permute-start(bf16[64,2048]{1,0:T(8,128)(2,1)S(1)} %add_convert_fusion.2), channel_id=1, source_target_pairs={{0,24},{1,25},{2,26},{3,27},{4,28},{5,29},{6,30},{7,31},{8,16},{9,... | collective-permute-start | bytes 786440 | tf_op jit(solution)/shard_map/T_f_r2/ppermute | solution.py:268
  133.4 12.3 %collective-permute-start.33 = (bf16[64,2048]{1,0:T(8,128)(2,1)S(1)}, bf16[64,2048]{1,0:T(8,128)(2,1)S(1)}, u32[]{:S(2)}, u32[]{:S(2)}) collective-permute-start(bf16[64,2048]{1,0:T(8,128)(2,1)S(1)} %add_convert_fusion.1), channel_id=1, source_target_pairs={{0,20},{1,21},{2,22},{3,23},{4,24},{5,25},{6,26},{7,27},{8,28},{9,... | collective-permute-start | bytes 786440 | tf_op jit(solution)/shard_map/T_f_r3/ppermute | solution.py:268

commit v3 on v2

--- a/solution.py
+++ b/solution.py
@@ -23,12 +23,10 @@
     return lax.rsqrt(jnp.mean(widened * widened, axis=-1, keepdims=True) + epsilon)
 
 
-def pack_kernel(experts, dy, x, gain, ids_b, gates_b, ids_f, gates_f, x_b, out_b, out_f, pair):
+def pack_kernel(experts, dy, x, gain, ids_b, gates_b, ids_f, gates_f, out_b, out_f):
     tokens, width = dy.shape
     wide = x[...].astype(f32)
     scale = lax.rsqrt(jnp.mean(wide * wide, axis=-1, keepdims=True) + epsilon)
-    pair[:tokens, :] = x_b[...]
-    pair[tokens:, :] = dy[...]
     values = (dy[...], (wide * scale * gain[...]).astype(bf16))
     spread = (experts, out_b.shape[1] - width)
     row = lax.broadcasted_iota(jnp.int32, spread, 0)
@@ -49,19 +47,19 @@
         out[:, width:] = columns.astype(bf16)
 
 
-def pack(experts, dy, x, gain, ids_b, gates_b, ids_f, gates_f, x_b):
+def pack(experts, dy, x, gain, ids_b, gates_b, ids_f, gates_f):
     tokens, width = dy.shape
     columns = -(-2 * experts // LANES) * LANES
     vmem = pl.BlockSpec(memory_space=pltpu.VMEM)
     one = jax.ShapeDtypeStruct((tokens, width + columns), bf16)
     return pl.pallas_call(
         functools.partial(pack_kernel, experts),
-        out_shape=[one, one, jax.ShapeDtypeStruct((2 * tokens, width), bf16)],
-        in_specs=[vmem] * 8,
-        out_specs=[vmem] * 3,
+        out_shape=[one, one],
+        in_specs=[vmem] * 7,
+        out_specs=[vmem] * 2,
         compiler_params=pltpu.CompilerParams(vmem_limit_bytes=PACK_VMEM_LIMIT),
         name="pack",
-    )(dy, x, gain, ids_b.T, gates_b.T, ids_f.T, gates_f.T, x_b)
+    )(dy, x, gain, ids_b.T, gates_b.T, ids_f.T, gates_f.T)
 
 
 def experts_kernel(backward, experts, tokens, capacity, chunk, apart, starts, table, *refs):
@@ -294,28 +292,24 @@
     table = jnp.stack([scalars_of(chunk) for chunk in chunks])
     packed = pack(
         experts, dy_backward[0], input_rows, gain,
-        ids_backward[0], gates_backward[0], ids_forward[0], gates_forward[0], x_backward[0],
+        ids_backward[0], gates_backward[0], ids_forward[0], gates_forward[0],
     )
     held = {True: {0: packed[0]}, False: {0: packed[1]}}
     across = {True: {}, False: {}}
     names = {True: "b", False: "f"}
 
-    def go_along(backward, i, *earlier):
-        before, moved = held[backward], []
-        ready = {k: after(v, *earlier) for k, v in before.items()}
-        for k in chunks[i]:
-            if k:
-                before[k] = farther(ready, k, names[backward])
-                moved.append(before[k])
-        return moved
-
-    def go_across(backward, ks, *earlier):
-        moved = []
-        for k in ks:
-            value = swap(after(held[backward][k], *earlier), 2, f"T_{names[backward]}_x{k}")
-            across[backward][k] = value
-            moved.append(value)
-        return moved
+    def along(backward, k, *earlier):
+        ready = {j: after(v, *earlier) for j, v in held[backward].items()}
+        held[backward][k] = farther(ready, k, names[backward])
+        return [held[backward][k]]
+
+    def aside(backward, k, *earlier):
+        known, name = across[backward], names[backward]
+        if 2 * k <= line:
+            known[k] = swap(after(held[backward][k], *earlier), 2, f"T_{name}_x{k}")
+        else:
+            known[k] = shift(after(known[(k + 1) % line], *earlier), -1, f"T_{name}_w{k}")
+        return [known[k]]
 
     def experts_on(backward, i, *earlier):
         chunk, apart = chunks[i], not backward and i == last
@@ -326,96 +320,107 @@
         )
         return dict(zip(chunk, out)), out[len(chunk) :]
 
-    def chip_sums(chunk, own, sent, label, *earlier):
+    def chip_sum(backward, k, own, piece):
+        total = own + piece.astype(f32)
+        return total if backward and k == 0 else total.astype(bf16)
+
+    def chip_sums(backward, chunk, own, sent, label, *earlier):
         came = swap(after(sent[0], *earlier), 2, label)
-        return {
-            k: (own[k] + came[i * tokens : (i + 1) * tokens].astype(f32)).astype(bf16)
-            for i, k in enumerate(chunk)
-        }, came
+        pieces = {k: came[i * tokens : (i + 1) * tokens] for i, k in enumerate(chunk)}
+        return {k: chip_sum(backward, k, own[k], piece) for k, piece in pieces.items()}, came
 
     def send_sums(backward, sums, *earlier):
         moved = []
         for k, value in sums.items():
-            label = f"T_{names[backward]}_r{k}"
-            moved.append(relay(after(value, *earlier), -1 if backward else 1, label, -k))
+            label, value = f"T_{names[backward]}_r{k}", after(value, *earlier)
+            if not backward:
+                moved.append(relay(value, 1, label, -k))
+            elif k:
+                moved.append(shift(value, -k, label))
+            else:
+                came[True].append(value)
+        came[backward].extend(moved)
         return moved
 
-    wave = go_along(True, 0) + go_across(True, [0]) + go_across(False, [0])
+    near, far = chunks[0][1], chunks[-1][-1]
+    wave = along(True, near) + aside(True, 0)
     theirs_gate = swap(after(w_gate, packed[0]), 1, "T_wg")
     theirs_up = swap(after(w_up, packed[0]), 1, "T_wu")
-    wave += [theirs_gate, theirs_up]
+    theirs_kept_gate = swap(after(saved_gate, packed[0]), 1, "T_sg")
+    wave += [theirs_gate, theirs_up, theirs_kept_gate]
     table = after(table, *wave)
     theirs_down = swap(after(w_down, *wave), 1, "T_wd")
-    theirs_kept_gate = swap(after(saved_gate, *wave), 1, "T_sg")
     theirs_kept_up = swap(after(saved_up, *wave), 1, "T_su")
-    near = go_across(True, chunks[0][1:], *wave)
-    wave = near + [theirs_down, theirs_kept_gate, theirs_kept_up]
-    flying = go_along(True, 1)
+    moved = aside(True, near, *wave)
+    for k in chunks[1]:
+        moved += along(True, k, *wave)
+    wave = moved + [theirs_down, theirs_kept_up, table]
+    kept_theirs = (theirs_kept_gate, theirs_kept_up)
     mine, theirs = (w_gate, w_up, w_down), (theirs_gate, theirs_up, theirs_down)
-    kept_mine, kept_theirs = (saved_gate, saved_up), (theirs_kept_gate, theirs_kept_up)
-
-    steps = [(True, i) for i in range(last + 1)] + [(False, i) for i in range(last + 1)]
-    half = last + 1
-    runs, sums, ends = {}, {}, {}
-    came = {True: [], False: []}
-    for p, (backward, i) in enumerate(steps):
-        if backward and i:
-            wave += go_across(True, chunks[i], *wave)
-        moved, flying = flying, []
-        if p == 0:
-            moved += go_along(False, 0, *wave)
-            pair = relay(after(packed[2], *wave), -1, "T_y2")
-            moved.append(pair)
-        if backward and 0 < i < last:
-            moved += go_along(True, i + 1, *wave)
-        ahead, side = p - half + 2, p - half + 1
-        if 1 <= ahead <= last:
-            moved += go_along(False, ahead, *wave)
-        if 0 <= side <= last:
-            moved += go_across(False, [k for k in chunks[side] if k], *wave)
+    kept_mine = (saved_gate, saved_up)
+
+    runs, came = {}, {True: [], False: []}
+    sums = []
+    half = len(chunks)
+    for p in range(2 * half):
+        backward, i = p < half, p % half
+        moved = []
+        if backward and i < last:
+            for k in chunks[i + 1]:
+                moved += aside(True, k, *wave)
+            if i + 1 < last:
+                for k in chunks[i + 2]:
+                    moved += along(True, k, *wave)
+        if p == half - 2:
+            moved += aside(False, 0, *wave) + along(False, near, *wave)
+            residual = relay(after(input_rows, *wave), 1, "T_y1")
+            moved.append(residual)
         if p == half - 1:
-            ends["residual"] = relay(after(input_rows, *wave), 1, "T_y1")
-            moved.append(ends["residual"])
-        if p >= 2:
-            way, j = steps[p - 2]
-            moved += send_sums(way, sums[p - 2], *wave)
-            came[way] += moved[-len(chunks[j]) :]
+            moved += aside(False, near, *wave)
+        if 0 <= p - half + 1 < last:
+            for k in chunks[p - half + 2]:
+                moved += along(False, k, *wave)
+        if 0 <= p - half < last:
+            for k in chunks[p - half + 1]:
+                moved += aside(False, k, *wave)
+        for way, chunk_sums in sums:
+            moved += send_sums(way, chunk_sums, *wave)
+        sums = []
         if p:
-            way, j = steps[p - 1]
-            sums[p - 1], arrived = chip_sums(
-                chunks[j], *runs[p - 1], f"T_{names[way]}_s{j}", *wave
+            way, j = p <= half, (p - 1) % half
+            own, sent = runs[p - 1]
+            chunk_sums, arrived = chip_sums(
+                way, chunks[j], own, sent, f"T_{names[way]}_s{j}", *wave
             )
+            sums = [(way, chunk_sums)]
             moved.append(arrived)
         runs[p] = experts_on(backward, i, *wave)
         wave = moved + list(runs[p][1])
-    p = len(steps)
-    came[False] += send_sums(False, sums[p - 2], *wave)
-    own, sent = runs[p - 1]
-    for k, value in zip(chunks[last], sent):
-        arrived = swap(after(value, *wave), 2, f"T_f_s{k}")
-        chip = (own[k] + arrived.astype(f32)).astype(bf16)
-        came[False] += send_sums(False, {k: chip})
-        wave = [arrived]
-
     def summed(values):
         total = values[0].astype(f32)
         for value in values[1:]:
             total = total + value.astype(f32)
         return total
 
-    residual = ends["residual"].astype(f32)
-    saved_input, gradient = pair[:tokens].astype(f32), pair[tokens:].astype(f32)
     weighted = summed(came[True])
-    scale_rows = inverse_rms(saved_input)
+    saved_input = x_backward[0].astype(f32)
+    scale_rows = inverse_rms(x_backward[0])
     inner = jnp.mean(weighted * saved_input, axis=-1, keepdims=True)
-    next_backward = (
-        gradient
+    d_input = (
+        dy_backward[0].astype(f32)
         + scale_rows * weighted
         - saved_input * scale_rows * scale_rows * scale_rows * inner
     ).astype(bf16)
-
-    combined = summed(came[False])
-    next_forward = (residual + combined).astype(bf16)
+    next_backward = relay(d_input, -1, "T_b_y")
+
+    send_sums(*sums[0], *wave)
+    own, sent = runs[2 * half - 1]
+    ahead = d_input
+    for k, value in zip(chunks[last], sent):
+        arrived = swap(after(value, *wave), 2, f"T_f_s{k}")
+        send_sums(False, {k: after(chip_sum(False, k, own[k], arrived), ahead)})
+        ahead, wave = came[False][-1], [arrived]
+    next_forward = (summed(came[False]) + residual.astype(f32)).astype(bf16)
     return (next_forward[None], next_backward[None])
 
 

time: 147 us -> 140 us (0.952)
  starting transfers between devices: 42 us -> 34.3 us
    ppermute x18 -> x16, waiting for transfers between devices: 38.9 us -> 21 us  [swap(): return lax.ppermute(value, 'expert', [(i, i ^ bit) for i in range(experts)])]
    ppermute x6 -> x11, waiting for transfers between devices: 1.4 us -> 17.8 us  [shift(): lax.ppermute(value, 'expert', [(i, (i + 4 * steps) % experts) for i in ra...]
    ppermute x10 -> x6, starting transfers between devices: 10.7 us -> 6.31 us  [relay(): return lax.ppermute(value, ('section', 'expert'), pairs)]
    ppermute x18 -> x16, starting transfers between devices: 18.4 us -> 14.1 us  [swap(): return lax.ppermute(value, 'expert', [(i, i ^ bit) for i in range(experts)])]
    ppermute x10 -> x6, waiting for transfers between devices: 12.3 us -> 14.8 us  [relay(): return lax.ppermute(value, ('section', 'expert'), pairs)]
    ppermute x6 -> x11, starting transfers between devices: 12.9 us -> 13.8 us  [shift(): lax.ppermute(value, 'expert', [(i, (i + 4 * steps) % experts) for i in ra...]
  transfers between devices with their start and end apart: 34 -> 33, of which waited for: 13 -> 12; matrix products, arithmetic and copies ran while one was open for 2% -> 1% of each run, Pallas kernels for 30% -> 32%
where the time goes in v3:
time: 140 us
  waiting for transfers between devices  53.6 us (38%)
  Pallas kernels  46.5 us (33%)
  starting transfers between devices  34.3 us (24%)
  other arithmetic  2.47 us (2%)
  local copies, waits for them, and re-layouts  1.98 us (1%)
    pallas_call x4, Pallas kernels, run_experts(): pl.pallas_call(functools.partial(experts_kernel, backward, experts, token...  44.4 us
    ppermute x16, waiting for transfers between devices, swap(): return lax.ppermute(value, 'expert', [(i, i ^ bit) for i in range(experts)])  21 us
    ppermute x11, waiting for transfers between devices, shift(): lax.ppermute(value, 'expert', [(i, (i + 4 * steps) % experts) for i in ra...  17.8 us
    ppermute x6, waiting for transfers between devices, relay(): return lax.ppermute(value, ('section', 'expert'), pairs)  14.8 us
    ppermute x16, starting transfers between devices, swap(): return lax.ppermute(value, 'expert', [(i, i ^ bit) for i in range(experts)])  14.1 us
    ppermute x11, starting transfers between devices, shift(): lax.ppermute(value, 'expert', [(i, (i + 4 * steps) % experts) for i in ra...  13.8 us
    ppermute x6, starting transfers between devices, relay(): return lax.ppermute(value, ('section', 'expert'), pairs)  6.31 us
  transfers between devices with their start and end apart: 33, of which 12 were waited for; matrix products, arithmetic and copies ran while one was open for 1% of the time, Pallas kernels for 32%

profile of v3, /device:TPU:0, one launch (start us, length us, event | category | flops | bytes accessed | tf_op | source)
XLA Modules:
  0.0 139.8 jit_solution(11067457653278002861)
XLA Ops:
  0.6 2.1 %pack.1 = (bf16[64,2176]{1,0:T(8,128)(2,1)}, bf16[64,2176]{1,0:T(8,128)(2,1)}) custom-call(bf16[64,2048]{1,0:T(8,128)(2,1)} %bitcast.35, bf16[64,2048]{1,0:T(8,128)(2,1)} %bitcast.36, f32[1,2048]{1,0:T(1,128)} %refs_14_.3, s32[8,64]{1,0:T(8,128)} %bitcast.39, f32[8,64]{1,0:T(8,128)} %bitcast.40, s32[8,64]{1,0:T(8,128)} %bitcast.41, f32[8,64]{1,0:T(8,128)} %bitcast.42), custom_call_target="tpu_custom_call" | custom-call | tf_op jit(solution)/shard_map/pack/pallas_call | solution.py:55
  2.7 0.5 collective-permute-start.2
  3.2 0.1 collective-permute-start.3
  3.2 0.5 collective-permute-start.4
  3.7 2.5 %collective-permute-start.1 = (bf16[64,2176]{1,0:T(8,128)(2,1)}, bf16[64,2176]{1,0:T(8,128)(2,1)S(1)}, u32[]{:S(2)}, u32[]{:S(2)}) collective-permute-start(bf16[64,2176]{1,0:T(8,128)(2,1)} %get-tuple-element.57.refs_0_), channel_id=1, source_target_pairs={{0,2},{1,3},{2,0},{3,1},{4,6},{5,7},{6,4},{7,5},{8,10},{9,11},{10,... | collective-permute-start | bytes 835592 | tf_op jit(solution)/shard_map/T_b_x0/ppermute | solution.py:251
  6.2 1.6 %collective-permute-start = (bf16[64,2176]{1,0:T(8,128)(2,1)}, bf16[64,2176]{1,0:T(8,128)(2,1)}, u32[]{:S(2)}, u32[]{:S(2)}) collective-permute-start(bf16[64,2176]{1,0:T(8,128)(2,1)} %get-tuple-element.57.refs_0_), channel_id=1, source_target_pairs={{0,4},{1,5},{2,6},{3,7},{4,8},{5,9},{6,10},{7,11},{8,12},{9,13},{1... | collective-permute-start | bytes 835592 | tf_op jit(solution)/shard_map/T_b_z1/ppermute | solution.py:255
  7.7 6.0 %collective-permute-done.1.refs_1_ = bf16[64,2176]{1,0:T(8,128)(2,1)S(1)} collective-permute-done((bf16[64,2176]{1,0:T(8,128)(2,1)}, bf16[64,2176]{1,0:T(8,128)(2,1)S(1)}, u32[]{:S(2)}, u32[]{:S(2)}) %collective-permute-start.1) | collective-permute-done | bytes 278560 | tf_op jit(solution)/shard_map/T_b_x0/ppermute | solution.py:251
  13.7 3.5 %collective-permute-done.refs_2_ = bf16[64,2176]{1,0:T(8,128)(2,1)} collective-permute-done((bf16[64,2176]{1,0:T(8,128)(2,1)}, bf16[64,2176]{1,0:T(8,128)(2,1)}, u32[]{:S(2)}, u32[]{:S(2)}) %collective-permute-start) | collective-permute-done | bytes 278560 | tf_op jit(solution)/shard_map/T_b_z1/ppermute | solution.py:255
  17.2 0.0 collective-permute-done.2.refs_7_
  17.2 1.0 copy-done.1
  18.2 0.5 collective-permute-start.9
  18.7 0.6 collective-permute-start.6
  19.3 1.5 %collective-permute-start.5 = (bf16[64,2176]{1,0:T(8,128)(2,1)}, bf16[64,2176]{1,0:T(8,128)(2,1)}, u32[]{:S(2)}, u32[]{:S(2)}) collective-permute-start(bf16[64,2176]{1,0:T(8,128)(2,1)} %collective-permute-done.refs_2_), channel_id=1, source_target_pairs={{0,2},{1,3},{2,0},{3,1},{4,6},{5,7},{6,4},{7,5},{8,10},{9,11},{10,... | collective-permute-start | bytes 835592 | tf_op jit(solution)/shard_map/T_b_x1/ppermute | solution.py:251
  20.8 2.2 %collective-permute-start.7 = (bf16[64,2176]{1,0:T(8,128)(2,1)}, bf16[64,2176]{1,0:T(8,128)(2,1)}, u32[]{:S(2)}, u32[]{:S(2)}) collective-permute-start(bf16[64,2176]{1,0:T(8,128)(2,1)} %get-tuple-element.57.refs_0_), channel_id=1, source_target_pairs={{0,12},{1,13},{2,14},{3,15},{4,0},{5,1},{6,2},{7,3},{8,4},{9,5},{1... | collective-permute-start | bytes 835592 | tf_op jit(solution)/shard_map/T_b_z3/ppermute | solution.py:255
  23.1 0.1 stack.59
  23.1 0.1 stack.53
  23.2 0.6 pad_add_fusion.table
  23.8 6.6 %collective-permute-done.6.refs_0_ = bf16[64,2176]{1,0:T(8,128)(2,1)} collective-permute-done((bf16[64,2176]{1,0:T(8,128)(2,1)}, bf16[64,2176]{1,0:T(8,128)(2,1)}, u32[]{:S(2)}, u32[]{:S(2)}) %collective-permute-start.6) | collective-permute-done | bytes 278560 | tf_op jit(solution)/shard_map/T_b_z2/ppermute | solution.py:255
  30.4 4.9 %collective-permute-done.7.refs_2_ = bf16[64,2176]{1,0:T(8,128)(2,1)} collective-permute-done((bf16[64,2176]{1,0:T(8,128)(2,1)}, bf16[64,2176]{1,0:T(8,128)(2,1)}, u32[]{:S(2)}, u32[]{:S(2)}) %collective-permute-start.7) | collective-permute-done | bytes 278560 | tf_op jit(solution)/shard_map/T_b_z3/ppermute | solution.py:255
  35.3 0.6 collective-permute-start.13
  35.9 0.9 collective-permute-start.10
  36.7 1.5 %collective-permute-start.14 = (bf16[64,2048]{1,0:T(8,128)(2,1)}, bf16[64,2048]{1,0:T(8,128)(2,1)S(1)}, u32[]{:S(2)}, u32[]{:S(2)}) collective-permute-start(bf16[64,2048]{1,0:T(8,128)(2,1)} %bitcast.37), channel_id=1, source_target_pairs={{0,16},{1,17},{2,18},{3,19},{4,20},{5,21},{6,22},{7,23},{8,24},{9,... | collective-permute-start | bytes 786440 | tf_op jit(solution)/shard_map/T_y1/ppermute | solution.py:266
  38.2 1.4 collective-permute-start.11
  39.6 3.1 %collective-permute-start.12 = (bf16[64,2176]{1,0:T(8,128)(2,1)S(1)}, bf16[64,2176]{1,0:T(8,128)(2,1)S(1)}, u32[]{:S(2)}, u32[]{:S(2)}) collective-permute-start(bf16[64,2176]{1,0:T(8,128)(2,1)S(1)} %collective-permute-done.1.refs_1_), channel_id=1, source_target_pairs={{0,12},{1,13},{2,14},{3,15},{4,0},{5,1},{6,2},{7,3},{8,4},{9,5},{1... | collective-permute-start | bytes 835592 | tf_op jit(solution)/shard_map/T_b_w3/ppermute | solution.py:255
  42.7 11.4 %experts_backward.2 = (f32[64,2048]{1,0:T(8,128)}, f32[64,2048]{1,0:T(8,128)}, bf16[128,2048]{1,0:T(8,128)(2,1)}) custom-call(s32[2,6]{1,0:T(2,128)} %pad_add_fusion.table, bf16[64,2176]{1,0:T(8,128)(2,1)} %get-tuple-element.57.refs_0_, bf16[64,2176]{1,0:T(8,128)(2,1)} %copy-done.20, bf16[64,2176]{1,0:T(8,128)(2,1)} %collective-permute-done.refs_2_, ...), custom_call_target="tpu_custom_call" | custom-call | flops 4831838208 | bytes 18874368 | tf_op jit(solution)/shard_map/experts_backward/pallas_call | solution.py:210
  54.2 0.6 collective-permute-start.18
  54.8 1.5 %collective-permute-start.15 = (bf16[64,2176]{1,0:T(8,128)(2,1)S(1)}, bf16[64,2176]{1,0:T(8,128)(2,1)S(1)}, u32[]{:S(2)}, u32[]{:S(2)}) collective-permute-start(bf16[64,2176]{1,0:T(8,128)(2,1)S(1)} %collective-permute-done.10.refs_2_), channel_id=1, source_target_pairs={{0,2},{1,3},{2,0},{3,1},{4,6},{5,7},{6,4},{7,5},{8,10},{9,11},{10,... | collective-permute-start | bytes 835592 | tf_op jit(solution)/shard_map/T_f_x1/ppermute | solution.py:251
  56.3 3.8 %collective-permute-start.17 = (bf16[64,2176]{1,0:T(8,128)(2,1)S(1)}, bf16[64,2176]{1,0:T(8,128)(2,1)S(1)}, u32[]{:S(2)}, u32[]{:S(2)}) collective-permute-start(bf16[64,2176]{1,0:T(8,128)(2,1)S(1)} %copy-done.12), channel_id=1, source_target_pairs={{0,12},{1,13},{2,14},{3,15},{4,0},{5,1},{6,2},{7,3},{8,4},{9,5},{1... | collective-permute-start | bytes 835592 | tf_op jit(solution)/shard_map/T_f_z3/ppermute | solution.py:255
  60.1 11.4 %experts_backward.3 = (f32[64,2048]{1,0:T(8,128)}, f32[64,2048]{1,0:T(8,128)}, bf16[128,2048]{1,0:T(8,128)(2,1)}) custom-call(s32[2,6]{1,0:T(2,128)} %pad_add_fusion.table, bf16[64,2176]{1,0:T(8,128)(2,1)} %collective-permute-done.6.refs_0_, bf16[64,2176]{1,0:T(8,128)(2,1)} %copy-done.21, bf16[64,2176]{1,0:T(8,128)(2,1)} %collective-permute-done.7.refs_2_, ...), custom_call_target="tpu_custom_call" | custom-call | flops 4831838208 | bytes 18874368 | tf_op jit(solution)/shard_map/experts_backward/pallas_call | solution.py:210
  71.5 1.1 collective-permute-done.15.refs_3_
  72.7 1.0 collective-permute-start.22
  73.6 0.1 convert_add_fusion.1
  73.8 0.1 collective-permute-start.21
  73.8 1.4 %collective-permute-start.19 = (bf16[64,2176]{1,0:T(8,128)(2,1)S(1)}, bf16[64,2176]{1,0:T(8,128)(2,1)S(1)}, u32[]{:S(2)}, u32[]{:S(2)}) collective-permute-start(bf16[64,2176]{1,0:T(8,128)(2,1)S(1)} %collective-permute-done.16.refs_0_), channel_id=1, source_target_pairs={{0,2},{1,3},{2,0},{3,1},{4,6},{5,7},{6,4},{7,5},{8,10},{9,11},{10,... | collective-permute-start | bytes 835592 | tf_op jit(solution)/shard_map/T_f_x2/ppermute | solution.py:251
  75.3 0.1 collective-permute-start.20
  75.3 10.8 %experts_forward.2 = (f32[64,2048]{1,0:T(8,128)}, f32[64,2048]{1,0:T(8,128)}, bf16[128,2048]{1,0:T(8,128)(2,1)}) custom-call(s32[2,6]{1,0:T(2,128)} %pad_add_fusion.table, bf16[64,2176]{1,0:T(8,128)(2,1)} %get-tuple-element.67.refs_0_, bf16[64,2176]{1,0:T(8,128)(2,1)} %copy-done.13, bf16[64,2176]{1,0:T(8,128)(2,1)} %copy-done.15, ...), custom_call_target="tpu_custom_call" | custom-call | flops 4831838208 | bytes 18874368 | tf_op jit(solution)/shard_map/experts_forward/pallas_call | solution.py:210
  86.2 4.0 %collective-permute-done.19.refs_1_ = bf16[64,2176]{1,0:T(8,128)(2,1)S(1)} collective-permute-done((bf16[64,2176]{1,0:T(8,128)(2,1)S(1)}, bf16[64,2176]{1,0:T(8,128)(2,1)S(1)}, u32[]{:S(2)}, u32[]{:S(2)}) %collective-permute-start.19) | collective-permute-done | bytes 278560 | tf_op jit(solution)/shard_map/T_f_x2/ppermute | solution.py:251
  90.3 0.1 add_convert_fusion.4
  90.4 0.0 copy-start.3
  90.4 0.0 copy-start.2
  90.4 0.1 collective-permute-start.24
  90.5 1.4 %collective-permute-start.25 = (bf16[64,2048]{1,0:T(8,128)(2,1)S(1)}, bf16[64,2048]{1,0:T(8,128)(2,1)S(1)}, u32[]{:S(2)}, u32[]{:S(2)}) collective-permute-start(bf16[64,2048]{1,0:T(8,128)(2,1)S(1)} %get-tuple-element.83), channel_id=1, source_target_pairs={{0,4},{1,5},{2,6},{3,7},{4,8},{5,9},{6,10},{7,11},{8,12},{9,13},{1... | collective-permute-start | bytes 786440 | tf_op jit(solution)/shard_map/T_b_r3/ppermute | solution.py:255
  91.9 1.7 %collective-permute-start.23 = (bf16[128,2048]{1,0:T(8,128)(2,1)}, bf16[128,2048]{1,0:T(8,128)(2,1)S(1)}, u32[]{:S(2)}, u32[]{:S(2)}) collective-permute-start(bf16[128,2048]{1,0:T(8,128)(2,1)} %get-tuple-element.79), channel_id=1, source_target_pairs={{0,2},{1,3},{2,0},{3,1},{4,6},{5,7},{6,4},{7,5},{8,10},{9,11},{10,... | collective-permute-start | bytes 1572872 | tf_op jit(solution)/shard_map/T_f_s0/ppermute | solution.py:251
  93.7 10.8 %experts_forward.3 = (f32[64,2048]{1,0:T(8,128)}, f32[64,2048]{1,0:T(8,128)}, bf16[64,2048]{1,0:T(8,128)(2,1)}, bf16[64,2048]{1,0:T(8,128)(2,1)}) custom-call(s32[2,6]{1,0:T(2,128)} %pad_add_fusion.table, bf16[64,2176]{1,0:T(8,128)(2,1)} %copy-done.14, bf16[64,2176]{1,0:T(8,128)(2,1)} %copy-done.18, bf16[64,2176]{1,0:T(8,128)(2,1)} %copy-done.16, ...), custom_call_target="tpu_custom_call" | custom-call | flops 4831838208 | bytes 18874368 | tf_op jit(solution)/shard_map/experts_forward/pallas_call | solution.py:210
  104.5 0.0 copy-start.24
  104.5 0.0 copy-start.23
  104.6 2.9 %collective-permute-done.24 = bf16[64,2048]{1,0:T(8,128)(2,1)S(1)} collective-permute-done((bf16[64,2048]{1,0:T(8,128)(2,1)S(1)}, bf16[64,2048]{1,0:T(8,128)(2,1)S(1)}, u32[]{:S(2)}, u32[]{:S(2)}) %collective-permute-start.24) | collective-permute-done | bytes 262176 | tf_op jit(solution)/shard_map/T_b_r2/ppermute | solution.py:255
  107.4 0.3 fusion
  107.7 0.3 fusion.5
  108.0 1.3 collective-permute-start.32
  109.3 0.5 collective-permute-start.28
  109.8 0.1 add_convert_fusion.6
  109.9 0.1 collective-permute-start.27
  110.0 2.0 %collective-permute-start.26 = (bf16[64,2048]{1,0:T(8,128)(2,1)S(1)}, bf16[64,2048]{1,0:T(8,128)(2,1)S(1)}, u32[]{:S(2)}, u32[]{:S(2)}) collective-permute-start(bf16[64,2048]{1,0:T(8,128)(2,1)S(1)} %get-tuple-element.87), channel_id=1, source_target_pairs={{0,16},{1,17},{2,18},{3,19},{4,20},{5,21},{6,22},{7,23},{8,24},{9,... | collective-permute-start | bytes 786440 | tf_op jit(solution)/shard_map/T_f_r0/ppermute | solution.py:266
  112.0 5.0 %collective-permute-done.28 = bf16[64,2048]{1,0:T(8,128)(2,1)S(1)} collective-permute-done((bf16[64,2048]{1,0:T(8,128)(2,1)S(1)}, bf16[64,2048]{1,0:T(8,128)(2,1)S(1)}, u32[]{:S(2)}, u32[]{:S(2)}) %collective-permute-start.28) | collective-permute-done | bytes 262176 | tf_op jit(solution)/shard_map/T_f_s2/ppermute | solution.py:251
  117.0 0.0 collective-permute-start.30
  117.1 1.5 %collective-permute-start.29 = (bf16[64,2048]{1,0:T(8,128)(2,1)S(1)}, bf16[64,2048]{1,0:T(8,128)(2,1)S(1)}, u32[]{:S(2)}, u32[]{:S(2)}) collective-permute-start(bf16[64,2048]{1,0:T(8,128)(2,1)S(1)} %add_convert_fusion.2), channel_id=1, source_target_pairs={{0,24},{1,25},{2,26},{3,27},{4,28},{5,29},{6,30},{7,31},{8,16},{9,... | collective-permute-start | bytes 786440 | tf_op jit(solution)/shard_map/T_f_r2/ppermute | solution.py:266
  118.5 4.8 %collective-permute-done.30 = bf16[64,2048]{1,0:T(8,128)(2,1)S(1)} collective-permute-done((bf16[64,2048]{1,0:T(8,128)(2,1)S(1)}, bf16[64,2048]{1,0:T(8,128)(2,1)S(1)}, u32[]{:S(2)}, u32[]{:S(2)}) %collective-permute-start.30) | collective-permute-done | bytes 262176 | tf_op jit(solution)/shard_map/T_f_s3/ppermute | solution.py:251
  123.4 0.1 add_convert_fusion.1
  123.5 4.8 %collective-permute-done.29 = bf16[64,2048]{1,0:T(8,128)(2,1)S(1)} collective-permute-done((bf16[64,2048]{1,0:T(8,128)(2,1)S(1)}, bf16[64,2048]{1,0:T(8,128)(2,1)S(1)}, u32[]{:S(2)}, u32[]{:S(2)}) %collective-permute-start.29) | collective-permute-done | bytes 262176 | tf_op jit(solution)/shard_map/T_f_r2/ppermute | solution.py:266
  128.2 2.9 %collective-permute-done.26 = bf16[64,2048]{1,0:T(8,128)(2,1)S(1)} collective-permute-done((bf16[64,2048]{1,0:T(8,128)(2,1)S(1)}, bf16[64,2048]{1,0:T(8,128)(2,1)S(1)}, u32[]{:S(2)}, u32[]{:S(2)}) %collective-permute-start.26) | collective-permute-done | bytes 262176 | tf_op jit(solution)/shard_map/T_f_r0/ppermute | solution.py:266
  131.1 7.1 %collective-permute-done.31 = bf16[64,2048]{1,0:T(8,128)(2,1)S(1)} collective-permute-done((bf16[64,2048]{1,0:T(8,128)(2,1)S(1)}, bf16[64,2048]{1,0:T(8,128)(2,1)S(1)}, u32[]{:S(2)}, u32[]{:S(2)}) %collective-permute-start.31) | collective-permute-done | bytes 262176 | tf_op jit(solution)/shard_map/T_f_r3/ppermute | solution.py:266
  138.2 0.9 fusion.7
  139.1 0.7 copy.16
  (70 shorter events, 0.2 us)
Async XLA Ops:
  2.7 14.5 %collective-permute-start.2 = (bf16[1,1,2048,768]{3,2,1,0:T(8,128)(2,1)}, bf16[1,1,2048,768]{3,2,1,0:T(8,128)(2,1)S(1)}, u32[]{:S(2)}, u32[]{:S(2)}) collective-permute-start(bf16[1,1,2048,768]{3,2,1,0:T(8,128)(2,1)} %refs_4_.7), channel_id=1, source_target_pairs={{0,1},{1,0},{2,3},{3,2},{4,5},{5,4},{6,7},{7,6},{8,9},{9,8},{10,11... | collective-permute-start | bytes 9437192 | tf_op jit(solution)/shard_map/T_wg/ppermute | solution.py:251
  3.2 15.0 %collective-permute-start.3 = (bf16[1,1,2048,768]{3,2,1,0:T(8,128)(2,1)}, bf16[1,1,2048,768]{3,2,1,0:T(8,128)(2,1)}, u32[]{:S(2)}, u32[]{:S(2)}) collective-permute-start(bf16[1,1,2048,768]{3,2,1,0:T(8,128)(2,1)} %refs_5_.7), channel_id=1, source_target_pairs={{0,1},{1,0},{2,3},{3,2},{4,5},{5,4},{6,7},{7,6},{8,9},{9,8},{10,11... | collective-permute-start | bytes 9437192 | tf_op jit(solution)/shard_map/T_wu/ppermute | solution.py:251
  3.2 13.9 %collective-permute-start.4 = (bf16[1,1,16,48,768]{4,3,2,1,0:T(8,128)(2,1)}, bf16[1,1,16,48,768]{4,3,2,1,0:T(8,128)(2,1)S(1)}, u32[]{:S(2)}, u32[]{:S(2)}) collective-permute-start(bf16[1,1,16,48,768]{4,3,2,1,0:T(8,128)(2,1)} %refs_10_.3), channel_id=1, source_target_pairs={{0,1},{1,0},{2,3},{3,2},{4,5},{5,4},{6,7},{7,6},{8,9},{9,8},{10,11... | collective-permute-start | bytes 3538952 | tf_op jit(solution)/shard_map/T_sg/ppermute | solution.py:251
  3.7 10.0 %collective-permute-start.1 = (bf16[64,2176]{1,0:T(8,128)(2,1)}, bf16[64,2176]{1,0:T(8,128)(2,1)S(1)}, u32[]{:S(2)}, u32[]{:S(2)}) collective-permute-start(bf16[64,2176]{1,0:T(8,128)(2,1)} %get-tuple-element.57.refs_0_), channel_id=1, source_target_pairs={{0,2},{1,3},{2,0},{3,1},{4,6},{5,7},{6,4},{7,5},{8,10},{9,11},{10,... | collective-permute-start | bytes 835592 | tf_op jit(solution)/shard_map/T_b_x0/ppermute | solution.py:251
  6.2 11.0 %collective-permute-start = (bf16[64,2176]{1,0:T(8,128)(2,1)}, bf16[64,2176]{1,0:T(8,128)(2,1)}, u32[]{:S(2)}, u32[]{:S(2)}) collective-permute-start(bf16[64,2176]{1,0:T(8,128)(2,1)} %get-tuple-element.57.refs_0_), channel_id=1, source_target_pairs={{0,4},{1,5},{2,6},{3,7},{4,8},{5,9},{6,10},{7,11},{8,12},{9,13},{1... | collective-permute-start | bytes 835592 | tf_op jit(solution)/shard_map/T_b_z1/ppermute | solution.py:255
  13.7 29.0 %copy-start.20 = (bf16[64,2176]{1,0:T(8,128)(2,1)}, bf16[64,2176]{1,0:T(8,128)(2,1)S(1)}, u32[]{:S(2)}) copy-start(bf16[64,2176]{1,0:T(8,128)(2,1)S(1)} %collective-permute-done.1.refs_1_) | copy-start | bytes 835588
  17.2 1.0 copy-start.1
  18.2 24.5 %copy-start = (bf16[1,1,2048,768]{3,2,1,0:T(8,128)(2,1)}, bf16[1,1,2048,768]{3,2,1,0:T(8,128)(2,1)S(1)}, u32[]{:S(2)}) copy-start(bf16[1,1,2048,768]{3,2,1,0:T(8,128)(2,1)S(1)} %collective-permute-done.2.refs_7_) | copy-start | bytes 9437188
  18.2 17.1 %collective-permute-start.8 = (bf16[1,1,768,2048]{3,2,1,0:T(8,128)(2,1)}, bf16[1,1,768,2048]{3,2,1,0:T(8,128)(2,1)}, u32[]{:S(2)}, u32[]{:S(2)}) collective-permute-start(bf16[1,1,768,2048]{3,2,1,0:T(8,128)(2,1)} %refs_6_.7), channel_id=1, source_target_pairs={{0,1},{1,0},{2,3},{3,2},{4,5},{5,4},{6,7},{7,6},{8,9},{9,8},{10,11... | collective-permute-start | bytes 9437192 | tf_op jit(solution)/shard_map/T_wd/ppermute | solution.py:251
  18.2 17.1 %collective-permute-start.9 = (bf16[1,1,16,48,768]{4,3,2,1,0:T(8,128)(2,1)}, bf16[1,1,16,48,768]{4,3,2,1,0:T(8,128)(2,1)}, u32[]{:S(2)}, u32[]{:S(2)}) collective-permute-start(bf16[1,1,16,48,768]{4,3,2,1,0:T(8,128)(2,1)} %refs_11_.3), channel_id=1, source_target_pairs={{0,1},{1,0},{2,3},{3,2},{4,5},{5,4},{6,7},{7,6},{8,9},{9,8},{10,11... | collective-permute-start | bytes 3538952 | tf_op jit(solution)/shard_map/T_su/ppermute | solution.py:251
  18.7 11.7 %collective-permute-start.6 = (bf16[64,2176]{1,0:T(8,128)(2,1)}, bf16[64,2176]{1,0:T(8,128)(2,1)}, u32[]{:S(2)}, u32[]{:S(2)}) collective-permute-start(bf16[64,2176]{1,0:T(8,128)(2,1)} %collective-permute-done.refs_2_), channel_id=1, source_target_pairs={{0,4},{1,5},{2,6},{3,7},{4,8},{5,9},{6,10},{7,11},{8,12},{9,13},{1... | collective-permute-start | bytes 835592 | tf_op jit(solution)/shard_map/T_b_z2/ppermute | solution.py:255
  19.3 11.1 %collective-permute-start.5 = (bf16[64,2176]{1,0:T(8,128)(2,1)}, bf16[64,2176]{1,0:T(8,128)(2,1)}, u32[]{:S(2)}, u32[]{:S(2)}) collective-permute-start(bf16[64,2176]{1,0:T(8,128)(2,1)} %collective-permute-done.refs_2_), channel_id=1, source_target_pairs={{0,2},{1,3},{2,0},{3,1},{4,6},{5,7},{6,4},{7,5},{8,10},{9,11},{10,... | collective-permute-start | bytes 835592 | tf_op jit(solution)/shard_map/T_b_x1/ppermute | solution.py:251
  20.8 14.4 %collective-permute-start.7 = (bf16[64,2176]{1,0:T(8,128)(2,1)}, bf16[64,2176]{1,0:T(8,128)(2,1)}, u32[]{:S(2)}, u32[]{:S(2)}) collective-permute-start(bf16[64,2176]{1,0:T(8,128)(2,1)} %get-tuple-element.57.refs_0_), channel_id=1, source_target_pairs={{0,12},{1,13},{2,14},{3,15},{4,0},{5,1},{6,2},{7,3},{8,4},{9,5},{1... | collective-permute-start | bytes 835592 | tf_op jit(solution)/shard_map/T_b_z3/ppermute | solution.py:255
  35.2 21.0 %copy-start.12 = (bf16[64,2176]{1,0:T(8,128)(2,1)S(1)}, bf16[64,2176]{1,0:T(8,128)(2,1)}, u32[]{:S(2)}) copy-start(bf16[64,2176]{1,0:T(8,128)(2,1)} %get-tuple-element.67.refs_0_) | copy-start | bytes 835588
  35.3 18.8 %collective-permute-start.13 = (bf16[64,2176]{1,0:T(8,128)(2,1)}, bf16[64,2176]{1,0:T(8,128)(2,1)S(1)}, u32[]{:S(2)}, u32[]{:S(2)}) collective-permute-start(bf16[64,2176]{1,0:T(8,128)(2,1)} %get-tuple-element.67.refs_0_), channel_id=1, source_target_pairs={{0,2},{1,3},{2,0},{3,1},{4,6},{5,7},{6,4},{7,5},{8,10},{9,11},{10,... | collective-permute-start | bytes 835592 | tf_op jit(solution)/shard_map/T_f_x0/ppermute | solution.py:251
  35.9 18.2 %collective-permute-start.10 = (bf16[64,2176]{1,0:T(8,128)(2,1)}, bf16[64,2176]{1,0:T(8,128)(2,1)S(1)}, u32[]{:S(2)}, u32[]{:S(2)}) collective-permute-start(bf16[64,2176]{1,0:T(8,128)(2,1)} %get-tuple-element.67.refs_0_), channel_id=1, source_target_pairs={{0,4},{1,5},{2,6},{3,7},{4,8},{5,9},{6,10},{7,11},{8,12},{9,13},{1... | collective-permute-start | bytes 835592 | tf_op jit(solution)/shard_map/T_f_z1/ppermute | solution.py:255
  36.7 17.3 %collective-permute-start.14 = (bf16[64,2048]{1,0:T(8,128)(2,1)}, bf16[64,2048]{1,0:T(8,128)(2,1)S(1)}, u32[]{:S(2)}, u32[]{:S(2)}) collective-permute-start(bf16[64,2048]{1,0:T(8,128)(2,1)} %bitcast.37), channel_id=1, source_target_pairs={{0,16},{1,17},{2,18},{3,19},{4,20},{5,21},{6,22},{7,23},{8,24},{9,... | collective-permute-start | bytes 786440 | tf_op jit(solution)/shard_map/T_y1/ppermute | solution.py:266
  38.2 15.9 %collective-permute-start.11 = (bf16[64,2176]{1,0:T(8,128)(2,1)}, bf16[64,2176]{1,0:T(8,128)(2,1)S(1)}, u32[]{:S(2)}, u32[]{:S(2)}) collective-permute-start(bf16[64,2176]{1,0:T(8,128)(2,1)} %collective-permute-done.6.refs_0_), channel_id=1, source_target_pairs={{0,2},{1,3},{2,0},{3,1},{4,6},{5,7},{6,4},{7,5},{8,10},{9,11},{10,... | collective-permute-start | bytes 835592 | tf_op jit(solution)/shard_map/T_b_x2/ppermute | solution.py:251
  39.6 14.5 %collective-permute-start.12 = (bf16[64,2176]{1,0:T(8,128)(2,1)S(1)}, bf16[64,2176]{1,0:T(8,128)(2,1)S(1)}, u32[]{:S(2)}, u32[]{:S(2)}) collective-permute-start(bf16[64,2176]{1,0:T(8,128)(2,1)S(1)} %collective-permute-done.1.refs_1_), channel_id=1, source_target_pairs={{0,12},{1,13},{2,14},{3,15},{4,0},{5,1},{6,2},{7,3},{8,4},{9,5},{1... | collective-permute-start | bytes 835592 | tf_op jit(solution)/shard_map/T_b_w3/ppermute | solution.py:255
  54.1 21.2 %copy-start.13 = (bf16[64,2176]{1,0:T(8,128)(2,1)}, bf16[64,2176]{1,0:T(8,128)(2,1)S(1)}, u32[]{:S(2)}) copy-start(bf16[64,2176]{1,0:T(8,128)(2,1)S(1)} %collective-permute-done.13.refs_1_) | copy-start | bytes 835588
  54.1 17.4 %copy-start.15 = (bf16[64,2176]{1,0:T(8,128)(2,1)}, bf16[64,2176]{1,0:T(8,128)(2,1)S(1)}, u32[]{:S(2)}) copy-start(bf16[64,2176]{1,0:T(8,128)(2,1)S(1)} %collective-permute-done.10.refs_2_) | copy-start | bytes 835588
  54.1 6.0 %copy-start.21 = (bf16[64,2176]{1,0:T(8,128)(2,1)}, bf16[64,2176]{1,0:T(8,128)(2,1)S(1)}, u32[]{:S(2)}) copy-start(bf16[64,2176]{1,0:T(8,128)(2,1)S(1)} %collective-permute-done.11.refs_1_) | copy-start | bytes 835588
  54.1 6.0 %copy-start.22 = (bf16[64,2176]{1,0:T(8,128)(2,1)}, bf16[64,2176]{1,0:T(8,128)(2,1)S(1)}, u32[]{:S(2)}) copy-start(bf16[64,2176]{1,0:T(8,128)(2,1)S(1)} %collective-permute-done.12.refs_3_) | copy-start | bytes 835588
  54.2 19.5 %copy-start.10 = (f32[64,2048]{1,0:T(8,128)S(1)}, f32[64,2048]{1,0:T(8,128)}, u32[]{:S(2)}) copy-start(f32[64,2048]{1,0:T(8,128)} %get-tuple-element.92) | copy-start | bytes 1572868
  54.2 19.5 %copy-start.11 = (f32[64,2048]{1,0:T(8,128)S(1)}, f32[64,2048]{1,0:T(8,128)}, u32[]{:S(2)}) copy-start(f32[64,2048]{1,0:T(8,128)} %get-tuple-element.76) | copy-start | bytes 1572868
  54.2 18.5 %collective-permute-start.18 = (bf16[128,2048]{1,0:T(8,128)(2,1)}, bf16[128,2048]{1,0:T(8,128)(2,1)S(1)}, u32[]{:S(2)}, u32[]{:S(2)}) collective-permute-start(bf16[128,2048]{1,0:T(8,128)(2,1)} %get-tuple-element.68), channel_id=1, source_target_pairs={{0,2},{1,3},{2,0},{3,1},{4,6},{5,7},{6,4},{7,5},{8,10},{9,11},{10,... | collective-permute-start | bytes 1572872 | tf_op jit(solution)/shard_map/T_b_s0/ppermute | solution.py:251
  54.8 16.7 %collective-permute-start.16 = (bf16[64,2176]{1,0:T(8,128)(2,1)S(1)}, bf16[64,2176]{1,0:T(8,128)(2,1)S(1)}, u32[]{:S(2)}, u32[]{:S(2)}) collective-permute-start(bf16[64,2176]{1,0:T(8,128)(2,1)S(1)} %collective-permute-done.10.refs_2_), channel_id=1, source_target_pairs={{0,4},{1,5},{2,6},{3,7},{4,8},{5,9},{6,10},{7,11},{8,12},{9,13},{1... | collective-permute-start | bytes 835592 | tf_op jit(solution)/shard_map/T_f_z2/ppermute | solution.py:255
  54.8 17.9 %collective-permute-start.15 = (bf16[64,2176]{1,0:T(8,128)(2,1)S(1)}, bf16[64,2176]{1,0:T(8,128)(2,1)S(1)}, u32[]{:S(2)}, u32[]{:S(2)}) collective-permute-start(bf16[64,2176]{1,0:T(8,128)(2,1)S(1)} %collective-permute-done.10.refs_2_), channel_id=1, source_target_pairs={{0,2},{1,3},{2,0},{3,1},{4,6},{5,7},{6,4},{7,5},{8,10},{9,11},{10,... | collective-permute-start | bytes 835592 | tf_op jit(solution)/shard_map/T_f_x1/ppermute | solution.py:251
  56.3 16.4 %collective-permute-start.17 = (bf16[64,2176]{1,0:T(8,128)(2,1)S(1)}, bf16[64,2176]{1,0:T(8,128)(2,1)S(1)}, u32[]{:S(2)}, u32[]{:S(2)}) collective-permute-start(bf16[64,2176]{1,0:T(8,128)(2,1)S(1)} %copy-done.12), channel_id=1, source_target_pairs={{0,12},{1,13},{2,14},{3,15},{4,0},{5,1},{6,2},{7,3},{8,4},{9,5},{1... | collective-permute-start | bytes 835592 | tf_op jit(solution)/shard_map/T_f_z3/ppermute | solution.py:255
  71.5 14.7 %copy-start.14 = (bf16[64,2176]{1,0:T(8,128)(2,1)}, bf16[64,2176]{1,0:T(8,128)(2,1)S(1)}, u32[]{:S(2)}) copy-start(bf16[64,2176]{1,0:T(8,128)(2,1)S(1)} %collective-permute-done.16.refs_0_) | copy-start | bytes 835588
  72.7 2.7 %copy-start.17 = (bf16[64,2176]{1,0:T(8,128)(2,1)}, bf16[64,2176]{1,0:T(8,128)(2,1)S(1)}, u32[]{:S(2)}) copy-start(bf16[64,2176]{1,0:T(8,128)(2,1)S(1)} %collective-permute-done.15.refs_3_) | copy-start | bytes 835588
  72.7 13.5 %copy-start.16 = (bf16[64,2176]{1,0:T(8,128)(2,1)}, bf16[64,2176]{1,0:T(8,128)(2,1)S(1)}, u32[]{:S(2)}) copy-start(bf16[64,2176]{1,0:T(8,128)(2,1)S(1)} %collective-permute-done.17.refs_2_) | copy-start | bytes 835588
  72.7 17.6 %collective-permute-start.22 = (bf16[128,2048]{1,0:T(8,128)(2,1)}, bf16[128,2048]{1,0:T(8,128)(2,1)S(1)}, u32[]{:S(2)}, u32[]{:S(2)}) collective-permute-start(bf16[128,2048]{1,0:T(8,128)(2,1)} %get-tuple-element.78), channel_id=1, source_target_pairs={{0,2},{1,3},{2,0},{3,1},{4,6},{5,7},{6,4},{7,5},{8,10},{9,11},{10,... | collective-permute-start | bytes 1572872 | tf_op jit(solution)/shard_map/T_b_s1/ppermute | solution.py:251
  73.7 16.5 %copy-start.8 = (f32[64,2048]{1,0:T(8,128)S(1)}, f32[64,2048]{1,0:T(8,128)}, u32[]{:S(2)}) copy-start(f32[64,2048]{1,0:T(8,128)} %get-tuple-element.80) | copy-start | bytes 1572868
  73.8 16.5 %copy-start.9 = (f32[64,2048]{1,0:T(8,128)S(1)}, f32[64,2048]{1,0:T(8,128)}, u32[]{:S(2)}) copy-start(f32[64,2048]{1,0:T(8,128)} %get-tuple-element.82) | copy-start | bytes 1572868
  73.8 12.4 %collective-permute-start.21 = (bf16[64,2048]{1,0:T(8,128)(2,1)S(1)}, bf16[64,2048]{1,0:T(8,128)(2,1)S(1)}, u32[]{:S(2)}, u32[]{:S(2)}) collective-permute-start(bf16[64,2048]{1,0:T(8,128)(2,1)S(1)} %get-tuple-element.77), channel_id=1, source_target_pairs={{0,12},{1,13},{2,14},{3,15},{4,0},{5,1},{6,2},{7,3},{8,4},{9,5},{1... | collective-permute-start | bytes 786440 | tf_op jit(solution)/shard_map/T_b_r1/ppermute | solution.py:255
  73.8 16.4 %collective-permute-start.19 = (bf16[64,2176]{1,0:T(8,128)(2,1)S(1)}, bf16[64,2176]{1,0:T(8,128)(2,1)S(1)}, u32[]{:S(2)}, u32[]{:S(2)}) collective-permute-start(bf16[64,2176]{1,0:T(8,128)(2,1)S(1)} %collective-permute-done.16.refs_0_), channel_id=1, source_target_pairs={{0,2},{1,3},{2,0},{3,1},{4,6},{5,7},{6,4},{7,5},{8,10},{9,11},{10,... | collective-permute-start | bytes 835592 | tf_op jit(solution)/shard_map/T_f_x2/ppermute | solution.py:251
  75.3 15.0 %collective-permute-start.20 = (bf16[64,2176]{1,0:T(8,128)(2,1)S(1)}, bf16[64,2176]{1,0:T(8,128)(2,1)S(1)}, u32[]{:S(2)}, u32[]{:S(2)}) collective-permute-start(bf16[64,2176]{1,0:T(8,128)(2,1)S(1)} %collective-permute-done.13.refs_1_), channel_id=1, source_target_pairs={{0,12},{1,13},{2,14},{3,15},{4,0},{5,1},{6,2},{7,3},{8,4},{9,5},{1... | collective-permute-start | bytes 835592 | tf_op jit(solution)/shard_map/T_f_w3/ppermute | solution.py:255
  90.3 3.4 %copy-start.18 = (bf16[64,2176]{1,0:T(8,128)(2,1)}, bf16[64,2176]{1,0:T(8,128)(2,1)S(1)}, u32[]{:S(2)}) copy-start(bf16[64,2176]{1,0:T(8,128)(2,1)S(1)} %collective-permute-done.19.refs_1_) | copy-start | bytes 835588
  90.3 3.4 %copy-start.19 = (bf16[64,2176]{1,0:T(8,128)(2,1)}, bf16[64,2176]{1,0:T(8,128)(2,1)S(1)}, u32[]{:S(2)}) copy-start(bf16[64,2176]{1,0:T(8,128)(2,1)S(1)} %collective-permute-done.20.refs_3_) | copy-start | bytes 835588
  90.4 17.0 %copy-start.3 = (bf16[1,64,2048]{2,1,0:T(8,128)(2,1)S(1)}, bf16[1,64,2048]{2,1,0:T(8,128)(2,1)}, u32[]{:S(2)}) copy-start(bf16[1,64,2048]{2,1,0:T(8,128)(2,1)} %param.20) | copy-start | bytes 786436
  90.4 17.3 %copy-start.2 = (bf16[1,64,2048]{2,1,0:T(8,128)(2,1)S(1)}, bf16[1,64,2048]{2,1,0:T(8,128)(2,1)}, u32[]{:S(2)}) copy-start(bf16[1,64,2048]{2,1,0:T(8,128)(2,1)} %param.21) | copy-start | bytes 786436
  90.4 17.0 %collective-permute-start.24 = (bf16[64,2048]{1,0:T(8,128)(2,1)S(1)}, bf16[64,2048]{1,0:T(8,128)(2,1)S(1)}, u32[]{:S(2)}, u32[]{:S(2)}) collective-permute-start(bf16[64,2048]{1,0:T(8,128)(2,1)S(1)} %get-tuple-element.81), channel_id=1, source_target_pairs={{0,8},{1,9},{2,10},{3,11},{4,12},{5,13},{6,14},{7,15},{8,0},{9,1},... | collective-permute-start | bytes 786440 | tf_op jit(solution)/shard_map/T_b_r2/ppermute | solution.py:255
  90.5 16.9 %collective-permute-start.25 = (bf16[64,2048]{1,0:T(8,128)(2,1)S(1)}, bf16[64,2048]{1,0:T(8,128)(2,1)S(1)}, u32[]{:S(2)}, u32[]{:S(2)}) collective-permute-start(bf16[64,2048]{1,0:T(8,128)(2,1)S(1)} %get-tuple-element.83), channel_id=1, source_target_pairs={{0,4},{1,5},{2,6},{3,7},{4,8},{5,9},{6,10},{7,11},{8,12},{9,13},{1... | collective-permute-start | bytes 786440 | tf_op jit(solution)/shard_map/T_b_r3/ppermute | solution.py:255
  91.9 17.4 %collective-permute-start.23 = (bf16[128,2048]{1,0:T(8,128)(2,1)}, bf16[128,2048]{1,0:T(8,128)(2,1)S(1)}, u32[]{:S(2)}, u32[]{:S(2)}) collective-permute-start(bf16[128,2048]{1,0:T(8,128)(2,1)} %get-tuple-element.79), channel_id=1, source_target_pairs={{0,2},{1,3},{2,0},{3,1},{4,6},{5,7},{6,4},{7,5},{8,10},{9,11},{10,... | collective-permute-start | bytes 1572872 | tf_op jit(solution)/shard_map/T_f_s0/ppermute | solution.py:251
  104.5 4.8 %copy-start.24 = (bf16[64,2048]{1,0:T(8,128)(2,1)S(1)}, bf16[64,2048]{1,0:T(8,128)(2,1)}, u32[]{:S(2)}) copy-start(bf16[64,2048]{1,0:T(8,128)(2,1)} %get-tuple-element.91) | copy-start | bytes 786436
  104.5 5.3 %copy-start.6 = (f32[64,2048]{1,0:T(8,128)S(1)}, f32[64,2048]{1,0:T(8,128)}, u32[]{:S(2)}) copy-start(f32[64,2048]{1,0:T(8,128)} %get-tuple-element.72) | copy-start | bytes 1572868
  104.5 5.3 %copy-start.7 = (f32[64,2048]{1,0:T(8,128)S(1)}, f32[64,2048]{1,0:T(8,128)}, u32[]{:S(2)}) copy-start(f32[64,2048]{1,0:T(8,128)} %get-tuple-element.88) | copy-start | bytes 1572868
  104.5 12.5 %copy-start.23 = (bf16[64,2048]{1,0:T(8,128)(2,1)S(1)}, bf16[64,2048]{1,0:T(8,128)(2,1)}, u32[]{:S(2)}) copy-start(bf16[64,2048]{1,0:T(8,128)(2,1)} %get-tuple-element.96) | copy-start | bytes 786436
  104.5 12.5 %copy-start.5 = (f32[64,2048]{1,0:T(8,128)S(1)}, f32[64,2048]{1,0:T(8,128)}, u32[]{:S(2)}) copy-start(f32[64,2048]{1,0:T(8,128)} %get-tuple-element.90) | copy-start | bytes 1572868
  104.5 18.8 %copy-start.4 = (f32[64,2048]{1,0:T(8,128)S(1)}, f32[64,2048]{1,0:T(8,128)}, u32[]{:S(2)}) copy-start(f32[64,2048]{1,0:T(8,128)} %get-tuple-element.95) | copy-start | bytes 1572868
  108.0 20.2 %collective-permute-start.32 = (bf16[64,2048]{1,0:T(8,128)(2,1)S(1)}, bf16[64,2048]{1,0:T(8,128)(2,1)S(1)}, u32[]{:S(2)}, u32[]{:S(2)}) collective-permute-start(bf16[64,2048]{1,0:T(8,128)(2,1)S(1)} %fusion.5), channel_id=1, source_target_pairs={{0,16},{1,17},{2,18},{3,19},{4,20},{5,21},{6,22},{7,23},{8,24},{9,... | collective-permute-start | bytes 786440 | tf_op jit(solution)/shard_map/T_b_y/ppermute | solution.py:266
  109.3 7.7 %collective-permute-start.28 = (bf16[64,2048]{1,0:T(8,128)(2,1)S(1)}, bf16[64,2048]{1,0:T(8,128)(2,1)S(1)}, u32[]{:S(2)}, u32[]{:S(2)}) collective-permute-start(bf16[64,2048]{1,0:T(8,128)(2,1)S(1)} %copy-done.24), channel_id=1, source_target_pairs={{0,2},{1,3},{2,0},{3,1},{4,6},{5,7},{6,4},{7,5},{8,10},{9,11},{10,... | collective-permute-start | bytes 786440 | tf_op jit(solution)/shard_map/T_f_s2/ppermute | solution.py:251
  109.9 18.3 %collective-permute-start.27 = (bf16[64,2048]{1,0:T(8,128)(2,1)S(1)}, bf16[64,2048]{1,0:T(8,128)(2,1)S(1)}, u32[]{:S(2)}, u32[]{:S(2)}) collective-permute-start(bf16[64,2048]{1,0:T(8,128)(2,1)S(1)} %get-tuple-element.89), channel_id=1, source_target_pairs={{0,28},{1,29},{2,30},{3,31},{4,16},{5,17},{6,18},{7,19},{8,20},{9,... | collective-permute-start | bytes 786440 | tf_op jit(solution)/shard_map/T_f_r1/ppermute | solution.py:266
  110.0 21.1 %collective-permute-start.26 = (bf16[64,2048]{1,0:T(8,128)(2,1)S(1)}, bf16[64,2048]{1,0:T(8,128)(2,1)S(1)}, u32[]{:S(2)}, u32[]{:S(2)}) collective-permute-start(bf16[64,2048]{1,0:T(8,128)(2,1)S(1)} %get-tuple-element.87), channel_id=1, source_target_pairs={{0,16},{1,17},{2,18},{3,19},{4,20},{5,21},{6,22},{7,23},{8,24},{9,... | collective-permute-start | bytes 786440 | tf_op jit(solution)/shard_map/T_f_r0/ppermute | solution.py:266
  117.0 6.4 %collective-permute-start.30 = (bf16[64,2048]{1,0:T(8,128)(2,1)S(1)}, bf16[64,2048]{1,0:T(8,128)(2,1)S(1)}, u32[]{:S(2)}, u32[]{:S(2)}) collective-permute-start(bf16[64,2048]{1,0:T(8,128)(2,1)S(1)} %copy-done.23), channel_id=1, source_target_pairs={{0,2},{1,3},{2,0},{3,1},{4,6},{5,7},{6,4},{7,5},{8,10},{9,11},{10,... | collective-permute-start | bytes 786440 | tf_op jit(solution)/shard_map/T_f_s3/ppermute | solution.py:251
  117.1 11.1 %collective-permute-start.29 = (bf16[64,2048]{1,0:T(8,128)(2,1)S(1)}, bf16[64,2048]{1,0:T(8,128)(2,1)S(1)}, u32[]{:S(2)}, u32[]{:S(2)}) collective-permute-start(bf16[64,2048]{1,0:T(8,128)(2,1)S(1)} %add_convert_fusion.2), channel_id=1, source_target_pairs={{0,24},{1,25},{2,26},{3,27},{4,28},{5,29},{6,30},{7,31},{8,16},{9,... | collective-permute-start | bytes 786440 | tf_op jit(solution)/shard_map/T_f_r2/ppermute | solution.py:266
  128.2 10.0 %collective-permute-start.31 = (bf16[64,2048]{1,0:T(8,128)(2,1)S(1)}, bf16[64,2048]{1,0:T(8,128)(2,1)S(1)}, u32[]{:S(2)}, u32[]{:S(2)}) collective-permute-start(bf16[64,2048]{1,0:T(8,128)(2,1)S(1)} %add_convert_fusion.1), channel_id=1, source_target_pairs={{0,20},{1,21},{2,22},{3,23},{4,24},{5,25},{6,26},{7,27},{8,28},{9,... | collective-permute-start | bytes 786440 | tf_op jit(solution)/shard_map/T_f_r3/ppermute | solution.py:266

commit v4 on v3

--- a/solution.py
+++ b/solution.py
@@ -12,7 +12,7 @@
 bf16 = jnp.bfloat16
 LANES = 128
 TILE = 256
-OWN = f32
+OWN = bf16
 VMEM_LIMIT = 56 * 1024 * 1024
 PACK_VMEM_LIMIT = 56 * 1024 * 1024
 TURNED = (((1,), (1,)), ((), ()))
@@ -303,26 +303,27 @@
         held[backward][k] = farther(ready, k, names[backward])
         return [held[backward][k]]
 
-    def aside(backward, k, *earlier):
+    def aside(backward, k, hop, *earlier):
         known, name = across[backward], names[backward]
-        if 2 * k <= line:
+        if hop:
+            value = after(known[(k - hop) % line], *earlier)
+            known[k] = shift(value, hop, f"T_{name}_w{k}")
+        else:
             known[k] = swap(after(held[backward][k], *earlier), 2, f"T_{name}_x{k}")
-        else:
-            known[k] = shift(after(known[(k + 1) % line], *earlier), -1, f"T_{name}_w{k}")
         return [known[k]]
 
-    def experts_on(backward, i, *earlier):
-        chunk, apart = chunks[i], not backward and i == last
+    def experts_on(backward, chunk, *earlier):
+        apart = not backward and chunk == chunks[last]
         rows = [(r, 0) for k in chunk for r in (held[backward][k], across[backward][k])]
         out = run_experts(
-            backward, experts, tokens, i, apart, after(table, *earlier), rows,
-            mine, theirs, kept_mine, kept_theirs, gain,
+            backward, experts, tokens, chunks.index(chunk), apart,
+            after(table, *earlier), rows, mine, theirs, kept_mine, kept_theirs, gain,
         )
         return dict(zip(chunk, out)), out[len(chunk) :]
 
     def chip_sum(backward, k, own, piece):
-        total = own + piece.astype(f32)
-        return total if backward and k == 0 else total.astype(bf16)
+        total = own.astype(f32) + piece.astype(f32)
+        return total if k == 0 else total.astype(bf16)
 
     def chip_sums(backward, chunk, own, sent, label, *earlier):
         came = swap(after(sent[0], *earlier), 2, label)
@@ -342,84 +343,96 @@
         came[backward].extend(moved)
         return moved
 
-    near, far = chunks[0][1], chunks[-1][-1]
-    wave = along(True, near) + aside(True, 0)
+    near = chunks[0][1]
+    wave = along(True, near) + aside(True, 0, 0)
     theirs_gate = swap(after(w_gate, packed[0]), 1, "T_wg")
-    theirs_up = swap(after(w_up, packed[0]), 1, "T_wu")
     theirs_kept_gate = swap(after(saved_gate, packed[0]), 1, "T_sg")
-    wave += [theirs_gate, theirs_up, theirs_kept_gate]
+    theirs_kept_up = swap(after(saved_up, packed[0]), 1, "T_su")
+    wave += [theirs_gate, theirs_kept_gate, theirs_kept_up]
     table = after(table, *wave)
+    theirs_up = swap(after(w_up, *wave), 1, "T_wu")
     theirs_down = swap(after(w_down, *wave), 1, "T_wd")
-    theirs_kept_up = swap(after(saved_up, *wave), 1, "T_su")
-    moved = aside(True, near, *wave)
+    moved = aside(True, near, 0, *wave)
     for k in chunks[1]:
         moved += along(True, k, *wave)
-    wave = moved + [theirs_down, theirs_kept_up, table]
+    wave = moved + [theirs_up, theirs_down, table]
     kept_theirs = (theirs_kept_gate, theirs_kept_up)
     mine, theirs = (w_gate, w_up, w_down), (theirs_gate, theirs_up, theirs_down)
     kept_mine = (saved_gate, saved_up)
 
-    runs, came = {}, {True: [], False: []}
-    sums = []
-    half = len(chunks)
-    for p in range(2 * half):
-        backward, i = p < half, p % half
-        moved = []
-        if backward and i < last:
-            for k in chunks[i + 1]:
-                moved += aside(True, k, *wave)
-            if i + 1 < last:
-                for k in chunks[i + 2]:
-                    moved += along(True, k, *wave)
-        if p == half - 2:
-            moved += aside(False, 0, *wave) + along(False, near, *wave)
-            residual = relay(after(input_rows, *wave), 1, "T_y1")
-            moved.append(residual)
-        if p == half - 1:
-            moved += aside(False, near, *wave)
-        if 0 <= p - half + 1 < last:
-            for k in chunks[p - half + 2]:
-                moved += along(False, k, *wave)
-        if 0 <= p - half < last:
-            for k in chunks[p - half + 1]:
-                moved += aside(False, k, *wave)
-        for way, chunk_sums in sums:
-            moved += send_sums(way, chunk_sums, *wave)
-        sums = []
-        if p:
-            way, j = p <= half, (p - 1) % half
-            own, sent = runs[p - 1]
-            chunk_sums, arrived = chip_sums(
-                way, chunks[j], own, sent, f"T_{names[way]}_s{j}", *wave
-            )
-            sums = [(way, chunk_sums)]
-            moved.append(arrived)
-        runs[p] = experts_on(backward, i, *wave)
-        wave = moved + list(runs[p][1])
     def summed(values):
         total = values[0].astype(f32)
         for value in values[1:]:
             total = total + value.astype(f32)
         return total
 
-    weighted = summed(came[True])
-    saved_input = x_backward[0].astype(f32)
-    scale_rows = inverse_rms(x_backward[0])
-    inner = jnp.mean(weighted * saved_input, axis=-1, keepdims=True)
-    d_input = (
-        dy_backward[0].astype(f32)
-        + scale_rows * weighted
-        - saved_input * scale_rows * scale_rows * scale_rows * inner
-    ).astype(bf16)
+    def end_backward(*earlier):
+        weighted = summed([after(value, *earlier) for value in came[True]])
+        saved_input = x_backward[0].astype(f32)
+        scale_rows = inverse_rms(x_backward[0])
+        inner = jnp.mean(weighted * saved_input, axis=-1, keepdims=True)
+        d_input = (
+            dy_backward[0].astype(f32)
+            + scale_rows * weighted
+            - saved_input * scale_rows * scale_rows * scale_rows * inner
+        ).astype(bf16)
+        return d_input
+
+    half = len(chunks)
+    works = [(True, chunk) for chunk in chunks] + [(False, chunk) for chunk in chunks]
+    runs, came, sums = [], {True: [], False: []}, {}
+    for p, (backward, chunk) in enumerate(works):
+        moved = []
+        if p < last:
+            right, left = chunks[p + 1]
+            moved += aside(True, right, 0, *wave) + aside(True, left, -1, *wave)
+            if p + 1 < last:
+                for k in chunks[p + 2]:
+                    moved += along(True, k, *wave)
+        if p == half - 2:
+            moved += aside(False, 0, 0, *wave) + along(False, near, *wave)
+            residual = relay(after(input_rows, *wave), 1, "T_y1")
+            moved.append(residual)
+        if p == half - 1:
+            moved += aside(False, near, 0, *wave)
+        if 0 < p - half + 2 <= last:
+            for k in chunks[p - half + 2]:
+                moved += along(False, k, *wave)
+        if 0 < p - half + 1 <= last:
+            right, left = chunks[p - half + 1]
+            moved += aside(False, right, 0, *wave) + aside(False, left, -1, *wave)
+        if p == half + 2:
+            near_sums = sums[half]
+        elif p >= 2:
+            moved += send_sums(works[p - 2][0], sums[p - 2], *wave)
+        if p:
+            way, before = works[p - 1]
+            own, sent = runs[p - 1]
+            label = f"T_{names[way]}_s{before[0]}"
+            sums[p - 1], arrived = chip_sums(way, before, own, sent, label, *wave)
+            moved.append(arrived)
+        runs.append(experts_on(backward, chunk, *wave))
+        wave = moved + list(runs[p][1])
+    own, sent = runs[-1]
+    d_input = end_backward(*wave)
     next_backward = relay(d_input, -1, "T_b_y")
-
-    send_sums(*sums[0], *wave)
-    own, sent = runs[2 * half - 1]
-    ahead = d_input
+    def end_near(*earlier):
+        part = shift(after(near_sums[near], *earlier), -near, "T_f_near")
+        return (near_sums[0] + part.astype(f32)).astype(bf16)
+
+    if half > 2:
+        send_sums(False, sums[len(works) - 2], *wave)
+        joined = end_near(*wave)
+    else:
+        near_sums = sums[len(works) - 2]
+        joined = end_near(*wave)
+    came[False].append(relay(joined, 1, "T_f_joined"))
+    before, ahead = wave, d_input
     for k, value in zip(chunks[last], sent):
-        arrived = swap(after(value, *wave), 2, f"T_f_s{k}")
-        send_sums(False, {k: after(chip_sum(False, k, own[k], arrived), ahead)})
-        ahead, wave = came[False][-1], [arrived]
+        arrived = swap(after(value, *before), 2, f"T_f_s{k}")
+        final = chip_sum(False, k, own[k], arrived)
+        send_sums(False, {k: after(final, ahead)})
+        before, ahead = [arrived], joined
     next_forward = (summed(came[False]) + residual.astype(f32)).astype(bf16)
     return (next_forward[None], next_backward[None])
 

time: 140 us -> 137 us (0.979)
  waiting for transfers between devices: 53.6 us -> 48.2 us
  starting transfers between devices: 34.3 us -> 36.3 us
    ppermute x11 -> x12, starting transfers between devices: 13.8 us -> 16.8 us  [shift(): lax.ppermute(value, 'expert', [(i, (i + 4 * steps) % experts) for i in ra...]
    ppermute x6 -> x5, waiting for transfers between devices: 14.8 us -> 12 us  [relay(): return lax.ppermute(value, ('section', 'expert'), pairs)]
    ppermute x16, waiting for transfers between devices: 21 us -> 18.5 us  [swap(): return lax.ppermute(value, 'expert', [(i, i ^ bit) for i in range(experts)])]
    ppermute x16, starting transfers between devices: 14.1 us -> 12.3 us  [swap(): return lax.ppermute(value, 'expert', [(i, i ^ bit) for i in range(experts)])]
    ppermute x6 -> x5, starting transfers between devices: 6.31 us -> 7.16 us  [relay(): return lax.ppermute(value, ('section', 'expert'), pairs)]
    ppermute x11 -> x12, waiting for transfers between devices: 17.8 us -> 17.7 us  [shift(): lax.ppermute(value, 'expert', [(i, (i + 4 * steps) % experts) for i in ra...]
where the time goes in v4:
time: 137 us; the launch traced here: 136 us
  waiting for transfers between devices  48.2 us (35%)
  Pallas kernels  46 us (34%)
  starting transfers between devices  36.3 us (26%)
  other arithmetic  2.51 us (2%)
  local copies, waits for them, and re-layouts  2.35 us (2%)
    pallas_call x4, Pallas kernels, run_experts(): pl.pallas_call(functools.partial(experts_kernel, backward, experts, token...  43.9 us
    ppermute x16, waiting for transfers between devices, swap(): return lax.ppermute(value, 'expert', [(i, i ^ bit) for i in range(experts)])  18.5 us
    ppermute x12, waiting for transfers between devices, shift(): lax.ppermute(value, 'expert', [(i, (i + 4 * steps) % experts) for i in ra...  17.7 us
    ppermute x12, starting transfers between devices, shift(): lax.ppermute(value, 'expert', [(i, (i + 4 * steps) % experts) for i in ra...  16.8 us
    ppermute x16, starting transfers between devices, swap(): return lax.ppermute(value, 'expert', [(i, i ^ bit) for i in range(experts)])  12.3 us
    ppermute x5, waiting for transfers between devices, relay(): return lax.ppermute(value, ('section', 'expert'), pairs)  12 us
    ppermute x5, starting transfers between devices, relay(): return lax.ppermute(value, ('section', 'expert'), pairs)  7.16 us
  transfers between devices with their start and end apart: 33, of which 12 were waited for; matrix products, arithmetic and copies ran while one was open for 1% of the time, Pallas kernels for 32%

profile of v4, /device:TPU:0, one launch (start us, length us, event | category | flops | bytes accessed | tf_op | source)
XLA Modules:
  0.0 136.3 jit_solution(2415151508934455181)
XLA Ops:
  0.6 2.1 %pack.1 = (bf16[64,2176]{1,0:T(8,128)(2,1)}, bf16[64,2176]{1,0:T(8,128)(2,1)}) custom-call(bf16[64,2048]{1,0:T(8,128)(2,1)} %bitcast.35, bf16[64,2048]{1,0:T(8,128)(2,1)} %bitcast.36, f32[1,2048]{1,0:T(1,128)} %refs_14_.3, s32[8,64]{1,0:T(8,128)} %bitcast.39, f32[8,64]{1,0:T(8,128)} %bitcast.40, s32[8,64]{1,0:T(8,128)} %bitcast.41, f32[8,64]{1,0:T(8,128)} %bitcast.42), custom_call_target="tpu_custom_call" | custom-call | tf_op jit(solution)/shard_map/pack/pallas_call | solution.py:55
  2.7 0.5 collective-permute-start.2
  3.2 0.1 collective-permute-start.3
  3.2 0.5 collective-permute-start.4
  3.7 2.5 %collective-permute-start.1 = (bf16[64,2176]{1,0:T(8,128)(2,1)}, bf16[64,2176]{1,0:T(8,128)(2,1)S(1)}, u32[]{:S(2)}, u32[]{:S(2)}) collective-permute-start(bf16[64,2176]{1,0:T(8,128)(2,1)} %get-tuple-element.60.refs_0_), channel_id=1, source_target_pairs={{0,2},{1,3},{2,0},{3,1},{4,6},{5,7},{6,4},{7,5},{8,10},{9,11},{10,... | collective-permute-start | bytes 835592 | tf_op jit(solution)/shard_map/T_b_x0/ppermute | solution.py:251
  6.2 1.6 %collective-permute-start = (bf16[64,2176]{1,0:T(8,128)(2,1)}, bf16[64,2176]{1,0:T(8,128)(2,1)}, u32[]{:S(2)}, u32[]{:S(2)}) collective-permute-start(bf16[64,2176]{1,0:T(8,128)(2,1)} %get-tuple-element.60.refs_0_), channel_id=1, source_target_pairs={{0,4},{1,5},{2,6},{3,7},{4,8},{5,9},{6,10},{7,11},{8,12},{9,13},{1... | collective-permute-start | bytes 835592 | tf_op jit(solution)/shard_map/T_b_z1/ppermute | solution.py:255
  7.7 6.0 %collective-permute-done.1.refs_1_ = bf16[64,2176]{1,0:T(8,128)(2,1)S(1)} collective-permute-done((bf16[64,2176]{1,0:T(8,128)(2,1)}, bf16[64,2176]{1,0:T(8,128)(2,1)S(1)}, u32[]{:S(2)}, u32[]{:S(2)}) %collective-permute-start.1) | collective-permute-done | bytes 278560 | tf_op jit(solution)/shard_map/T_b_x0/ppermute | solution.py:251
  13.7 3.5 %collective-permute-done.refs_2_ = bf16[64,2176]{1,0:T(8,128)(2,1)} collective-permute-done((bf16[64,2176]{1,0:T(8,128)(2,1)}, bf16[64,2176]{1,0:T(8,128)(2,1)}, u32[]{:S(2)}, u32[]{:S(2)}) %collective-permute-start) | collective-permute-done | bytes 278560 | tf_op jit(solution)/shard_map/T_b_z1/ppermute | solution.py:255
  17.2 1.0 copy-done.1
  18.2 0.4 copy-done.2
  18.6 0.1 collective-permute-start.8
  18.7 1.7 %collective-permute-start.7 = (bf16[64,2176]{1,0:T(8,128)(2,1)}, bf16[64,2176]{1,0:T(8,128)(2,1)S(1)}, u32[]{:S(2)}, u32[]{:S(2)}) collective-permute-start(bf16[64,2176]{1,0:T(8,128)(2,1)} %get-tuple-element.60.refs_0_), channel_id=1, source_target_pairs={{0,12},{1,13},{2,14},{3,15},{4,0},{5,1},{6,2},{7,3},{8,4},{9,5},{1... | collective-permute-start | bytes 835592 | tf_op jit(solution)/shard_map/T_b_z3/ppermute | solution.py:255
  20.4 0.5 collective-permute-start.5
  21.0 0.3 collective-permute-start.6
  21.3 0.1 stack.59
  21.4 0.1 stack.53
  21.4 0.5 pad_add_fusion.table
  22.0 6.3 %collective-permute-done.7.refs_2_ = bf16[64,2176]{1,0:T(8,128)(2,1)S(1)} collective-permute-done((bf16[64,2176]{1,0:T(8,128)(2,1)}, bf16[64,2176]{1,0:T(8,128)(2,1)S(1)}, u32[]{:S(2)}, u32[]{:S(2)}) %collective-permute-start.7) | collective-permute-done | bytes 278560 | tf_op jit(solution)/shard_map/T_b_z3/ppermute | solution.py:255
  28.3 1.1 collective-permute-done.5.refs_3_
  29.4 4.7 %collective-permute-done.6.refs_0_ = bf16[64,2176]{1,0:T(8,128)(2,1)} collective-permute-done((bf16[64,2176]{1,0:T(8,128)(2,1)}, bf16[64,2176]{1,0:T(8,128)(2,1)}, u32[]{:S(2)}, u32[]{:S(2)}) %collective-permute-start.6) | collective-permute-done | bytes 278560 | tf_op jit(solution)/shard_map/T_b_z2/ppermute | solution.py:255
  34.1 1.7 %collective-permute-start.10 = (bf16[64,2176]{1,0:T(8,128)(2,1)}, bf16[64,2176]{1,0:T(8,128)(2,1)S(1)}, u32[]{:S(2)}, u32[]{:S(2)}) collective-permute-start(bf16[64,2176]{1,0:T(8,128)(2,1)} %get-tuple-element.70.refs_0_), channel_id=1, source_target_pairs={{0,4},{1,5},{2,6},{3,7},{4,8},{5,9},{6,10},{7,11},{8,12},{9,13},{1... | collective-permute-start | bytes 835592 | tf_op jit(solution)/shard_map/T_f_z1/ppermute | solution.py:255
  35.8 0.5 collective-permute-start.13
  36.3 2.2 %collective-permute-start.12 = (bf16[64,2176]{1,0:T(8,128)(2,1)}, bf16[64,2176]{1,0:T(8,128)(2,1)S(1)}, u32[]{:S(2)}, u32[]{:S(2)}) collective-permute-start(bf16[64,2176]{1,0:T(8,128)(2,1)} %copy-done.14), channel_id=1, source_target_pairs={{0,12},{1,13},{2,14},{3,15},{4,0},{5,1},{6,2},{7,3},{8,4},{9,5},{1... | collective-permute-start | bytes 835592 | tf_op jit(solution)/shard_map/T_b_w3/ppermute | solution.py:255
  38.5 1.5 %collective-permute-start.11 = (bf16[64,2176]{1,0:T(8,128)(2,1)}, bf16[64,2176]{1,0:T(8,128)(2,1)S(1)}, u32[]{:S(2)}, u32[]{:S(2)}) collective-permute-start(bf16[64,2176]{1,0:T(8,128)(2,1)} %collective-permute-done.6.refs_0_), channel_id=1, source_target_pairs={{0,2},{1,3},{2,0},{3,1},{4,6},{5,7},{6,4},{7,5},{8,10},{9,11},{10,... | collective-permute-start | bytes 835592 | tf_op jit(solution)/shard_map/T_b_x2/ppermute | solution.py:251
  40.0 1.5 %collective-permute-start.14 = (bf16[64,2048]{1,0:T(8,128)(2,1)}, bf16[64,2048]{1,0:T(8,128)(2,1)S(1)}, u32[]{:S(2)}, u32[]{:S(2)}) collective-permute-start(bf16[64,2048]{1,0:T(8,128)(2,1)} %bitcast.37), channel_id=1, source_target_pairs={{0,16},{1,17},{2,18},{3,19},{4,20},{5,21},{6,22},{7,23},{8,24},{9,... | collective-permute-start | bytes 786440 | tf_op jit(solution)/shard_map/T_y1/ppermute | solution.py:266
  41.5 11.2 %experts_backward.2 = (bf16[64,2048]{1,0:T(8,128)(2,1)}, bf16[64,2048]{1,0:T(8,128)(2,1)}, bf16[128,2048]{1,0:T(8,128)(2,1)}) custom-call(s32[2,6]{1,0:T(2,128)} %pad_add_fusion.table, bf16[64,2176]{1,0:T(8,128)(2,1)} %get-tuple-element.60.refs_0_, bf16[64,2176]{1,0:T(8,128)(2,1)} %copy-done.14, bf16[64,2176]{1,0:T(8,128)(2,1)} %collective-permute-done.refs_2_, ...), custom_call_target="tpu_custom_call" | custom-call | flops 4831838208 | bytes 18874368 | tf_op jit(solution)/shard_map/experts_backward/pallas_call | solution.py:210
  52.9 0.6 collective-permute-start.18
  53.5 1.5 %collective-permute-start.15 = (bf16[64,2176]{1,0:T(8,128)(2,1)S(1)}, bf16[64,2176]{1,0:T(8,128)(2,1)S(1)}, u32[]{:S(2)}, u32[]{:S(2)}) collective-permute-start(bf16[64,2176]{1,0:T(8,128)(2,1)S(1)} %collective-permute-done.10.refs_2_), channel_id=1, source_target_pairs={{0,2},{1,3},{2,0},{3,1},{4,6},{5,7},{6,4},{7,5},{8,10},{9,11},{10,... | collective-permute-start | bytes 835592 | tf_op jit(solution)/shard_map/T_f_x1/ppermute | solution.py:251
  55.0 3.8 %collective-permute-start.17 = (bf16[64,2176]{1,0:T(8,128)(2,1)S(1)}, bf16[64,2176]{1,0:T(8,128)(2,1)S(1)}, u32[]{:S(2)}, u32[]{:S(2)}) collective-permute-start(bf16[64,2176]{1,0:T(8,128)(2,1)S(1)} %copy-done.5), channel_id=1, source_target_pairs={{0,12},{1,13},{2,14},{3,15},{4,0},{5,1},{6,2},{7,3},{8,4},{9,5},{1... | collective-permute-start | bytes 835592 | tf_op jit(solution)/shard_map/T_f_z3/ppermute | solution.py:255
  58.8 11.2 %experts_backward.3 = (bf16[64,2048]{1,0:T(8,128)(2,1)}, bf16[64,2048]{1,0:T(8,128)(2,1)}, bf16[128,2048]{1,0:T(8,128)(2,1)}) custom-call(s32[2,6]{1,0:T(2,128)} %pad_add_fusion.table, bf16[64,2176]{1,0:T(8,128)(2,1)} %collective-permute-done.6.refs_0_, bf16[64,2176]{1,0:T(8,128)(2,1)} %copy-done.16, bf16[64,2176]{1,0:T(8,128)(2,1)} %copy-done.13, ...), custom_call_target="tpu_custom_call" | custom-call | flops 4831838208 | bytes 18874368 | tf_op jit(solution)/shard_map/experts_backward/pallas_call | solution.py:210
  70.0 1.1 collective-permute-done.15.refs_3_
  71.1 0.6 collective-permute-start.22
  71.7 0.1 convert_add_fusion.1
  71.8 1.2 collective-permute-start.21
  73.1 1.4 %collective-permute-start.20 = (bf16[64,2176]{1,0:T(8,128)(2,1)S(1)}, bf16[64,2176]{1,0:T(8,128)(2,1)S(1)}, u32[]{:S(2)}, u32[]{:S(2)}) collective-permute-start(bf16[64,2176]{1,0:T(8,128)(2,1)S(1)} %collective-permute-done.13.refs_1_), channel_id=1, source_target_pairs={{0,12},{1,13},{2,14},{3,15},{4,0},{5,1},{6,2},{7,3},{8,4},{9,5},{1... | collective-permute-start | bytes 835592 | tf_op jit(solution)/shard_map/T_f_w3/ppermute | solution.py:255
  74.5 0.3 collective-permute-start.19
  74.8 10.8 %experts_forward.2 = (bf16[64,2048]{1,0:T(8,128)(2,1)}, bf16[64,2048]{1,0:T(8,128)(2,1)}, bf16[128,2048]{1,0:T(8,128)(2,1)}) custom-call(s32[2,6]{1,0:T(2,128)} %pad_add_fusion.table, bf16[64,2176]{1,0:T(8,128)(2,1)} %get-tuple-element.70.refs_0_, bf16[64,2176]{1,0:T(8,128)(2,1)} %copy-done.6, bf16[64,2176]{1,0:T(8,128)(2,1)} %copy-done.7, ...), custom_call_target="tpu_custom_call" | custom-call | flops 4831838208 | bytes 18874368 | tf_op jit(solution)/shard_map/experts_forward/pallas_call | solution.py:210
  85.7 3.5 %collective-permute-done.19.refs_1_ = bf16[64,2176]{1,0:T(8,128)(2,1)S(1)} collective-permute-done((bf16[64,2176]{1,0:T(8,128)(2,1)S(1)}, bf16[64,2176]{1,0:T(8,128)(2,1)S(1)}, u32[]{:S(2)}, u32[]{:S(2)}) %collective-permute-start.19) | collective-permute-done | bytes 278560 | tf_op jit(solution)/shard_map/T_f_x2/ppermute | solution.py:251
  89.2 0.5 collective-permute-start.23
  89.8 0.1 add_convert_fusion.4
  89.9 0.3 collective-permute-start.25
  90.2 0.0 copy-start.3
  90.2 1.7 %collective-permute-start.24 = (bf16[64,2048]{1,0:T(8,128)(2,1)S(1)}, bf16[64,2048]{1,0:T(8,128)(2,1)S(1)}, u32[]{:S(2)}, u32[]{:S(2)}) collective-permute-start(bf16[64,2048]{1,0:T(8,128)(2,1)S(1)} %get-tuple-element.85), channel_id=1, source_target_pairs={{0,8},{1,9},{2,10},{3,11},{4,12},{5,13},{6,14},{7,15},{8,0},{9,1},... | collective-permute-start | bytes 786440 | tf_op jit(solution)/shard_map/T_b_r2/ppermute | solution.py:255
  91.9 10.6 %experts_forward.3 = (bf16[64,2048]{1,0:T(8,128)(2,1)}, bf16[64,2048]{1,0:T(8,128)(2,1)}, bf16[64,2048]{1,0:T(8,128)(2,1)}, bf16[64,2048]{1,0:T(8,128)(2,1)}) custom-call(s32[2,6]{1,0:T(2,128)} %pad_add_fusion.table, bf16[64,2176]{1,0:T(8,128)(2,1)} %copy-done.8, bf16[64,2176]{1,0:T(8,128)(2,1)} %copy-done.12, bf16[64,2176]{1,0:T(8,128)(2,1)} %copy-done.9, ...), custom_call_target="tpu_custom_call" | custom-call | flops 4831838208 | bytes 18874368 | tf_op jit(solution)/shard_map/experts_forward/pallas_call | solution.py:210
  102.6 3.3 %collective-permute-done.24 = bf16[64,2048]{1,0:T(8,128)(2,1)S(1)} collective-permute-done((bf16[64,2048]{1,0:T(8,128)(2,1)S(1)}, bf16[64,2048]{1,0:T(8,128)(2,1)S(1)}, u32[]{:S(2)}, u32[]{:S(2)}) %collective-permute-start.24) | collective-permute-done | bytes 262176 | tf_op jit(solution)/shard_map/T_b_r2/ppermute | solution.py:255
  105.9 1.5 %collective-permute-start.28 = (bf16[64,2048]{1,0:T(8,128)(2,1)}, bf16[64,2048]{1,0:T(8,128)(2,1)S(1)}, u32[]{:S(2)}, u32[]{:S(2)}) collective-permute-start(bf16[64,2048]{1,0:T(8,128)(2,1)} %get-tuple-element.93), channel_id=1, source_target_pairs={{0,2},{1,3},{2,0},{3,1},{4,6},{5,7},{6,4},{7,5},{8,10},{9,11},{10,... | collective-permute-start | bytes 786440 | tf_op jit(solution)/shard_map/T_f_s2/ppermute | solution.py:251
  107.4 0.1 add_convert_fusion.6
  107.4 0.8 collective-permute-start.26
  108.3 0.3 fusion
  108.6 0.3 fusion.5
  108.9 2.5 %collective-permute-start.32 = (bf16[64,2048]{1,0:T(8,128)(2,1)S(1)}, bf16[64,2048]{1,0:T(8,128)(2,1)S(1)}, u32[]{:S(2)}, u32[]{:S(2)}) collective-permute-start(bf16[64,2048]{1,0:T(8,128)(2,1)S(1)} %fusion.5), channel_id=1, source_target_pairs={{0,16},{1,17},{2,18},{3,19},{4,20},{5,21},{6,22},{7,23},{8,24},{9,... | collective-permute-start | bytes 786440 | tf_op jit(solution)/shard_map/T_b_y/ppermute | solution.py:266
  111.4 2.1 %collective-permute-done.28 = bf16[64,2048]{1,0:T(8,128)(2,1)S(1)} collective-permute-done((bf16[64,2048]{1,0:T(8,128)(2,1)}, bf16[64,2048]{1,0:T(8,128)(2,1)S(1)}, u32[]{:S(2)}, u32[]{:S(2)}) %collective-permute-start.28) | collective-permute-done | bytes 262176 | tf_op jit(solution)/shard_map/T_f_s2/ppermute | solution.py:251
  113.5 0.1 add_convert_fusion.2
  113.5 1.9 %collective-permute-start.29 = (bf16[64,2048]{1,0:T(8,128)(2,1)S(1)}, bf16[64,2048]{1,0:T(8,128)(2,1)S(1)}, u32[]{:S(2)}, u32[]{:S(2)}) collective-permute-start(bf16[64,2048]{1,0:T(8,128)(2,1)S(1)} %add_convert_fusion.2), channel_id=1, source_target_pairs={{0,24},{1,25},{2,26},{3,27},{4,28},{5,29},{6,30},{7,31},{8,16},{9,... | collective-permute-start | bytes 786440 | tf_op jit(solution)/shard_map/T_f_r2/ppermute | solution.py:266
  115.5 1.1 collective-permute-start.30
  116.6 0.1 add_convert_fusion.3
  116.7 1.2 collective-permute-start.27
  117.9 4.7 %collective-permute-done.30 = bf16[64,2048]{1,0:T(8,128)(2,1)S(1)} collective-permute-done((bf16[64,2048]{1,0:T(8,128)(2,1)S(1)}, bf16[64,2048]{1,0:T(8,128)(2,1)S(1)}, u32[]{:S(2)}, u32[]{:S(2)}) %collective-permute-start.30) | collective-permute-done | bytes 262176 | tf_op jit(solution)/shard_map/T_f_s3/ppermute | solution.py:251
  122.6 0.1 add_convert_fusion.1
  122.6 0.1 collective-permute-start.31
  122.7 9.8 %collective-permute-done.29 = bf16[64,2048]{1,0:T(8,128)(2,1)S(1)} collective-permute-done((bf16[64,2048]{1,0:T(8,128)(2,1)S(1)}, bf16[64,2048]{1,0:T(8,128)(2,1)S(1)}, u32[]{:S(2)}, u32[]{:S(2)}) %collective-permute-start.29) | collective-permute-done | bytes 262176 | tf_op jit(solution)/shard_map/T_f_r2/ppermute | solution.py:266
  132.5 2.2 %collective-permute-done.27 = bf16[64,2048]{1,0:T(8,128)(2,1)S(1)} collective-permute-done((bf16[64,2048]{1,0:T(8,128)(2,1)S(1)}, bf16[64,2048]{1,0:T(8,128)(2,1)S(1)}, u32[]{:S(2)}, u32[]{:S(2)}) %collective-permute-start.27) | collective-permute-done | bytes 262176 | tf_op jit(solution)/shard_map/T_f_joined/ppermute | solution.py:266
  134.8 0.8 fusion.7
  135.6 0.7 copy.16
  (73 shorter events, 0.2 us)
Async XLA Ops:
  2.7 14.5 %collective-permute-start.2 = (bf16[1,1,2048,768]{3,2,1,0:T(8,128)(2,1)}, bf16[1,1,2048,768]{3,2,1,0:T(8,128)(2,1)S(1)}, u32[]{:S(2)}, u32[]{:S(2)}) collective-permute-start(bf16[1,1,2048,768]{3,2,1,0:T(8,128)(2,1)} %refs_4_.7), channel_id=1, source_target_pairs={{0,1},{1,0},{2,3},{3,2},{4,5},{5,4},{6,7},{7,6},{8,9},{9,8},{10,11... | collective-permute-start | bytes 9437192 | tf_op jit(solution)/shard_map/T_wg/ppermute | solution.py:251
  3.2 14.0 %collective-permute-start.3 = (bf16[1,1,16,48,768]{4,3,2,1,0:T(8,128)(2,1)}, bf16[1,1,16,48,768]{4,3,2,1,0:T(8,128)(2,1)S(1)}, u32[]{:S(2)}, u32[]{:S(2)}) collective-permute-start(bf16[1,1,16,48,768]{4,3,2,1,0:T(8,128)(2,1)} %refs_10_.3), channel_id=1, source_target_pairs={{0,1},{1,0},{2,3},{3,2},{4,5},{5,4},{6,7},{7,6},{8,9},{9,8},{10,11... | collective-permute-start | bytes 3538952 | tf_op jit(solution)/shard_map/T_sg/ppermute | solution.py:251
  3.2 13.9 %collective-permute-start.4 = (bf16[1,1,16,48,768]{4,3,2,1,0:T(8,128)(2,1)}, bf16[1,1,16,48,768]{4,3,2,1,0:T(8,128)(2,1)S(1)}, u32[]{:S(2)}, u32[]{:S(2)}) collective-permute-start(bf16[1,1,16,48,768]{4,3,2,1,0:T(8,128)(2,1)} %refs_11_.3), channel_id=1, source_target_pairs={{0,1},{1,0},{2,3},{3,2},{4,5},{5,4},{6,7},{7,6},{8,9},{9,8},{10,11... | collective-permute-start | bytes 3538952 | tf_op jit(solution)/shard_map/T_su/ppermute | solution.py:251
  3.7 10.0 %collective-permute-start.1 = (bf16[64,2176]{1,0:T(8,128)(2,1)}, bf16[64,2176]{1,0:T(8,128)(2,1)S(1)}, u32[]{:S(2)}, u32[]{:S(2)}) collective-permute-start(bf16[64,2176]{1,0:T(8,128)(2,1)} %get-tuple-element.60.refs_0_), channel_id=1, source_target_pairs={{0,2},{1,3},{2,0},{3,1},{4,6},{5,7},{6,4},{7,5},{8,10},{9,11},{10,... | collective-permute-start | bytes 835592 | tf_op jit(solution)/shard_map/T_b_x0/ppermute | solution.py:251
  6.2 11.0 %collective-permute-start = (bf16[64,2176]{1,0:T(8,128)(2,1)}, bf16[64,2176]{1,0:T(8,128)(2,1)}, u32[]{:S(2)}, u32[]{:S(2)}) collective-permute-start(bf16[64,2176]{1,0:T(8,128)(2,1)} %get-tuple-element.60.refs_0_), channel_id=1, source_target_pairs={{0,4},{1,5},{2,6},{3,7},{4,8},{5,9},{6,10},{7,11},{8,12},{9,13},{1... | collective-permute-start | bytes 835592 | tf_op jit(solution)/shard_map/T_b_z1/ppermute | solution.py:255
  13.7 4.5 %copy-start.14 = (bf16[64,2176]{1,0:T(8,128)(2,1)}, bf16[64,2176]{1,0:T(8,128)(2,1)S(1)}, u32[]{:S(2)}) copy-start(bf16[64,2176]{1,0:T(8,128)(2,1)S(1)} %collective-permute-done.1.refs_1_) | copy-start | bytes 835588
  17.2 1.0 copy-start.1
  17.2 1.4 %copy-start.2 = (bf16[1,1,16,48,768]{4,3,2,1,0:T(8,128)(2,1)}, bf16[1,1,16,48,768]{4,3,2,1,0:T(8,128)(2,1)S(1)}, u32[]{:S(2)}) copy-start(bf16[1,1,16,48,768]{4,3,2,1,0:T(8,128)(2,1)S(1)} %collective-permute-done.4.refs_13_) | copy-start | bytes 3538948
  18.2 23.3 %copy-start = (bf16[1,1,2048,768]{3,2,1,0:T(8,128)(2,1)}, bf16[1,1,2048,768]{3,2,1,0:T(8,128)(2,1)S(1)}, u32[]{:S(2)}) copy-start(bf16[1,1,2048,768]{3,2,1,0:T(8,128)(2,1)S(1)} %collective-permute-done.2.refs_7_) | copy-start | bytes 9437188
  18.2 15.9 %collective-permute-start.9 = (bf16[1,1,768,2048]{3,2,1,0:T(8,128)(2,1)}, bf16[1,1,768,2048]{3,2,1,0:T(8,128)(2,1)}, u32[]{:S(2)}, u32[]{:S(2)}) collective-permute-start(bf16[1,1,768,2048]{3,2,1,0:T(8,128)(2,1)} %refs_6_.7), channel_id=1, source_target_pairs={{0,1},{1,0},{2,3},{3,2},{4,5},{5,4},{6,7},{7,6},{8,9},{9,8},{10,11... | collective-permute-start | bytes 9437192 | tf_op jit(solution)/shard_map/T_wd/ppermute | solution.py:251
  18.6 15.5 %collective-permute-start.8 = (bf16[1,1,2048,768]{3,2,1,0:T(8,128)(2,1)}, bf16[1,1,2048,768]{3,2,1,0:T(8,128)(2,1)}, u32[]{:S(2)}, u32[]{:S(2)}) collective-permute-start(bf16[1,1,2048,768]{3,2,1,0:T(8,128)(2,1)} %refs_5_.7), channel_id=1, source_target_pairs={{0,1},{1,0},{2,3},{3,2},{4,5},{5,4},{6,7},{7,6},{8,9},{9,8},{10,11... | collective-permute-start | bytes 9437192 | tf_op jit(solution)/shard_map/T_wu/ppermute | solution.py:251
  18.7 9.6 %collective-permute-start.7 = (bf16[64,2176]{1,0:T(8,128)(2,1)}, bf16[64,2176]{1,0:T(8,128)(2,1)S(1)}, u32[]{:S(2)}, u32[]{:S(2)}) collective-permute-start(bf16[64,2176]{1,0:T(8,128)(2,1)} %get-tuple-element.60.refs_0_), channel_id=1, source_target_pairs={{0,12},{1,13},{2,14},{3,15},{4,0},{5,1},{6,2},{7,3},{8,4},{9,5},{1... | collective-permute-start | bytes 835592 | tf_op jit(solution)/shard_map/T_b_z3/ppermute | solution.py:255
  20.4 9.0 %collective-permute-start.5 = (bf16[64,2176]{1,0:T(8,128)(2,1)}, bf16[64,2176]{1,0:T(8,128)(2,1)}, u32[]{:S(2)}, u32[]{:S(2)}) collective-permute-start(bf16[64,2176]{1,0:T(8,128)(2,1)} %collective-permute-done.refs_2_), channel_id=1, source_target_pairs={{0,2},{1,3},{2,0},{3,1},{4,6},{5,7},{6,4},{7,5},{8,10},{9,11},{10,... | collective-permute-start | bytes 835592 | tf_op jit(solution)/shard_map/T_b_x1/ppermute | solution.py:251
  21.0 13.1 %collective-permute-start.6 = (bf16[64,2176]{1,0:T(8,128)(2,1)}, bf16[64,2176]{1,0:T(8,128)(2,1)}, u32[]{:S(2)}, u32[]{:S(2)}) collective-permute-start(bf16[64,2176]{1,0:T(8,128)(2,1)} %collective-permute-done.refs_2_), channel_id=1, source_target_pairs={{0,4},{1,5},{2,6},{3,7},{4,8},{5,9},{6,10},{7,11},{8,12},{9,13},{1... | collective-permute-start | bytes 835592 | tf_op jit(solution)/shard_map/T_b_z2/ppermute | solution.py:255
  28.3 24.5 %copy-start.13 = (bf16[64,2176]{1,0:T(8,128)(2,1)}, bf16[64,2176]{1,0:T(8,128)(2,1)S(1)}, u32[]{:S(2)}) copy-start(bf16[64,2176]{1,0:T(8,128)(2,1)S(1)} %collective-permute-done.7.refs_2_) | copy-start | bytes 835588
  34.1 20.9 %copy-start.5 = (bf16[64,2176]{1,0:T(8,128)(2,1)S(1)}, bf16[64,2176]{1,0:T(8,128)(2,1)}, u32[]{:S(2)}) copy-start(bf16[64,2176]{1,0:T(8,128)(2,1)} %get-tuple-element.70.refs_0_) | copy-start | bytes 835588
  34.1 18.7 %collective-permute-start.10 = (bf16[64,2176]{1,0:T(8,128)(2,1)}, bf16[64,2176]{1,0:T(8,128)(2,1)S(1)}, u32[]{:S(2)}, u32[]{:S(2)}) collective-permute-start(bf16[64,2176]{1,0:T(8,128)(2,1)} %get-tuple-element.70.refs_0_), channel_id=1, source_target_pairs={{0,4},{1,5},{2,6},{3,7},{4,8},{5,9},{6,10},{7,11},{8,12},{9,13},{1... | collective-permute-start | bytes 835592 | tf_op jit(solution)/shard_map/T_f_z1/ppermute | solution.py:255
  35.8 17.1 %collective-permute-start.13 = (bf16[64,2176]{1,0:T(8,128)(2,1)}, bf16[64,2176]{1,0:T(8,128)(2,1)S(1)}, u32[]{:S(2)}, u32[]{:S(2)}) collective-permute-start(bf16[64,2176]{1,0:T(8,128)(2,1)} %get-tuple-element.70.refs_0_), channel_id=1, source_target_pairs={{0,2},{1,3},{2,0},{3,1},{4,6},{5,7},{6,4},{7,5},{8,10},{9,11},{10,... | collective-permute-start | bytes 835592 | tf_op jit(solution)/shard_map/T_f_x0/ppermute | solution.py:251
  36.3 16.5 %collective-permute-start.12 = (bf16[64,2176]{1,0:T(8,128)(2,1)}, bf16[64,2176]{1,0:T(8,128)(2,1)S(1)}, u32[]{:S(2)}, u32[]{:S(2)}) collective-permute-start(bf16[64,2176]{1,0:T(8,128)(2,1)} %copy-done.14), channel_id=1, source_target_pairs={{0,12},{1,13},{2,14},{3,15},{4,0},{5,1},{6,2},{7,3},{8,4},{9,5},{1... | collective-permute-start | bytes 835592 | tf_op jit(solution)/shard_map/T_b_w3/ppermute | solution.py:255
  38.5 14.3 %collective-permute-start.11 = (bf16[64,2176]{1,0:T(8,128)(2,1)}, bf16[64,2176]{1,0:T(8,128)(2,1)S(1)}, u32[]{:S(2)}, u32[]{:S(2)}) collective-permute-start(bf16[64,2176]{1,0:T(8,128)(2,1)} %collective-permute-done.6.refs_0_), channel_id=1, source_target_pairs={{0,2},{1,3},{2,0},{3,1},{4,6},{5,7},{6,4},{7,5},{8,10},{9,11},{10,... | collective-permute-start | bytes 835592 | tf_op jit(solution)/shard_map/T_b_x2/ppermute | solution.py:251
  40.0 12.8 %collective-permute-start.14 = (bf16[64,2048]{1,0:T(8,128)(2,1)}, bf16[64,2048]{1,0:T(8,128)(2,1)S(1)}, u32[]{:S(2)}, u32[]{:S(2)}) collective-permute-start(bf16[64,2048]{1,0:T(8,128)(2,1)} %bitcast.37), channel_id=1, source_target_pairs={{0,16},{1,17},{2,18},{3,19},{4,20},{5,21},{6,22},{7,23},{8,24},{9,... | collective-permute-start | bytes 786440 | tf_op jit(solution)/shard_map/T_y1/ppermute | solution.py:266
  52.8 6.0 %copy-start.15 = (bf16[64,2176]{1,0:T(8,128)(2,1)}, bf16[64,2176]{1,0:T(8,128)(2,1)S(1)}, u32[]{:S(2)}) copy-start(bf16[64,2176]{1,0:T(8,128)(2,1)S(1)} %collective-permute-done.12.refs_3_) | copy-start | bytes 835588
  52.8 6.0 %copy-start.16 = (bf16[64,2176]{1,0:T(8,128)(2,1)}, bf16[64,2176]{1,0:T(8,128)(2,1)S(1)}, u32[]{:S(2)}) copy-start(bf16[64,2176]{1,0:T(8,128)(2,1)S(1)} %collective-permute-done.11.refs_1_) | copy-start | bytes 835588
  52.8 17.2 %copy-start.7 = (bf16[64,2176]{1,0:T(8,128)(2,1)}, bf16[64,2176]{1,0:T(8,128)(2,1)S(1)}, u32[]{:S(2)}) copy-start(bf16[64,2176]{1,0:T(8,128)(2,1)S(1)} %collective-permute-done.10.refs_2_) | copy-start | bytes 835588
  52.8 20.2 %copy-start.6 = (bf16[64,2176]{1,0:T(8,128)(2,1)}, bf16[64,2176]{1,0:T(8,128)(2,1)S(1)}, u32[]{:S(2)}) copy-start(bf16[64,2176]{1,0:T(8,128)(2,1)S(1)} %collective-permute-done.13.refs_1_) | copy-start | bytes 835588
  52.8 18.9 %copy-start.19 = (bf16[64,2048]{1,0:T(8,128)(2,1)S(1)}, bf16[64,2048]{1,0:T(8,128)(2,1)}, u32[]{:S(2)}) copy-start(bf16[64,2048]{1,0:T(8,128)(2,1)} %get-tuple-element.94) | copy-start | bytes 786436
  52.8 18.9 %copy-start.20 = (bf16[64,2048]{1,0:T(8,128)(2,1)S(1)}, bf16[64,2048]{1,0:T(8,128)(2,1)}, u32[]{:S(2)}) copy-start(bf16[64,2048]{1,0:T(8,128)(2,1)} %get-tuple-element.79) | copy-start | bytes 786436
  52.9 18.2 %collective-permute-start.18 = (bf16[128,2048]{1,0:T(8,128)(2,1)}, bf16[128,2048]{1,0:T(8,128)(2,1)S(1)}, u32[]{:S(2)}, u32[]{:S(2)}) collective-permute-start(bf16[128,2048]{1,0:T(8,128)(2,1)} %get-tuple-element.71), channel_id=1, source_target_pairs={{0,2},{1,3},{2,0},{3,1},{4,6},{5,7},{6,4},{7,5},{8,10},{9,11},{10,... | collective-permute-start | bytes 1572872 | tf_op jit(solution)/shard_map/T_b_s0/ppermute | solution.py:251
  53.5 17.6 %collective-permute-start.15 = (bf16[64,2176]{1,0:T(8,128)(2,1)S(1)}, bf16[64,2176]{1,0:T(8,128)(2,1)S(1)}, u32[]{:S(2)}, u32[]{:S(2)}) collective-permute-start(bf16[64,2176]{1,0:T(8,128)(2,1)S(1)} %collective-permute-done.10.refs_2_), channel_id=1, source_target_pairs={{0,2},{1,3},{2,0},{3,1},{4,6},{5,7},{6,4},{7,5},{8,10},{9,11},{10,... | collective-permute-start | bytes 835592 | tf_op jit(solution)/shard_map/T_f_x1/ppermute | solution.py:251
  54.9 16.1 %collective-permute-start.16 = (bf16[64,2176]{1,0:T(8,128)(2,1)S(1)}, bf16[64,2176]{1,0:T(8,128)(2,1)S(1)}, u32[]{:S(2)}, u32[]{:S(2)}) collective-permute-start(bf16[64,2176]{1,0:T(8,128)(2,1)S(1)} %collective-permute-done.10.refs_2_), channel_id=1, source_target_pairs={{0,4},{1,5},{2,6},{3,7},{4,8},{5,9},{6,10},{7,11},{8,12},{9,13},{1... | collective-permute-start | bytes 835592 | tf_op jit(solution)/shard_map/T_f_z2/ppermute | solution.py:255
  55.0 15.1 %collective-permute-start.17 = (bf16[64,2176]{1,0:T(8,128)(2,1)S(1)}, bf16[64,2176]{1,0:T(8,128)(2,1)S(1)}, u32[]{:S(2)}, u32[]{:S(2)}) collective-permute-start(bf16[64,2176]{1,0:T(8,128)(2,1)S(1)} %copy-done.5), channel_id=1, source_target_pairs={{0,12},{1,13},{2,14},{3,15},{4,0},{5,1},{6,2},{7,3},{8,4},{9,5},{1... | collective-permute-start | bytes 835592 | tf_op jit(solution)/shard_map/T_f_z3/ppermute | solution.py:255
  70.0 15.6 %copy-start.9 = (bf16[64,2176]{1,0:T(8,128)(2,1)}, bf16[64,2176]{1,0:T(8,128)(2,1)S(1)}, u32[]{:S(2)}) copy-start(bf16[64,2176]{1,0:T(8,128)(2,1)S(1)} %collective-permute-done.17.refs_2_) | copy-start | bytes 835588
  71.1 3.7 %copy-start.10 = (bf16[64,2176]{1,0:T(8,128)(2,1)}, bf16[64,2176]{1,0:T(8,128)(2,1)S(1)}, u32[]{:S(2)}) copy-start(bf16[64,2176]{1,0:T(8,128)(2,1)S(1)} %collective-permute-done.15.refs_3_) | copy-start | bytes 835588
  71.1 14.5 %copy-start.8 = (bf16[64,2176]{1,0:T(8,128)(2,1)}, bf16[64,2176]{1,0:T(8,128)(2,1)S(1)}, u32[]{:S(2)}) copy-start(bf16[64,2176]{1,0:T(8,128)(2,1)S(1)} %collective-permute-done.16.refs_0_) | copy-start | bytes 835588
  71.1 18.1 %collective-permute-start.22 = (bf16[128,2048]{1,0:T(8,128)(2,1)}, bf16[128,2048]{1,0:T(8,128)(2,1)S(1)}, u32[]{:S(2)}, u32[]{:S(2)}) collective-permute-start(bf16[128,2048]{1,0:T(8,128)(2,1)} %get-tuple-element.81), channel_id=1, source_target_pairs={{0,2},{1,3},{2,0},{3,1},{4,6},{5,7},{6,4},{7,5},{8,10},{9,11},{10,... | collective-permute-start | bytes 1572872 | tf_op jit(solution)/shard_map/T_b_s2/ppermute | solution.py:251
  71.8 13.8 %collective-permute-start.21 = (bf16[64,2048]{1,0:T(8,128)(2,1)S(1)}, bf16[64,2048]{1,0:T(8,128)(2,1)S(1)}, u32[]{:S(2)}, u32[]{:S(2)}) collective-permute-start(bf16[64,2048]{1,0:T(8,128)(2,1)S(1)} %get-tuple-element.80), channel_id=1, source_target_pairs={{0,12},{1,13},{2,14},{3,15},{4,0},{5,1},{6,2},{7,3},{8,4},{9,5},{1... | collective-permute-start | bytes 786440 | tf_op jit(solution)/shard_map/T_b_r1/ppermute | solution.py:255
  73.1 12.6 %collective-permute-start.20 = (bf16[64,2176]{1,0:T(8,128)(2,1)S(1)}, bf16[64,2176]{1,0:T(8,128)(2,1)S(1)}, u32[]{:S(2)}, u32[]{:S(2)}) collective-permute-start(bf16[64,2176]{1,0:T(8,128)(2,1)S(1)} %collective-permute-done.13.refs_1_), channel_id=1, source_target_pairs={{0,12},{1,13},{2,14},{3,15},{4,0},{5,1},{6,2},{7,3},{8,4},{9,5},{1... | collective-permute-start | bytes 835592 | tf_op jit(solution)/shard_map/T_f_w3/ppermute | solution.py:255
  74.5 14.7 %collective-permute-start.19 = (bf16[64,2176]{1,0:T(8,128)(2,1)S(1)}, bf16[64,2176]{1,0:T(8,128)(2,1)S(1)}, u32[]{:S(2)}, u32[]{:S(2)}) collective-permute-start(bf16[64,2176]{1,0:T(8,128)(2,1)S(1)} %collective-permute-done.16.refs_0_), channel_id=1, source_target_pairs={{0,2},{1,3},{2,0},{3,1},{4,6},{5,7},{6,4},{7,5},{8,10},{9,11},{10,... | collective-permute-start | bytes 835592 | tf_op jit(solution)/shard_map/T_f_x2/ppermute | solution.py:251
  74.8 15.0 %copy-start.23 = (bf16[64,2048]{1,0:T(8,128)(2,1)S(1)}, bf16[64,2048]{1,0:T(8,128)(2,1)}, u32[]{:S(2)}) copy-start(bf16[64,2048]{1,0:T(8,128)(2,1)} %get-tuple-element.84) | copy-start | bytes 786436
  74.8 15.0 %copy-start.24 = (bf16[64,2048]{1,0:T(8,128)(2,1)S(1)}, bf16[64,2048]{1,0:T(8,128)(2,1)}, u32[]{:S(2)}) copy-start(bf16[64,2048]{1,0:T(8,128)(2,1)} %get-tuple-element.86) | copy-start | bytes 786436
  85.7 6.3 %copy-start.11 = (bf16[64,2176]{1,0:T(8,128)(2,1)}, bf16[64,2176]{1,0:T(8,128)(2,1)S(1)}, u32[]{:S(2)}) copy-start(bf16[64,2176]{1,0:T(8,128)(2,1)S(1)} %collective-permute-done.20.refs_3_) | copy-start | bytes 835588
  89.2 2.7 %copy-start.12 = (bf16[64,2176]{1,0:T(8,128)(2,1)}, bf16[64,2176]{1,0:T(8,128)(2,1)S(1)}, u32[]{:S(2)}) copy-start(bf16[64,2176]{1,0:T(8,128)(2,1)S(1)} %collective-permute-done.19.refs_1_) | copy-start | bytes 835588
  89.2 16.6 %collective-permute-start.23 = (bf16[128,2048]{1,0:T(8,128)(2,1)}, bf16[128,2048]{1,0:T(8,128)(2,1)S(1)}, u32[]{:S(2)}, u32[]{:S(2)}) collective-permute-start(bf16[128,2048]{1,0:T(8,128)(2,1)} %get-tuple-element.82), channel_id=1, source_target_pairs={{0,2},{1,3},{2,0},{3,1},{4,6},{5,7},{6,4},{7,5},{8,10},{9,11},{10,... | collective-permute-start | bytes 1572872 | tf_op jit(solution)/shard_map/T_f_s0/ppermute | solution.py:251
  89.9 12.7 %collective-permute-start.25 = (bf16[64,2048]{1,0:T(8,128)(2,1)S(1)}, bf16[64,2048]{1,0:T(8,128)(2,1)S(1)}, u32[]{:S(2)}, u32[]{:S(2)}) collective-permute-start(bf16[64,2048]{1,0:T(8,128)(2,1)S(1)} %get-tuple-element.87), channel_id=1, source_target_pairs={{0,4},{1,5},{2,6},{3,7},{4,8},{5,9},{6,10},{7,11},{8,12},{9,13},{1... | collective-permute-start | bytes 786440 | tf_op jit(solution)/shard_map/T_b_r3/ppermute | solution.py:255
  90.2 17.2 %copy-start.18 = (bf16[64,2048]{1,0:T(8,128)(2,1)S(1)}, bf16[64,2048]{1,0:T(8,128)(2,1)}, u32[]{:S(2)}) copy-start(bf16[64,2048]{1,0:T(8,128)(2,1)} %get-tuple-element.83) | copy-start | bytes 786436
  90.2 18.1 %copy-start.4 = (bf16[1,64,2048]{2,1,0:T(8,128)(2,1)S(1)}, bf16[1,64,2048]{2,1,0:T(8,128)(2,1)}, u32[]{:S(2)}) copy-start(bf16[1,64,2048]{2,1,0:T(8,128)(2,1)} %param.20) | copy-start | bytes 786436
  90.2 18.4 %copy-start.3 = (bf16[1,64,2048]{2,1,0:T(8,128)(2,1)S(1)}, bf16[1,64,2048]{2,1,0:T(8,128)(2,1)}, u32[]{:S(2)}) copy-start(bf16[1,64,2048]{2,1,0:T(8,128)(2,1)} %param.21) | copy-start | bytes 786436
  90.2 15.6 %collective-permute-start.24 = (bf16[64,2048]{1,0:T(8,128)(2,1)S(1)}, bf16[64,2048]{1,0:T(8,128)(2,1)S(1)}, u32[]{:S(2)}, u32[]{:S(2)}) collective-permute-start(bf16[64,2048]{1,0:T(8,128)(2,1)S(1)} %get-tuple-element.85), channel_id=1, source_target_pairs={{0,8},{1,9},{2,10},{3,11},{4,12},{5,13},{6,14},{7,15},{8,0},{9,1},... | collective-permute-start | bytes 786440 | tf_op jit(solution)/shard_map/T_b_r2/ppermute | solution.py:255
  102.6 10.9 %copy-start.21 = (bf16[64,2048]{1,0:T(8,128)(2,1)S(1)}, bf16[64,2048]{1,0:T(8,128)(2,1)}, u32[]{:S(2)}) copy-start(bf16[64,2048]{1,0:T(8,128)(2,1)} %get-tuple-element.92) | copy-start | bytes 786436
  102.6 12.9 %copy-start.25 = (bf16[64,2048]{1,0:T(8,128)(2,1)S(1)}, bf16[64,2048]{1,0:T(8,128)(2,1)}, u32[]{:S(2)}) copy-start(bf16[64,2048]{1,0:T(8,128)(2,1)} %get-tuple-element.102) | copy-start | bytes 786436
  102.6 14.0 %copy-start.22 = (bf16[64,2048]{1,0:T(8,128)(2,1)S(1)}, bf16[64,2048]{1,0:T(8,128)(2,1)}, u32[]{:S(2)}) copy-start(bf16[64,2048]{1,0:T(8,128)(2,1)} %get-tuple-element.75) | copy-start | bytes 786436
  105.9 7.6 %collective-permute-start.28 = (bf16[64,2048]{1,0:T(8,128)(2,1)}, bf16[64,2048]{1,0:T(8,128)(2,1)S(1)}, u32[]{:S(2)}, u32[]{:S(2)}) collective-permute-start(bf16[64,2048]{1,0:T(8,128)(2,1)} %get-tuple-element.93), channel_id=1, source_target_pairs={{0,2},{1,3},{2,0},{3,1},{4,6},{5,7},{6,4},{7,5},{8,10},{9,11},{10,... | collective-permute-start | bytes 786440 | tf_op jit(solution)/shard_map/T_f_s2/ppermute | solution.py:251
  107.4 15.2 %copy-start.17 = (bf16[64,2048]{1,0:T(8,128)(2,1)S(1)}, bf16[64,2048]{1,0:T(8,128)(2,1)}, u32[]{:S(2)}) copy-start(bf16[64,2048]{1,0:T(8,128)(2,1)} %get-tuple-element.101) | copy-start | bytes 786436
  107.4 9.2 %collective-permute-start.26 = (bf16[64,2048]{1,0:T(8,128)(2,1)S(1)}, bf16[64,2048]{1,0:T(8,128)(2,1)S(1)}, u32[]{:S(2)}, u32[]{:S(2)}) collective-permute-start(bf16[64,2048]{1,0:T(8,128)(2,1)S(1)} %add_convert_fusion.6), channel_id=1, source_target_pairs={{0,12},{1,13},{2,14},{3,15},{4,0},{5,1},{6,2},{7,3},{8,4},{9,5},{1... | collective-permute-start | bytes 786440 | tf_op jit(solution)/shard_map/T_f_near/ppermute | solution.py:255
  108.9 13.8 %collective-permute-start.32 = (bf16[64,2048]{1,0:T(8,128)(2,1)S(1)}, bf16[64,2048]{1,0:T(8,128)(2,1)S(1)}, u32[]{:S(2)}, u32[]{:S(2)}) collective-permute-start(bf16[64,2048]{1,0:T(8,128)(2,1)S(1)} %fusion.5), channel_id=1, source_target_pairs={{0,16},{1,17},{2,18},{3,19},{4,20},{5,21},{6,22},{7,23},{8,24},{9,... | collective-permute-start | bytes 786440 | tf_op jit(solution)/shard_map/T_b_y/ppermute | solution.py:266
  113.5 19.0 %collective-permute-start.29 = (bf16[64,2048]{1,0:T(8,128)(2,1)S(1)}, bf16[64,2048]{1,0:T(8,128)(2,1)S(1)}, u32[]{:S(2)}, u32[]{:S(2)}) collective-permute-start(bf16[64,2048]{1,0:T(8,128)(2,1)S(1)} %add_convert_fusion.2), channel_id=1, source_target_pairs={{0,24},{1,25},{2,26},{3,27},{4,28},{5,29},{6,30},{7,31},{8,16},{9,... | collective-permute-start | bytes 786440 | tf_op jit(solution)/shard_map/T_f_r2/ppermute | solution.py:266
  115.5 7.1 %collective-permute-start.30 = (bf16[64,2048]{1,0:T(8,128)(2,1)S(1)}, bf16[64,2048]{1,0:T(8,128)(2,1)S(1)}, u32[]{:S(2)}, u32[]{:S(2)}) collective-permute-start(bf16[64,2048]{1,0:T(8,128)(2,1)S(1)} %copy-done.25), channel_id=1, source_target_pairs={{0,2},{1,3},{2,0},{3,1},{4,6},{5,7},{6,4},{7,5},{8,10},{9,11},{10,... | collective-permute-start | bytes 786440 | tf_op jit(solution)/shard_map/T_f_s3/ppermute | solution.py:251
  116.7 18.0 %collective-permute-start.27 = (bf16[64,2048]{1,0:T(8,128)(2,1)S(1)}, bf16[64,2048]{1,0:T(8,128)(2,1)S(1)}, u32[]{:S(2)}, u32[]{:S(2)}) collective-permute-start(bf16[64,2048]{1,0:T(8,128)(2,1)S(1)} %add_convert_fusion.3), channel_id=1, source_target_pairs={{0,16},{1,17},{2,18},{3,19},{4,20},{5,21},{6,22},{7,23},{8,24},{9,... | collective-permute-start | bytes 786440 | tf_op jit(solution)/shard_map/T_f_joined/ppermute | solution.py:266
  122.6 12.1 %collective-permute-start.31 = (bf16[64,2048]{1,0:T(8,128)(2,1)S(1)}, bf16[64,2048]{1,0:T(8,128)(2,1)S(1)}, u32[]{:S(2)}, u32[]{:S(2)}) collective-permute-start(bf16[64,2048]{1,0:T(8,128)(2,1)S(1)} %add_convert_fusion.1), channel_id=1, source_target_pairs={{0,20},{1,21},{2,22},{3,23},{4,24},{5,25},{6,26},{7,27},{8,28},{9,... | collective-permute-start | bytes 786440 | tf_op jit(solution)/shard_map/T_f_r3/ppermute | solution.py:266

commit v5 on v4

--- a/solution.py
+++ b/solution.py
@@ -225,6 +225,16 @@
     )(table, *operands)
 
 
+def place_kernel(arrived, out):
+    out[...] = arrived[...]
+
+
+def placed_early(arrived):
+    return pl.pallas_call(
+        place_kernel, out_shape=jax.ShapeDtypeStruct(arrived.shape, arrived.dtype), name="place"
+    )(arrived)
+
+
 def shards(
     x_forward,
     norm_gain,
@@ -433,6 +443,8 @@
         final = chip_sum(False, k, own[k], arrived)
         send_sums(False, {k: after(final, ahead)})
         before, ahead = [arrived], joined
+    next_backward = placed_early(next_backward)
+    came[False] = [after(value, next_backward) for value in came[False]]
     next_forward = (summed(came[False]) + residual.astype(f32)).astype(bf16)
     return (next_forward[None], next_backward[None])
 

time: 137 us -> 139 us (1.015)
  Pallas kernels: 46 us -> 47.7 us
  starting transfers between devices: 36.3 us -> 37.7 us
    ppermute x5, waiting for transfers between devices: 12 us -> 9.94 us  [relay(): return lax.ppermute(value, ('section', 'expert'), pairs)]
    ppermute x12, waiting for transfers between devices: 17.7 us -> 19.8 us  [shift(): lax.ppermute(value, 'expert', [(i, (i + 4 * steps) % experts) for i in ra...]
    pallas_call x0 -> x1, Pallas kernels: none -> 1.67 us  [placed_early(): pl.pallas_call(place_kernel, out_shape=jax.ShapeDtypeStruct(arrived.shape...]
  transfers between devices with their start and end apart: 33 -> 33, of which waited for: 12 -> 12; matrix products, arithmetic and copies ran while one was open for 1% -> 1% of each run, Pallas kernels for 32% -> 33%
where the time goes in v5:
time: 139 us; the launch traced here: 138 us
  Pallas kernels  47.7 us (34%)
  waiting for transfers between devices  47.1 us (34%)
  starting transfers between devices  37.7 us (27%)
  other arithmetic  2.57 us (2%)
  local copies, waits for them, and re-layouts  2.37 us (2%)
    pallas_call x4, Pallas kernels, run_experts(): pl.pallas_call(functools.partial(experts_kernel, backward, experts, token...  43.9 us
    ppermute x12, waiting for transfers between devices, shift(): lax.ppermute(value, 'expert', [(i, (i + 4 * steps) % experts) for i in ra...  19.8 us
    ppermute x12, starting transfers between devices, shift(): lax.ppermute(value, 'expert', [(i, (i + 4 * steps) % experts) for i in ra...  17.8 us
    ppermute x16, waiting for transfers between devices, swap(): return lax.ppermute(value, 'expert', [(i, i ^ bit) for i in range(experts)])  17.4 us
    ppermute x16, starting transfers between devices, swap(): return lax.ppermute(value, 'expert', [(i, i ^ bit) for i in range(experts)])  12.5 us
    ppermute x5, waiting for transfers between devices, relay(): return lax.ppermute(value, ('section', 'expert'), pairs)  9.94 us
    ppermute x5, starting transfers between devices, relay(): return lax.ppermute(value, ('section', 'expert'), pairs)  7.37 us
  transfers between devices with their start and end apart: 33, of which 12 were waited for; matrix products, arithmetic and copies ran while one was open for 1% of the time, Pallas kernels for 33%

profile of v5, /device:TPU:0, one launch (start us, length us, event | category | flops | bytes accessed | tf_op | source)
XLA Modules:
  0.0 138.5 jit_solution(15724624822308740705)
XLA Ops:
  0.6 2.1 %pack.1 = (bf16[64,2176]{1,0:T(8,128)(2,1)}, bf16[64,2176]{1,0:T(8,128)(2,1)}) custom-call(bf16[64,2048]{1,0:T(8,128)(2,1)} %bitcast.35, bf16[64,2048]{1,0:T(8,128)(2,1)} %bitcast.36, f32[1,2048]{1,0:T(1,128)} %refs_14_.3, s32[8,64]{1,0:T(8,128)} %bitcast.39, f32[8,64]{1,0:T(8,128)} %bitcast.40, s32[8,64]{1,0:T(8,128)} %bitcast.41, f32[8,64]{1,0:T(8,128)} %bitcast.42), custom_call_target="tpu_custom_call" | custom-call | tf_op jit(solution)/shard_map/pack/pallas_call | solution.py:55
  2.7 0.5 collective-permute-start.2
  3.2 0.1 collective-permute-start.3
  3.2 0.5 collective-permute-start.4
  3.7 2.5 %collective-permute-start.1 = (bf16[64,2176]{1,0:T(8,128)(2,1)}, bf16[64,2176]{1,0:T(8,128)(2,1)S(1)}, u32[]{:S(2)}, u32[]{:S(2)}) collective-permute-start(bf16[64,2176]{1,0:T(8,128)(2,1)} %get-tuple-element.63.refs_0_), channel_id=1, source_target_pairs={{0,2},{1,3},{2,0},{3,1},{4,6},{5,7},{6,4},{7,5},{8,10},{9,11},{10,... | collective-permute-start | bytes 835592 | tf_op jit(solution)/shard_map/T_b_x0/ppermute | solution.py:261
  6.2 1.6 %collective-permute-start = (bf16[64,2176]{1,0:T(8,128)(2,1)}, bf16[64,2176]{1,0:T(8,128)(2,1)}, u32[]{:S(2)}, u32[]{:S(2)}) collective-permute-start(bf16[64,2176]{1,0:T(8,128)(2,1)} %get-tuple-element.63.refs_0_), channel_id=1, source_target_pairs={{0,4},{1,5},{2,6},{3,7},{4,8},{5,9},{6,10},{7,11},{8,12},{9,13},{1... | collective-permute-start | bytes 835592 | tf_op jit(solution)/shard_map/T_b_z1/ppermute | solution.py:265
  7.7 6.0 %collective-permute-done.1.refs_1_ = bf16[64,2176]{1,0:T(8,128)(2,1)S(1)} collective-permute-done((bf16[64,2176]{1,0:T(8,128)(2,1)}, bf16[64,2176]{1,0:T(8,128)(2,1)S(1)}, u32[]{:S(2)}, u32[]{:S(2)}) %collective-permute-start.1) | collective-permute-done | bytes 278560 | tf_op jit(solution)/shard_map/T_b_x0/ppermute | solution.py:261
  13.7 3.5 %collective-permute-done.refs_2_ = bf16[64,2176]{1,0:T(8,128)(2,1)} collective-permute-done((bf16[64,2176]{1,0:T(8,128)(2,1)}, bf16[64,2176]{1,0:T(8,128)(2,1)}, u32[]{:S(2)}, u32[]{:S(2)}) %collective-permute-start) | collective-permute-done | bytes 278560 | tf_op jit(solution)/shard_map/T_b_z1/ppermute | solution.py:265
  17.2 1.0 copy-done.1
  18.2 0.4 copy-done.2
  18.6 0.1 collective-permute-start.8
  18.7 1.7 %collective-permute-start.7 = (bf16[64,2176]{1,0:T(8,128)(2,1)}, bf16[64,2176]{1,0:T(8,128)(2,1)S(1)}, u32[]{:S(2)}, u32[]{:S(2)}) collective-permute-start(bf16[64,2176]{1,0:T(8,128)(2,1)} %get-tuple-element.63.refs_0_), channel_id=1, source_target_pairs={{0,12},{1,13},{2,14},{3,15},{4,0},{5,1},{6,2},{7,3},{8,4},{9,5},{1... | collective-permute-start | bytes 835592 | tf_op jit(solution)/shard_map/T_b_z3/ppermute | solution.py:265
  20.4 0.5 collective-permute-start.5
  21.0 0.3 collective-permute-start.6
  21.3 0.1 stack.59
  21.4 0.1 stack.53
  21.4 0.6 pad_add_fusion.table
  22.0 6.2 %collective-permute-done.7.refs_2_ = bf16[64,2176]{1,0:T(8,128)(2,1)S(1)} collective-permute-done((bf16[64,2176]{1,0:T(8,128)(2,1)}, bf16[64,2176]{1,0:T(8,128)(2,1)S(1)}, u32[]{:S(2)}, u32[]{:S(2)}) %collective-permute-start.7) | collective-permute-done | bytes 278560 | tf_op jit(solution)/shard_map/T_b_z3/ppermute | solution.py:265
  28.3 1.1 collective-permute-done.5.refs_3_
  29.4 4.7 %collective-permute-done.6.refs_0_ = bf16[64,2176]{1,0:T(8,128)(2,1)} collective-permute-done((bf16[64,2176]{1,0:T(8,128)(2,1)}, bf16[64,2176]{1,0:T(8,128)(2,1)}, u32[]{:S(2)}, u32[]{:S(2)}) %collective-permute-start.6) | collective-permute-done | bytes 278560 | tf_op jit(solution)/shard_map/T_b_z2/ppermute | solution.py:265
  34.1 1.7 %collective-permute-start.10 = (bf16[64,2176]{1,0:T(8,128)(2,1)}, bf16[64,2176]{1,0:T(8,128)(2,1)S(1)}, u32[]{:S(2)}, u32[]{:S(2)}) collective-permute-start(bf16[64,2176]{1,0:T(8,128)(2,1)} %get-tuple-element.73.refs_0_), channel_id=1, source_target_pairs={{0,4},{1,5},{2,6},{3,7},{4,8},{5,9},{6,10},{7,11},{8,12},{9,13},{1... | collective-permute-start | bytes 835592 | tf_op jit(solution)/shard_map/T_f_z1/ppermute | solution.py:265
  35.7 0.5 collective-permute-start.13
  36.3 2.2 %collective-permute-start.12 = (bf16[64,2176]{1,0:T(8,128)(2,1)}, bf16[64,2176]{1,0:T(8,128)(2,1)S(1)}, u32[]{:S(2)}, u32[]{:S(2)}) collective-permute-start(bf16[64,2176]{1,0:T(8,128)(2,1)} %copy-done.14), channel_id=1, source_target_pairs={{0,12},{1,13},{2,14},{3,15},{4,0},{5,1},{6,2},{7,3},{8,4},{9,5},{1... | collective-permute-start | bytes 835592 | tf_op jit(solution)/shard_map/T_b_w3/ppermute | solution.py:265
  38.5 1.5 %collective-permute-start.11 = (bf16[64,2176]{1,0:T(8,128)(2,1)}, bf16[64,2176]{1,0:T(8,128)(2,1)S(1)}, u32[]{:S(2)}, u32[]{:S(2)}) collective-permute-start(bf16[64,2176]{1,0:T(8,128)(2,1)} %collective-permute-done.6.refs_0_), channel_id=1, source_target_pairs={{0,2},{1,3},{2,0},{3,1},{4,6},{5,7},{6,4},{7,5},{8,10},{9,11},{10,... | collective-permute-start | bytes 835592 | tf_op jit(solution)/shard_map/T_b_x2/ppermute | solution.py:261
  40.0 1.5 %collective-permute-start.14 = (bf16[64,2048]{1,0:T(8,128)(2,1)}, bf16[64,2048]{1,0:T(8,128)(2,1)S(1)}, u32[]{:S(2)}, u32[]{:S(2)}) collective-permute-start(bf16[64,2048]{1,0:T(8,128)(2,1)} %bitcast.37), channel_id=1, source_target_pairs={{0,16},{1,17},{2,18},{3,19},{4,20},{5,21},{6,22},{7,23},{8,24},{9,... | collective-permute-start | bytes 786440 | tf_op jit(solution)/shard_map/T_y1/ppermute | solution.py:276
  41.5 11.2 %experts_backward.2 = (bf16[64,2048]{1,0:T(8,128)(2,1)}, bf16[64,2048]{1,0:T(8,128)(2,1)}, bf16[128,2048]{1,0:T(8,128)(2,1)}) custom-call(s32[2,6]{1,0:T(2,128)} %pad_add_fusion.table, bf16[64,2176]{1,0:T(8,128)(2,1)} %get-tuple-element.63.refs_0_, bf16[64,2176]{1,0:T(8,128)(2,1)} %copy-done.14, bf16[64,2176]{1,0:T(8,128)(2,1)} %collective-permute-done.refs_2_, ...), custom_call_target="tpu_custom_call" | custom-call | flops 4831838208 | bytes 18874368 | tf_op jit(solution)/shard_map/experts_backward/pallas_call | solution.py:210
  52.8 0.6 collective-permute-start.18
  53.4 1.5 %collective-permute-start.15 = (bf16[64,2176]{1,0:T(8,128)(2,1)S(1)}, bf16[64,2176]{1,0:T(8,128)(2,1)S(1)}, u32[]{:S(2)}, u32[]{:S(2)}) collective-permute-start(bf16[64,2176]{1,0:T(8,128)(2,1)S(1)} %collective-permute-done.10.refs_2_), channel_id=1, source_target_pairs={{0,2},{1,3},{2,0},{3,1},{4,6},{5,7},{6,4},{7,5},{8,10},{9,11},{10,... | collective-permute-start | bytes 835592 | tf_op jit(solution)/shard_map/T_f_x1/ppermute | solution.py:261
  54.9 3.8 %collective-permute-start.17 = (bf16[64,2176]{1,0:T(8,128)(2,1)S(1)}, bf16[64,2176]{1,0:T(8,128)(2,1)S(1)}, u32[]{:S(2)}, u32[]{:S(2)}) collective-permute-start(bf16[64,2176]{1,0:T(8,128)(2,1)S(1)} %copy-done.5), channel_id=1, source_target_pairs={{0,12},{1,13},{2,14},{3,15},{4,0},{5,1},{6,2},{7,3},{8,4},{9,5},{1... | collective-permute-start | bytes 835592 | tf_op jit(solution)/shard_map/T_f_z3/ppermute | solution.py:265
  58.8 11.2 %experts_backward.3 = (bf16[64,2048]{1,0:T(8,128)(2,1)}, bf16[64,2048]{1,0:T(8,128)(2,1)}, bf16[128,2048]{1,0:T(8,128)(2,1)}) custom-call(s32[2,6]{1,0:T(2,128)} %pad_add_fusion.table, bf16[64,2176]{1,0:T(8,128)(2,1)} %collective-permute-done.6.refs_0_, bf16[64,2176]{1,0:T(8,128)(2,1)} %copy-done.16, bf16[64,2176]{1,0:T(8,128)(2,1)} %copy-done.13, ...), custom_call_target="tpu_custom_call" | custom-call | flops 4831838208 | bytes 18874368 | tf_op jit(solution)/shard_map/experts_backward/pallas_call | solution.py:210
  70.0 1.0 collective-permute-done.15.refs_3_
  71.1 0.6 collective-permute-start.22
  71.7 0.1 convert_add_fusion.1
  71.8 1.2 collective-permute-start.21
  73.0 1.4 %collective-permute-start.20 = (bf16[64,2176]{1,0:T(8,128)(2,1)S(1)}, bf16[64,2176]{1,0:T(8,128)(2,1)S(1)}, u32[]{:S(2)}, u32[]{:S(2)}) collective-permute-start(bf16[64,2176]{1,0:T(8,128)(2,1)S(1)} %collective-permute-done.13.refs_1_), channel_id=1, source_target_pairs={{0,12},{1,13},{2,14},{3,15},{4,0},{5,1},{6,2},{7,3},{8,4},{9,5},{1... | collective-permute-start | bytes 835592 | tf_op jit(solution)/shard_map/T_f_w3/ppermute | solution.py:265
  74.5 0.3 collective-permute-start.19
  74.8 10.9 %experts_forward.2 = (bf16[64,2048]{1,0:T(8,128)(2,1)}, bf16[64,2048]{1,0:T(8,128)(2,1)}, bf16[128,2048]{1,0:T(8,128)(2,1)}) custom-call(s32[2,6]{1,0:T(2,128)} %pad_add_fusion.table, bf16[64,2176]{1,0:T(8,128)(2,1)} %get-tuple-element.73.refs_0_, bf16[64,2176]{1,0:T(8,128)(2,1)} %copy-done.6, bf16[64,2176]{1,0:T(8,128)(2,1)} %copy-done.7, ...), custom_call_target="tpu_custom_call" | custom-call | flops 4831838208 | bytes 18874368 | tf_op jit(solution)/shard_map/experts_forward/pallas_call | solution.py:210
  85.7 3.5 %collective-permute-done.19.refs_1_ = bf16[64,2176]{1,0:T(8,128)(2,1)S(1)} collective-permute-done((bf16[64,2176]{1,0:T(8,128)(2,1)S(1)}, bf16[64,2176]{1,0:T(8,128)(2,1)S(1)}, u32[]{:S(2)}, u32[]{:S(2)}) %collective-permute-start.19) | collective-permute-done | bytes 278560 | tf_op jit(solution)/shard_map/T_f_x2/ppermute | solution.py:261
  89.2 0.5 collective-permute-start.23
  89.7 0.1 add_convert_fusion.4
  89.9 0.3 collective-permute-start.25
  90.2 1.7 %collective-permute-start.24 = (bf16[64,2048]{1,0:T(8,128)(2,1)S(1)}, bf16[64,2048]{1,0:T(8,128)(2,1)S(1)}, u32[]{:S(2)}, u32[]{:S(2)}) collective-permute-start(bf16[64,2048]{1,0:T(8,128)(2,1)S(1)} %get-tuple-element.88), channel_id=1, source_target_pairs={{0,8},{1,9},{2,10},{3,11},{4,12},{5,13},{6,14},{7,15},{8,0},{9,1},... | collective-permute-start | bytes 786440 | tf_op jit(solution)/shard_map/T_b_r2/ppermute | solution.py:265
  91.9 10.7 %experts_forward.3 = (bf16[64,2048]{1,0:T(8,128)(2,1)}, bf16[64,2048]{1,0:T(8,128)(2,1)}, bf16[64,2048]{1,0:T(8,128)(2,1)}, bf16[64,2048]{1,0:T(8,128)(2,1)}) custom-call(s32[2,6]{1,0:T(2,128)} %pad_add_fusion.table, bf16[64,2176]{1,0:T(8,128)(2,1)} %copy-done.8, bf16[64,2176]{1,0:T(8,128)(2,1)} %copy-done.12, bf16[64,2176]{1,0:T(8,128)(2,1)} %copy-done.9, ...), custom_call_target="tpu_custom_call" | custom-call | flops 4831838208 | bytes 18874368 | tf_op jit(solution)/shard_map/experts_forward/pallas_call | solution.py:210
  102.6 3.4 %collective-permute-done.24 = bf16[64,2048]{1,0:T(8,128)(2,1)S(1)} collective-permute-done((bf16[64,2048]{1,0:T(8,128)(2,1)S(1)}, bf16[64,2048]{1,0:T(8,128)(2,1)S(1)}, u32[]{:S(2)}, u32[]{:S(2)}) %collective-permute-start.24) | collective-permute-done | bytes 262176 | tf_op jit(solution)/shard_map/T_b_r2/ppermute | solution.py:265
  106.1 0.1 add_convert_fusion.6
  106.1 1.8 %collective-permute-start.26 = (bf16[64,2048]{1,0:T(8,128)(2,1)S(1)}, bf16[64,2048]{1,0:T(8,128)(2,1)S(1)}, u32[]{:S(2)}, u32[]{:S(2)}) collective-permute-start(bf16[64,2048]{1,0:T(8,128)(2,1)S(1)} %add_convert_fusion.6), channel_id=1, source_target_pairs={{0,12},{1,13},{2,14},{3,15},{4,0},{5,1},{6,2},{7,3},{8,4},{9,5},{1... | collective-permute-start | bytes 786440 | tf_op jit(solution)/shard_map/T_f_near/ppermute | solution.py:265
  108.0 0.3 fusion
  108.3 0.3 fusion.5
  108.6 1.1 collective-permute-start.28
  109.7 1.7 %collective-permute-start.29 = (bf16[64,2048]{1,0:T(8,128)(2,1)S(1)}, bf16[64,2048]{1,0:T(8,128)(2,1)S(1)}, u32[]{:S(2)}, u32[]{:S(2)}) collective-permute-start(bf16[64,2048]{1,0:T(8,128)(2,1)S(1)} %copy-done.29), channel_id=1, source_target_pairs={{0,2},{1,3},{2,0},{3,1},{4,6},{5,7},{6,4},{7,5},{8,10},{9,11},{10,... | collective-permute-start | bytes 786440 | tf_op jit(solution)/shard_map/T_f_s2/ppermute | solution.py:261
  111.4 2.0 %collective-permute-done.26 = bf16[64,2048]{1,0:T(8,128)(2,1)S(1)} collective-permute-done((bf16[64,2048]{1,0:T(8,128)(2,1)S(1)}, bf16[64,2048]{1,0:T(8,128)(2,1)S(1)}, u32[]{:S(2)}, u32[]{:S(2)}) %collective-permute-start.26) | collective-permute-done | bytes 262176 | tf_op jit(solution)/shard_map/T_f_near/ppermute | solution.py:265
  113.3 0.1 add_convert_fusion.3
  113.4 3.0 %collective-permute-start.27 = (bf16[64,2048]{1,0:T(8,128)(2,1)S(1)}, bf16[64,2048]{1,0:T(8,128)(2,1)S(1)}, u32[]{:S(2)}, u32[]{:S(2)}) collective-permute-start(bf16[64,2048]{1,0:T(8,128)(2,1)S(1)} %add_convert_fusion.3), channel_id=1, source_target_pairs={{0,16},{1,17},{2,18},{3,19},{4,20},{5,21},{6,22},{7,23},{8,24},{9,... | collective-permute-start | bytes 786440 | tf_op jit(solution)/shard_map/T_f_joined/ppermute | solution.py:276
  116.4 0.3 collective-permute-done.29
  116.7 1.2 collective-permute-start.31
  117.9 0.1 add_convert_fusion.2
  118.0 0.1 collective-permute-start.30
  118.0 5.5 %collective-permute-done.31 = bf16[64,2048]{1,0:T(8,128)(2,1)S(1)} collective-permute-done((bf16[64,2048]{1,0:T(8,128)(2,1)S(1)}, bf16[64,2048]{1,0:T(8,128)(2,1)S(1)}, u32[]{:S(2)}, u32[]{:S(2)}) %collective-permute-start.31) | collective-permute-done | bytes 262176 | tf_op jit(solution)/shard_map/T_f_s3/ppermute | solution.py:261
  123.6 0.1 add_convert_fusion.1
  123.6 1.7 %collective-permute-start.32 = (bf16[64,2048]{1,0:T(8,128)(2,1)S(1)}, bf16[64,2048]{1,0:T(8,128)(2,1)S(1)}, u32[]{:S(2)}, u32[]{:S(2)}) collective-permute-start(bf16[64,2048]{1,0:T(8,128)(2,1)S(1)} %add_convert_fusion.1), channel_id=1, source_target_pairs={{0,20},{1,21},{2,22},{3,23},{4,24},{5,25},{6,26},{7,27},{8,28},{9,... | collective-permute-start | bytes 786440 | tf_op jit(solution)/shard_map/T_f_r3/ppermute | solution.py:276
  125.3 0.7 copy-done.24
  126.0 1.7 %place.1 = bf16[64,2048]{1,0:T(8,128)(2,1)} custom-call(bf16[64,2048]{1,0:T(8,128)(2,1)} %copy-done.24), custom_call_target="tpu_custom_call" | custom-call | tf_op jit(solution)/shard_map/place/pallas_call | solution.py:233
  127.7 9.9 %collective-permute-done.30 = bf16[64,2048]{1,0:T(8,128)(2,1)S(1)} collective-permute-done((bf16[64,2048]{1,0:T(8,128)(2,1)S(1)}, bf16[64,2048]{1,0:T(8,128)(2,1)S(1)}, u32[]{:S(2)}, u32[]{:S(2)}) %collective-permute-start.30) | collective-permute-done | bytes 262176 | tf_op jit(solution)/shard_map/T_f_r2/ppermute | solution.py:276
  137.6 0.8 fusion.7
  (81 shorter events, 0.2 us)
Async XLA Ops:
  2.7 14.5 %collective-permute-start.2 = (bf16[1,1,2048,768]{3,2,1,0:T(8,128)(2,1)}, bf16[1,1,2048,768]{3,2,1,0:T(8,128)(2,1)S(1)}, u32[]{:S(2)}, u32[]{:S(2)}) collective-permute-start(bf16[1,1,2048,768]{3,2,1,0:T(8,128)(2,1)} %refs_4_.7), channel_id=1, source_target_pairs={{0,1},{1,0},{2,3},{3,2},{4,5},{5,4},{6,7},{7,6},{8,9},{9,8},{10,11... | collective-permute-start | bytes 9437192 | tf_op jit(solution)/shard_map/T_wg/ppermute | solution.py:261
  3.2 14.0 %collective-permute-start.3 = (bf16[1,1,16,48,768]{4,3,2,1,0:T(8,128)(2,1)}, bf16[1,1,16,48,768]{4,3,2,1,0:T(8,128)(2,1)S(1)}, u32[]{:S(2)}, u32[]{:S(2)}) collective-permute-start(bf16[1,1,16,48,768]{4,3,2,1,0:T(8,128)(2,1)} %refs_10_.3), channel_id=1, source_target_pairs={{0,1},{1,0},{2,3},{3,2},{4,5},{5,4},{6,7},{7,6},{8,9},{9,8},{10,11... | collective-permute-start | bytes 3538952 | tf_op jit(solution)/shard_map/T_sg/ppermute | solution.py:261
  3.2 13.9 %collective-permute-start.4 = (bf16[1,1,16,48,768]{4,3,2,1,0:T(8,128)(2,1)}, bf16[1,1,16,48,768]{4,3,2,1,0:T(8,128)(2,1)S(1)}, u32[]{:S(2)}, u32[]{:S(2)}) collective-permute-start(bf16[1,1,16,48,768]{4,3,2,1,0:T(8,128)(2,1)} %refs_11_.3), channel_id=1, source_target_pairs={{0,1},{1,0},{2,3},{3,2},{4,5},{5,4},{6,7},{7,6},{8,9},{9,8},{10,11... | collective-permute-start | bytes 3538952 | tf_op jit(solution)/shard_map/T_su/ppermute | solution.py:261
  3.7 10.0 %collective-permute-start.1 = (bf16[64,2176]{1,0:T(8,128)(2,1)}, bf16[64,2176]{1,0:T(8,128)(2,1)S(1)}, u32[]{:S(2)}, u32[]{:S(2)}) collective-permute-start(bf16[64,2176]{1,0:T(8,128)(2,1)} %get-tuple-element.63.refs_0_), channel_id=1, source_target_pairs={{0,2},{1,3},{2,0},{3,1},{4,6},{5,7},{6,4},{7,5},{8,10},{9,11},{10,... | collective-permute-start | bytes 835592 | tf_op jit(solution)/shard_map/T_b_x0/ppermute | solution.py:261
  6.2 11.0 %collective-permute-start = (bf16[64,2176]{1,0:T(8,128)(2,1)}, bf16[64,2176]{1,0:T(8,128)(2,1)}, u32[]{:S(2)}, u32[]{:S(2)}) collective-permute-start(bf16[64,2176]{1,0:T(8,128)(2,1)} %get-tuple-element.63.refs_0_), channel_id=1, source_target_pairs={{0,4},{1,5},{2,6},{3,7},{4,8},{5,9},{6,10},{7,11},{8,12},{9,13},{1... | collective-permute-start | bytes 835592 | tf_op jit(solution)/shard_map/T_b_z1/ppermute | solution.py:265
  13.7 4.5 %copy-start.14 = (bf16[64,2176]{1,0:T(8,128)(2,1)}, bf16[64,2176]{1,0:T(8,128)(2,1)S(1)}, u32[]{:S(2)}) copy-start(bf16[64,2176]{1,0:T(8,128)(2,1)S(1)} %collective-permute-done.1.refs_1_) | copy-start | bytes 835588
  17.2 1.0 copy-start.1
  17.2 1.4 %copy-start.2 = (bf16[1,1,16,48,768]{4,3,2,1,0:T(8,128)(2,1)}, bf16[1,1,16,48,768]{4,3,2,1,0:T(8,128)(2,1)S(1)}, u32[]{:S(2)}) copy-start(bf16[1,1,16,48,768]{4,3,2,1,0:T(8,128)(2,1)S(1)} %collective-permute-done.4.refs_13_) | copy-start | bytes 3538948
  18.2 23.3 %copy-start = (bf16[1,1,2048,768]{3,2,1,0:T(8,128)(2,1)}, bf16[1,1,2048,768]{3,2,1,0:T(8,128)(2,1)S(1)}, u32[]{:S(2)}) copy-start(bf16[1,1,2048,768]{3,2,1,0:T(8,128)(2,1)S(1)} %collective-permute-done.2.refs_7_) | copy-start | bytes 9437188
  18.2 15.9 %collective-permute-start.9 = (bf16[1,1,768,2048]{3,2,1,0:T(8,128)(2,1)}, bf16[1,1,768,2048]{3,2,1,0:T(8,128)(2,1)}, u32[]{:S(2)}, u32[]{:S(2)}) collective-permute-start(bf16[1,1,768,2048]{3,2,1,0:T(8,128)(2,1)} %refs_6_.7), channel_id=1, source_target_pairs={{0,1},{1,0},{2,3},{3,2},{4,5},{5,4},{6,7},{7,6},{8,9},{9,8},{10,11... | collective-permute-start | bytes 9437192 | tf_op jit(solution)/shard_map/T_wd/ppermute | solution.py:261
  18.6 15.5 %collective-permute-start.8 = (bf16[1,1,2048,768]{3,2,1,0:T(8,128)(2,1)}, bf16[1,1,2048,768]{3,2,1,0:T(8,128)(2,1)}, u32[]{:S(2)}, u32[]{:S(2)}) collective-permute-start(bf16[1,1,2048,768]{3,2,1,0:T(8,128)(2,1)} %refs_5_.7), channel_id=1, source_target_pairs={{0,1},{1,0},{2,3},{3,2},{4,5},{5,4},{6,7},{7,6},{8,9},{9,8},{10,11... | collective-permute-start | bytes 9437192 | tf_op jit(solution)/shard_map/T_wu/ppermute | solution.py:261
  18.7 9.6 %collective-permute-start.7 = (bf16[64,2176]{1,0:T(8,128)(2,1)}, bf16[64,2176]{1,0:T(8,128)(2,1)S(1)}, u32[]{:S(2)}, u32[]{:S(2)}) collective-permute-start(bf16[64,2176]{1,0:T(8,128)(2,1)} %get-tuple-element.63.refs_0_), channel_id=1, source_target_pairs={{0,12},{1,13},{2,14},{3,15},{4,0},{5,1},{6,2},{7,3},{8,4},{9,5},{1... | collective-permute-start | bytes 835592 | tf_op jit(solution)/shard_map/T_b_z3/ppermute | solution.py:265
  20.4 9.0 %collective-permute-start.5 = (bf16[64,2176]{1,0:T(8,128)(2,1)}, bf16[64,2176]{1,0:T(8,128)(2,1)}, u32[]{:S(2)}, u32[]{:S(2)}) collective-permute-start(bf16[64,2176]{1,0:T(8,128)(2,1)} %collective-permute-done.refs_2_), channel_id=1, source_target_pairs={{0,2},{1,3},{2,0},{3,1},{4,6},{5,7},{6,4},{7,5},{8,10},{9,11},{10,... | collective-permute-start | bytes 835592 | tf_op jit(solution)/shard_map/T_b_x1/ppermute | solution.py:261
  21.0 13.1 %collective-permute-start.6 = (bf16[64,2176]{1,0:T(8,128)(2,1)}, bf16[64,2176]{1,0:T(8,128)(2,1)}, u32[]{:S(2)}, u32[]{:S(2)}) collective-permute-start(bf16[64,2176]{1,0:T(8,128)(2,1)} %collective-permute-done.refs_2_), channel_id=1, source_target_pairs={{0,4},{1,5},{2,6},{3,7},{4,8},{5,9},{6,10},{7,11},{8,12},{9,13},{1... | collective-permute-start | bytes 835592 | tf_op jit(solution)/shard_map/T_b_z2/ppermute | solution.py:265
  28.3 24.4 %copy-start.13 = (bf16[64,2176]{1,0:T(8,128)(2,1)}, bf16[64,2176]{1,0:T(8,128)(2,1)S(1)}, u32[]{:S(2)}) copy-start(bf16[64,2176]{1,0:T(8,128)(2,1)S(1)} %collective-permute-done.7.refs_2_) | copy-start | bytes 835588
  34.1 20.9 %copy-start.5 = (bf16[64,2176]{1,0:T(8,128)(2,1)S(1)}, bf16[64,2176]{1,0:T(8,128)(2,1)}, u32[]{:S(2)}) copy-start(bf16[64,2176]{1,0:T(8,128)(2,1)} %get-tuple-element.73.refs_0_) | copy-start | bytes 835588
  34.1 18.7 %collective-permute-start.10 = (bf16[64,2176]{1,0:T(8,128)(2,1)}, bf16[64,2176]{1,0:T(8,128)(2,1)S(1)}, u32[]{:S(2)}, u32[]{:S(2)}) collective-permute-start(bf16[64,2176]{1,0:T(8,128)(2,1)} %get-tuple-element.73.refs_0_), channel_id=1, source_target_pairs={{0,4},{1,5},{2,6},{3,7},{4,8},{5,9},{6,10},{7,11},{8,12},{9,13},{1... | collective-permute-start | bytes 835592 | tf_op jit(solution)/shard_map/T_f_z1/ppermute | solution.py:265
  35.7 17.1 %collective-permute-start.13 = (bf16[64,2176]{1,0:T(8,128)(2,1)}, bf16[64,2176]{1,0:T(8,128)(2,1)S(1)}, u32[]{:S(2)}, u32[]{:S(2)}) collective-permute-start(bf16[64,2176]{1,0:T(8,128)(2,1)} %get-tuple-element.73.refs_0_), channel_id=1, source_target_pairs={{0,2},{1,3},{2,0},{3,1},{4,6},{5,7},{6,4},{7,5},{8,10},{9,11},{10,... | collective-permute-start | bytes 835592 | tf_op jit(solution)/shard_map/T_f_x0/ppermute | solution.py:261
  36.3 16.5 %collective-permute-start.12 = (bf16[64,2176]{1,0:T(8,128)(2,1)}, bf16[64,2176]{1,0:T(8,128)(2,1)S(1)}, u32[]{:S(2)}, u32[]{:S(2)}) collective-permute-start(bf16[64,2176]{1,0:T(8,128)(2,1)} %copy-done.14), channel_id=1, source_target_pairs={{0,12},{1,13},{2,14},{3,15},{4,0},{5,1},{6,2},{7,3},{8,4},{9,5},{1... | collective-permute-start | bytes 835592 | tf_op jit(solution)/shard_map/T_b_w3/ppermute | solution.py:265
  38.5 14.3 %collective-permute-start.11 = (bf16[64,2176]{1,0:T(8,128)(2,1)}, bf16[64,2176]{1,0:T(8,128)(2,1)S(1)}, u32[]{:S(2)}, u32[]{:S(2)}) collective-permute-start(bf16[64,2176]{1,0:T(8,128)(2,1)} %collective-permute-done.6.refs_0_), channel_id=1, source_target_pairs={{0,2},{1,3},{2,0},{3,1},{4,6},{5,7},{6,4},{7,5},{8,10},{9,11},{10,... | collective-permute-start | bytes 835592 | tf_op jit(solution)/shard_map/T_b_x2/ppermute | solution.py:261
  40.0 12.7 %collective-permute-start.14 = (bf16[64,2048]{1,0:T(8,128)(2,1)}, bf16[64,2048]{1,0:T(8,128)(2,1)S(1)}, u32[]{:S(2)}, u32[]{:S(2)}) collective-permute-start(bf16[64,2048]{1,0:T(8,128)(2,1)} %bitcast.37), channel_id=1, source_target_pairs={{0,16},{1,17},{2,18},{3,19},{4,20},{5,21},{6,22},{7,23},{8,24},{9,... | collective-permute-start | bytes 786440 | tf_op jit(solution)/shard_map/T_y1/ppermute | solution.py:276
  52.7 17.3 %copy-start.17 = (bf16[64,2048]{1,0:T(8,128)(2,1)}, bf16[64,2048]{1,0:T(8,128)(2,1)S(1)}, u32[]{:S(2)}) copy-start(bf16[64,2048]{1,0:T(8,128)(2,1)S(1)} %collective-permute-done.14) | copy-start | bytes 786436
  52.7 6.0 %copy-start.15 = (bf16[64,2176]{1,0:T(8,128)(2,1)}, bf16[64,2176]{1,0:T(8,128)(2,1)S(1)}, u32[]{:S(2)}) copy-start(bf16[64,2176]{1,0:T(8,128)(2,1)S(1)} %collective-permute-done.12.refs_3_) | copy-start | bytes 835588
  52.8 6.0 %copy-start.16 = (bf16[64,2176]{1,0:T(8,128)(2,1)}, bf16[64,2176]{1,0:T(8,128)(2,1)S(1)}, u32[]{:S(2)}) copy-start(bf16[64,2176]{1,0:T(8,128)(2,1)S(1)} %collective-permute-done.11.refs_1_) | copy-start | bytes 835588
  52.8 17.2 %copy-start.7 = (bf16[64,2176]{1,0:T(8,128)(2,1)}, bf16[64,2176]{1,0:T(8,128)(2,1)S(1)}, u32[]{:S(2)}) copy-start(bf16[64,2176]{1,0:T(8,128)(2,1)S(1)} %collective-permute-done.10.refs_2_) | copy-start | bytes 835588
  52.8 20.2 %copy-start.6 = (bf16[64,2176]{1,0:T(8,128)(2,1)}, bf16[64,2176]{1,0:T(8,128)(2,1)S(1)}, u32[]{:S(2)}) copy-start(bf16[64,2176]{1,0:T(8,128)(2,1)S(1)} %collective-permute-done.13.refs_1_) | copy-start | bytes 835588
  52.8 18.9 %copy-start.21 = (bf16[64,2048]{1,0:T(8,128)(2,1)S(1)}, bf16[64,2048]{1,0:T(8,128)(2,1)}, u32[]{:S(2)}) copy-start(bf16[64,2048]{1,0:T(8,128)(2,1)} %get-tuple-element.95) | copy-start | bytes 786436
  52.8 18.9 %copy-start.22 = (bf16[64,2048]{1,0:T(8,128)(2,1)S(1)}, bf16[64,2048]{1,0:T(8,128)(2,1)}, u32[]{:S(2)}) copy-start(bf16[64,2048]{1,0:T(8,128)(2,1)} %get-tuple-element.82) | copy-start | bytes 786436
  52.8 18.2 %collective-permute-start.18 = (bf16[128,2048]{1,0:T(8,128)(2,1)}, bf16[128,2048]{1,0:T(8,128)(2,1)S(1)}, u32[]{:S(2)}, u32[]{:S(2)}) collective-permute-start(bf16[128,2048]{1,0:T(8,128)(2,1)} %get-tuple-element.74), channel_id=1, source_target_pairs={{0,2},{1,3},{2,0},{3,1},{4,6},{5,7},{6,4},{7,5},{8,10},{9,11},{10,... | collective-permute-start | bytes 1572872 | tf_op jit(solution)/shard_map/T_b_s0/ppermute | solution.py:261
  53.4 17.6 %collective-permute-start.15 = (bf16[64,2176]{1,0:T(8,128)(2,1)S(1)}, bf16[64,2176]{1,0:T(8,128)(2,1)S(1)}, u32[]{:S(2)}, u32[]{:S(2)}) collective-permute-start(bf16[64,2176]{1,0:T(8,128)(2,1)S(1)} %collective-permute-done.10.refs_2_), channel_id=1, source_target_pairs={{0,2},{1,3},{2,0},{3,1},{4,6},{5,7},{6,4},{7,5},{8,10},{9,11},{10,... | collective-permute-start | bytes 835592 | tf_op jit(solution)/shard_map/T_f_x1/ppermute | solution.py:261
  54.9 16.1 %collective-permute-start.16 = (bf16[64,2176]{1,0:T(8,128)(2,1)S(1)}, bf16[64,2176]{1,0:T(8,128)(2,1)S(1)}, u32[]{:S(2)}, u32[]{:S(2)}) collective-permute-start(bf16[64,2176]{1,0:T(8,128)(2,1)S(1)} %collective-permute-done.10.refs_2_), channel_id=1, source_target_pairs={{0,4},{1,5},{2,6},{3,7},{4,8},{5,9},{6,10},{7,11},{8,12},{9,13},{1... | collective-permute-start | bytes 835592 | tf_op jit(solution)/shard_map/T_f_z2/ppermute | solution.py:265
  54.9 15.1 %collective-permute-start.17 = (bf16[64,2176]{1,0:T(8,128)(2,1)S(1)}, bf16[64,2176]{1,0:T(8,128)(2,1)S(1)}, u32[]{:S(2)}, u32[]{:S(2)}) collective-permute-start(bf16[64,2176]{1,0:T(8,128)(2,1)S(1)} %copy-done.5), channel_id=1, source_target_pairs={{0,12},{1,13},{2,14},{3,15},{4,0},{5,1},{6,2},{7,3},{8,4},{9,5},{1... | collective-permute-start | bytes 835592 | tf_op jit(solution)/shard_map/T_f_z3/ppermute | solution.py:265
  70.0 15.6 %copy-start.9 = (bf16[64,2176]{1,0:T(8,128)(2,1)}, bf16[64,2176]{1,0:T(8,128)(2,1)S(1)}, u32[]{:S(2)}) copy-start(bf16[64,2176]{1,0:T(8,128)(2,1)S(1)} %collective-permute-done.17.refs_2_) | copy-start | bytes 835588
  71.1 3.7 %copy-start.10 = (bf16[64,2176]{1,0:T(8,128)(2,1)}, bf16[64,2176]{1,0:T(8,128)(2,1)S(1)}, u32[]{:S(2)}) copy-start(bf16[64,2176]{1,0:T(8,128)(2,1)S(1)} %collective-permute-done.15.refs_3_) | copy-start | bytes 835588
  71.1 14.6 %copy-start.8 = (bf16[64,2176]{1,0:T(8,128)(2,1)}, bf16[64,2176]{1,0:T(8,128)(2,1)S(1)}, u32[]{:S(2)}) copy-start(bf16[64,2176]{1,0:T(8,128)(2,1)S(1)} %collective-permute-done.16.refs_0_) | copy-start | bytes 835588
  71.1 18.1 %collective-permute-start.22 = (bf16[128,2048]{1,0:T(8,128)(2,1)}, bf16[128,2048]{1,0:T(8,128)(2,1)S(1)}, u32[]{:S(2)}, u32[]{:S(2)}) collective-permute-start(bf16[128,2048]{1,0:T(8,128)(2,1)} %get-tuple-element.84), channel_id=1, source_target_pairs={{0,2},{1,3},{2,0},{3,1},{4,6},{5,7},{6,4},{7,5},{8,10},{9,11},{10,... | collective-permute-start | bytes 1572872 | tf_op jit(solution)/shard_map/T_b_s2/ppermute | solution.py:261
  71.8 13.8 %collective-permute-start.21 = (bf16[64,2048]{1,0:T(8,128)(2,1)S(1)}, bf16[64,2048]{1,0:T(8,128)(2,1)S(1)}, u32[]{:S(2)}, u32[]{:S(2)}) collective-permute-start(bf16[64,2048]{1,0:T(8,128)(2,1)S(1)} %get-tuple-element.83), channel_id=1, source_target_pairs={{0,12},{1,13},{2,14},{3,15},{4,0},{5,1},{6,2},{7,3},{8,4},{9,5},{1... | collective-permute-start | bytes 786440 | tf_op jit(solution)/shard_map/T_b_r1/ppermute | solution.py:265
  73.0 12.6 %collective-permute-start.20 = (bf16[64,2176]{1,0:T(8,128)(2,1)S(1)}, bf16[64,2176]{1,0:T(8,128)(2,1)S(1)}, u32[]{:S(2)}, u32[]{:S(2)}) collective-permute-start(bf16[64,2176]{1,0:T(8,128)(2,1)S(1)} %collective-permute-done.13.refs_1_), channel_id=1, source_target_pairs={{0,12},{1,13},{2,14},{3,15},{4,0},{5,1},{6,2},{7,3},{8,4},{9,5},{1... | collective-permute-start | bytes 835592 | tf_op jit(solution)/shard_map/T_f_w3/ppermute | solution.py:265
  74.5 14.7 %collective-permute-start.19 = (bf16[64,2176]{1,0:T(8,128)(2,1)S(1)}, bf16[64,2176]{1,0:T(8,128)(2,1)S(1)}, u32[]{:S(2)}, u32[]{:S(2)}) collective-permute-start(bf16[64,2176]{1,0:T(8,128)(2,1)S(1)} %collective-permute-done.16.refs_0_), channel_id=1, source_target_pairs={{0,2},{1,3},{2,0},{3,1},{4,6},{5,7},{6,4},{7,5},{8,10},{9,11},{10,... | collective-permute-start | bytes 835592 | tf_op jit(solution)/shard_map/T_f_x2/ppermute | solution.py:261
  74.8 15.0 %copy-start.26 = (bf16[64,2048]{1,0:T(8,128)(2,1)S(1)}, bf16[64,2048]{1,0:T(8,128)(2,1)}, u32[]{:S(2)}) copy-start(bf16[64,2048]{1,0:T(8,128)(2,1)} %get-tuple-element.87) | copy-start | bytes 786436
  74.8 15.0 %copy-start.27 = (bf16[64,2048]{1,0:T(8,128)(2,1)S(1)}, bf16[64,2048]{1,0:T(8,128)(2,1)}, u32[]{:S(2)}) copy-start(bf16[64,2048]{1,0:T(8,128)(2,1)} %get-tuple-element.89) | copy-start | bytes 786436
  85.7 6.2 %copy-start.11 = (bf16[64,2176]{1,0:T(8,128)(2,1)}, bf16[64,2176]{1,0:T(8,128)(2,1)S(1)}, u32[]{:S(2)}) copy-start(bf16[64,2176]{1,0:T(8,128)(2,1)S(1)} %collective-permute-done.20.refs_3_) | copy-start | bytes 835588
  89.2 2.7 %copy-start.12 = (bf16[64,2176]{1,0:T(8,128)(2,1)}, bf16[64,2176]{1,0:T(8,128)(2,1)S(1)}, u32[]{:S(2)}) copy-start(bf16[64,2176]{1,0:T(8,128)(2,1)S(1)} %collective-permute-done.19.refs_1_) | copy-start | bytes 835588
  89.2 16.9 %collective-permute-start.23 = (bf16[128,2048]{1,0:T(8,128)(2,1)}, bf16[128,2048]{1,0:T(8,128)(2,1)S(1)}, u32[]{:S(2)}, u32[]{:S(2)}) collective-permute-start(bf16[128,2048]{1,0:T(8,128)(2,1)} %get-tuple-element.85), channel_id=1, source_target_pairs={{0,2},{1,3},{2,0},{3,1},{4,6},{5,7},{6,4},{7,5},{8,10},{9,11},{10,... | collective-permute-start | bytes 1572872 | tf_op jit(solution)/shard_map/T_f_s0/ppermute | solution.py:261
  89.9 12.7 %collective-permute-start.25 = (bf16[64,2048]{1,0:T(8,128)(2,1)S(1)}, bf16[64,2048]{1,0:T(8,128)(2,1)S(1)}, u32[]{:S(2)}, u32[]{:S(2)}) collective-permute-start(bf16[64,2048]{1,0:T(8,128)(2,1)S(1)} %get-tuple-element.90), channel_id=1, source_target_pairs={{0,4},{1,5},{2,6},{3,7},{4,8},{5,9},{6,10},{7,11},{8,12},{9,13},{1... | collective-permute-start | bytes 786440 | tf_op jit(solution)/shard_map/T_b_r3/ppermute | solution.py:265
  90.2 15.9 %copy-start.23 = (bf16[64,2048]{1,0:T(8,128)(2,1)S(1)}, bf16[64,2048]{1,0:T(8,128)(2,1)}, u32[]{:S(2)}) copy-start(bf16[64,2048]{1,0:T(8,128)(2,1)} %get-tuple-element.86) | copy-start | bytes 786436
  90.2 17.8 %copy-start.4 = (bf16[1,64,2048]{2,1,0:T(8,128)(2,1)S(1)}, bf16[1,64,2048]{2,1,0:T(8,128)(2,1)}, u32[]{:S(2)}) copy-start(bf16[1,64,2048]{2,1,0:T(8,128)(2,1)} %param.20) | copy-start | bytes 786436
  90.2 18.1 %copy-start.3 = (bf16[1,64,2048]{2,1,0:T(8,128)(2,1)S(1)}, bf16[1,64,2048]{2,1,0:T(8,128)(2,1)}, u32[]{:S(2)}) copy-start(bf16[1,64,2048]{2,1,0:T(8,128)(2,1)} %param.21) | copy-start | bytes 786436
  90.2 15.9 %collective-permute-start.24 = (bf16[64,2048]{1,0:T(8,128)(2,1)S(1)}, bf16[64,2048]{1,0:T(8,128)(2,1)S(1)}, u32[]{:S(2)}, u32[]{:S(2)}) collective-permute-start(bf16[64,2048]{1,0:T(8,128)(2,1)S(1)} %get-tuple-element.88), channel_id=1, source_target_pairs={{0,8},{1,9},{2,10},{3,11},{4,12},{5,13},{6,14},{7,15},{8,0},{9,1},... | collective-permute-start | bytes 786440 | tf_op jit(solution)/shard_map/T_b_r2/ppermute | solution.py:265
  102.6 7.1 %copy-start.29 = (bf16[64,2048]{1,0:T(8,128)(2,1)S(1)}, bf16[64,2048]{1,0:T(8,128)(2,1)}, u32[]{:S(2)}) copy-start(bf16[64,2048]{1,0:T(8,128)(2,1)} %get-tuple-element.103) | copy-start | bytes 786436
  102.6 10.8 %copy-start.25 = (bf16[64,2048]{1,0:T(8,128)(2,1)S(1)}, bf16[64,2048]{1,0:T(8,128)(2,1)}, u32[]{:S(2)}) copy-start(bf16[64,2048]{1,0:T(8,128)(2,1)} %get-tuple-element.78) | copy-start | bytes 786436
  102.6 14.1 %copy-start.28 = (bf16[64,2048]{1,0:T(8,128)(2,1)S(1)}, bf16[64,2048]{1,0:T(8,128)(2,1)}, u32[]{:S(2)}) copy-start(bf16[64,2048]{1,0:T(8,128)(2,1)} %get-tuple-element.107) | copy-start | bytes 786436
  102.6 15.3 %copy-start.20 = (bf16[64,2048]{1,0:T(8,128)(2,1)S(1)}, bf16[64,2048]{1,0:T(8,128)(2,1)}, u32[]{:S(2)}) copy-start(bf16[64,2048]{1,0:T(8,128)(2,1)} %get-tuple-element.102) | copy-start | bytes 786436
  106.1 17.5 %copy-start.19 = (bf16[64,2048]{1,0:T(8,128)(2,1)S(1)}, bf16[64,2048]{1,0:T(8,128)(2,1)}, u32[]{:S(2)}) copy-start(bf16[64,2048]{1,0:T(8,128)(2,1)} %get-tuple-element.106) | copy-start | bytes 786436
  106.1 31.5 %copy-start.18 = (bf16[64,2048]{1,0:T(8,128)(2,1)S(1)}, bf16[64,2048]{1,0:T(8,128)(2,1)}, u32[]{:S(2)}) copy-start(bf16[64,2048]{1,0:T(8,128)(2,1)} %copy-done.17) | copy-start | bytes 786436
  106.1 7.2 %collective-permute-start.26 = (bf16[64,2048]{1,0:T(8,128)(2,1)S(1)}, bf16[64,2048]{1,0:T(8,128)(2,1)S(1)}, u32[]{:S(2)}, u32[]{:S(2)}) collective-permute-start(bf16[64,2048]{1,0:T(8,128)(2,1)S(1)} %add_convert_fusion.6), channel_id=1, source_target_pairs={{0,12},{1,13},{2,14},{3,15},{4,0},{5,1},{6,2},{7,3},{8,4},{9,5},{1... | collective-permute-start | bytes 786440 | tf_op jit(solution)/shard_map/T_f_near/ppermute | solution.py:265
  108.6 16.7 %collective-permute-start.28 = (bf16[64,2048]{1,0:T(8,128)(2,1)S(1)}, bf16[64,2048]{1,0:T(8,128)(2,1)S(1)}, u32[]{:S(2)}, u32[]{:S(2)}) collective-permute-start(bf16[64,2048]{1,0:T(8,128)(2,1)S(1)} %fusion.5), channel_id=1, source_target_pairs={{0,16},{1,17},{2,18},{3,19},{4,20},{5,21},{6,22},{7,23},{8,24},{9,... | collective-permute-start | bytes 786440 | tf_op jit(solution)/shard_map/T_b_y/ppermute | solution.py:276
  109.7 7.0 %collective-permute-start.29 = (bf16[64,2048]{1,0:T(8,128)(2,1)S(1)}, bf16[64,2048]{1,0:T(8,128)(2,1)S(1)}, u32[]{:S(2)}, u32[]{:S(2)}) collective-permute-start(bf16[64,2048]{1,0:T(8,128)(2,1)S(1)} %copy-done.29), channel_id=1, source_target_pairs={{0,2},{1,3},{2,0},{3,1},{4,6},{5,7},{6,4},{7,5},{8,10},{9,11},{10,... | collective-permute-start | bytes 786440 | tf_op jit(solution)/shard_map/T_f_s2/ppermute | solution.py:261
  113.4 14.2 %collective-permute-start.27 = (bf16[64,2048]{1,0:T(8,128)(2,1)S(1)}, bf16[64,2048]{1,0:T(8,128)(2,1)S(1)}, u32[]{:S(2)}, u32[]{:S(2)}) collective-permute-start(bf16[64,2048]{1,0:T(8,128)(2,1)S(1)} %add_convert_fusion.3), channel_id=1, source_target_pairs={{0,16},{1,17},{2,18},{3,19},{4,20},{5,21},{6,22},{7,23},{8,24},{9,... | collective-permute-start | bytes 786440 | tf_op jit(solution)/shard_map/T_f_joined/ppermute | solution.py:276
  116.7 6.8 %collective-permute-start.31 = (bf16[64,2048]{1,0:T(8,128)(2,1)S(1)}, bf16[64,2048]{1,0:T(8,128)(2,1)S(1)}, u32[]{:S(2)}, u32[]{:S(2)}) collective-permute-start(bf16[64,2048]{1,0:T(8,128)(2,1)S(1)} %copy-done.28), channel_id=1, source_target_pairs={{0,2},{1,3},{2,0},{3,1},{4,6},{5,7},{6,4},{7,5},{8,10},{9,11},{10,... | collective-permute-start | bytes 786440 | tf_op jit(solution)/shard_map/T_f_s3/ppermute | solution.py:261
  118.0 19.7 %collective-permute-start.30 = (bf16[64,2048]{1,0:T(8,128)(2,1)S(1)}, bf16[64,2048]{1,0:T(8,128)(2,1)S(1)}, u32[]{:S(2)}, u32[]{:S(2)}) collective-permute-start(bf16[64,2048]{1,0:T(8,128)(2,1)S(1)} %add_convert_fusion.2), channel_id=1, source_target_pairs={{0,24},{1,25},{2,26},{3,27},{4,28},{5,29},{6,30},{7,31},{8,16},{9,... | collective-permute-start | bytes 786440 | tf_op jit(solution)/shard_map/T_f_r2/ppermute | solution.py:276
  123.6 14.0 %collective-permute-start.32 = (bf16[64,2048]{1,0:T(8,128)(2,1)S(1)}, bf16[64,2048]{1,0:T(8,128)(2,1)S(1)}, u32[]{:S(2)}, u32[]{:S(2)}) collective-permute-start(bf16[64,2048]{1,0:T(8,128)(2,1)S(1)} %add_convert_fusion.1), channel_id=1, source_target_pairs={{0,20},{1,21},{2,22},{3,23},{4,24},{5,25},{6,26},{7,27},{8,28},{9,... | collective-permute-start | bytes 786440 | tf_op jit(solution)/shard_map/T_f_r3/ppermute | solution.py:276
  125.3 0.7 copy-start.24
